TPU v7x, 32 devices: a whole 2x2x4 slice. The times are simulated.
32 devices in a mesh: dp: 16 (over z, y, x), tensor: 2 (over core).
Axes of the slice: x: 2, y: 2, z: 4, core: 2. Of those that a mesh axis runs over, the one named last changes fastest.
Arguments:
- tokens: bfloat16 [16384, 1024], P('dp', 'tensor'), may hold values from -15 to 15
- cotangent: bfloat16 [16384, 1024], P('dp', 'tensor'), may hold values from -6 to 6
- ln_weight: float32 [1024], replicated, may hold values from 0.25 to 1.75
- up_inner: bfloat16 [1024, 2048], P(None, 'tensor'), may hold values from -0.1875 to 0.1875
- up_gate: bfloat16 [1024, 2048], P(None, 'tensor'), may hold values from -0.1875 to 0.1875
- conv_weight: float32 [4, 2048], P(None, 'tensor'), may hold values from -3 to 3
- conv_bias: float32 [2048], P('tensor'), may hold values from -2 to 2
- query_weight: float32 [512, 4, 4], P('tensor'), may hold values from -3 to 3
- key_weight: float32 [512, 4, 4], P('tensor'), may hold values from -3 to 3
- value_weight: float32 [512, 4, 4], P('tensor'), may hold values from -3 to 3
- gate_weight: bfloat16 [3, 2048, 8], P(None, 'tensor'), may hold values from -0.078125 to 0.078125
- gate_bias: float32 [8], replicated, may hold values from -1 to 9
- group_weight: float32 [2048], P('tensor'), may hold values from 0.25 to 1.75
- skip_weight: float32 [2048], P('tensor'), may hold values from 0.5 to 1.5
- down_weight: bfloat16 [2048, 1024], P('tensor'), may hold values from -0.125 to 0.125
Outputs:
- out: bfloat16 [16384, 1024], P('dp', 'tensor')
- grad_tokens: float32 [16384, 1024], P('dp', 'tensor')
- grad_ln_weight: float32 [1024], P('tensor')
- grad_up_inner: float32 [1024, 2048], P(None, 'tensor')
- grad_up_gate: float32 [1024, 2048], P(None, 'tensor')
- grad_conv_weight: float32 [4, 2048], P(None, 'tensor')
- grad_conv_bias: float32 [2048], P('tensor')
- grad_query_weight: float32 [512, 4, 4], P('tensor')
- grad_key_weight: float32 [512, 4, 4], P('tensor')
- grad_value_weight: float32 [512, 4, 4], P('tensor')
- grad_gate_weight: float32 [3, 2048, 8], P(None, 'tensor')
- grad_gate_bias: float32 [8], replicated
- grad_group_weight: float32 [2048], P('tensor')
- grad_skip_weight: float32 [2048], P('tensor')
- grad_down_weight: float32 [2048, 1024], P('tensor')
- rms: float32 [1], replicated
All inputs are finite; a program needn't handle non-finite values.
Results may differ from a plain program's by a relative error of at most 0.023.
The roundings to bfloat16 on the way count: a program that leaves them out, or rounds other values in their place, can miss the bound.
Values may be sent and summed in bfloat16 or wider, within the bound.
No kernel may reach another device: no remote copies, remote signals or barrier semaphores. Data moves between devices by JAX's collectives and lax.ppermute only.
A program may use at most 448 MiB of HBM per device.

v0:
```python
import jax
import jax.numpy as jnp
from jax import lax
from jax.sharding import PartitionSpec as P

DH = 512
BLOCK = 64
SEQ_LEN = 8192


highest = lax.Precision.HIGHEST
norm_eps = 1e-05
far_below = -1e30


def shifted(block, axis, distance):
    devices = range(lax.axis_size(axis))
    route = [(i - distance, i) for i in devices if i - distance in devices]
    return lax.ppermute(block, axis, route)


def matmul(left, right):
    return jnp.dot(left, right, preferred_element_type=jnp.float32)


def inner_rows(left, right):
    return lax.dot_general(
        left, right, (((0,), (0,)), ((), ())), preferred_element_type=jnp.float32
    )


def outer_cols(left, right):
    return lax.dot_general(
        left, right, (((1,), (1,)), ((), ())), preferred_element_type=jnp.float32
    )


def layer_stats(values):
    centered = values - jnp.mean(values, axis=-1, keepdims=True)
    inverse = lax.rsqrt(jnp.mean(centered * centered, axis=-1, keepdims=True) + norm_eps)
    return (centered * inverse, inverse)


def layer_back(grad_hat, normed_hat, inverse):
    centered_grad = grad_hat - jnp.mean(grad_hat, axis=-1, keepdims=True)
    return inverse * (
        centered_grad - normed_hat * jnp.mean(grad_hat * normed_hat, axis=-1, keepdims=True)
    )


def band_entries(weight, offset):
    block_size = weight.shape[1]
    pieces = []
    for out_pos in range(block_size):
        if 0 <= out_pos + offset < block_size:
            pieces.append(weight[:, out_pos, out_pos + offset])
        else:
            pieces.append(jnp.zeros_like(weight[:, 0, 0]))
    return jnp.stack(pieces, axis=1).reshape(-1)


def band_apply(values, weight):
    block_size = weight.shape[1]
    summed = jnp.zeros_like(values)
    for offset in range(1 - block_size, block_size):
        summed = summed + band_entries(weight, offset) * jnp.roll(values, -offset, axis=1)
    return summed


def band_grad(grad_rows, values, block_size):
    block_count = grad_rows.shape[1] // block_size
    offset_sums = {}
    for offset in range(1 - block_size, block_size):
        offset_sums[offset] = jnp.sum(
            grad_rows * jnp.roll(values, -offset, axis=1), axis=0
        ).reshape(block_count, block_size)
    layers = []
    for out_pos in range(block_size):
        layers.append(
            jnp.stack(
                [offset_sums[in_pos - out_pos][:, out_pos] for in_pos in range(block_size)], axis=1
            )
        )
    return jnp.stack(layers, axis=1)


def gate_curves(forget_pre):
    cumulative = jnp.cumsum(jax.nn.log_sigmoid(forget_pre), axis=1)
    return (cumulative, cumulative[:, -1])


def block_updates(key_vecs, value_vecs, in_pre, cumulative, last_cum):
    key_scale = key_vecs.shape[-1] ** (-0.5)
    keep_weight = jnp.exp(last_cum[:, None] - cumulative + in_pre) * key_scale
    key_wide = key_vecs.astype(jnp.float32)
    weighted = (key_wide * keep_weight[..., None]).astype(jnp.bfloat16)
    update = jnp.einsum("csd,cse->cde", weighted, value_vecs, preferred_element_type=jnp.float32)
    norm_part = jnp.einsum("cs,csd->cd", keep_weight, key_wide, precision=highest)
    return (keep_weight, weighted, jnp.concatenate([update, norm_part[:, None, :]], axis=1))


def chain_forward(initial, decays, updates):

    def advance(state_now, step_item):
        decay_now, update_now = step_item
        return (decay_now * state_now + update_now, state_now)

    return lax.scan(advance, initial, (decays, updates))


def chain_backward(final_grad, decays, local_grad):

    def retreat(grad_end, step_item):
        decay_now, local_now = step_item
        return (local_now + decay_now * grad_end, grad_end)

    return lax.scan(retreat, final_grad, (decays, local_grad), reverse=True)


def block_mix(queries, key_vecs, value_vecs, in_pre, cumulative, starts):
    head_dim = key_vecs.shape[-1]
    key_scale = head_dim ** (-0.5)
    length = key_vecs.shape[1]
    causal = lax.broadcasted_iota(jnp.int32, (length, length), 0) >= lax.broadcasted_iota(
        jnp.int32, (length, length), 1
    )
    damping = jnp.exp(
        jnp.where(
            causal, cumulative[:, :, None] - cumulative[:, None, :] + in_pre[:, None, :], far_below
        )
    )
    scores = jnp.einsum("ctd,csd->cts", queries, key_vecs, preferred_element_type=jnp.float32)
    weights = scores * damping * key_scale
    weights_low = weights.astype(jnp.bfloat16)
    inside = jnp.einsum("cts,csd->ctd", weights_low, value_vecs, preferred_element_type=jnp.float32)
    state_low = starts[:, :head_dim].astype(jnp.bfloat16)
    cross_term = jnp.einsum("ctd,cde->cte", queries, state_low, preferred_element_type=jnp.float32)
    growth = jnp.exp(cumulative)
    carried = growth[..., None] * cross_term
    norm_cross = growth * jnp.einsum(
        "ctd,cd->ct", queries.astype(jnp.float32), starts[:, head_dim], precision=highest
    )
    numerator = inside + carried
    normal = jnp.sum(weights, axis=2) + norm_cross
    denominator = jnp.maximum(jnp.abs(normal), 1.0)
    return (
        damping,
        scores,
        weights_low,
        state_low,
        carried,
        growth,
        norm_cross,
        numerator,
        normal,
        denominator,
    )


def head_prepare(key_vecs, value_vecs, in_pre, forget_pre):
    cumulative, last_cum = gate_curves(forget_pre)
    keep_weight, weighted, updates = block_updates(
        key_vecs, value_vecs, in_pre, cumulative, last_cum
    )
    step_decay = jnp.exp(last_cum)
    final_state, _ = chain_forward(jnp.zeros_like(updates[0]), step_decay, updates)
    prepared = (cumulative, step_decay, keep_weight, weighted, updates)
    return (prepared, jnp.exp(jnp.sum(last_cum)), final_state)


def head_outputs(queries, key_vecs, value_vecs, in_pre, prepared, initial):
    cumulative, step_decay, keep_weight, weighted, updates = prepared
    _, starts = chain_forward(initial, step_decay, updates)
    mixed_parts = block_mix(queries, key_vecs, value_vecs, in_pre, cumulative, starts)
    return (mixed_parts[7] / mixed_parts[9][..., None], starts, mixed_parts)


def head_first(queries, prepared, mixed_parts, head_grad):
    step_decay = prepared[1]
    growth = mixed_parts[5]
    numerator = mixed_parts[7]
    normal = mixed_parts[8]
    denominator = mixed_parts[9]
    mixed = numerator / denominator[..., None]
    numer_grad = head_grad / denominator[..., None]
    denom_grad = -jnp.sum(head_grad * mixed, axis=-1) / denominator
    normal_grad = jnp.where(jnp.abs(normal) > 1.0, jnp.sign(normal) * denom_grad, 0.0)
    cross_low = (growth[..., None] * numer_grad).astype(jnp.bfloat16)
    state_part = jnp.einsum("ctd,cte->cde", queries, cross_low, preferred_element_type=jnp.float32)
    norm_part = jnp.einsum(
        "ct,ctd->cd", normal_grad * growth, queries.astype(jnp.float32), precision=highest
    )
    local_grad = jnp.concatenate([state_part, norm_part[:, None, :]], axis=1)
    first_grad, _ = chain_backward(jnp.zeros_like(local_grad[0]), step_decay, local_grad)
    return (first_grad, (numer_grad, normal_grad, cross_low, local_grad))


def head_rest(
    queries, key_vecs, value_vecs, forget_pre, prepared, starts, mixed_parts, kept_grads, end_grad
):
    head_dim = key_vecs.shape[-1]
    key_scale = head_dim ** (-0.5)
    cumulative, step_decay, keep_weight, weighted, updates = prepared
    (
        damping,
        scores,
        weights_low,
        state_low,
        carried,
        growth,
        norm_cross,
        numerator,
        normal,
        denominator,
    ) = mixed_parts
    numer_grad, normal_grad, cross_low, local_grad = kept_grads
    _, end_grads = chain_backward(end_grad, step_decay, local_grad)
    numer_low = numer_grad.astype(jnp.bfloat16)
    weights_grad = (
        jnp.einsum("ctd,csd->cts", numer_low, value_vecs, preferred_element_type=jnp.float32)
        + normal_grad[..., None]
    )
    value_grad = jnp.einsum(
        "cts,ctd->csd", weights_low, numer_low, preferred_element_type=jnp.float32
    )
    scores_low = (weights_grad * key_scale * damping).astype(jnp.bfloat16)
    expo_grad = weights_grad * key_scale * scores * damping
    query_grad = jnp.einsum(
        "cts,csd->ctd", scores_low, key_vecs, preferred_element_type=jnp.float32
    )
    key_grad = jnp.einsum("cts,ctd->csd", scores_low, queries, preferred_element_type=jnp.float32)
    cum_grad = jnp.sum(expo_grad, axis=2) - jnp.sum(expo_grad, axis=1)
    in_grad = jnp.sum(expo_grad, axis=1)
    cum_grad = cum_grad + jnp.sum(numer_grad * carried, axis=-1) + normal_grad * norm_cross
    query_grad = query_grad + jnp.einsum(
        "cte,cde->ctd", cross_low, state_low, preferred_element_type=jnp.float32
    )
    query_grad = query_grad + (normal_grad * growth)[..., None] * starts[:, None, head_dim, :]
    end_state = end_grads[:, :head_dim]
    end_norm = end_grads[:, head_dim]
    last_grad = step_decay * (
        jnp.sum(end_state * starts[:, :head_dim], axis=(1, 2))
        + jnp.sum(end_norm * starts[:, head_dim], axis=1)
    )
    update_low = end_state.astype(jnp.bfloat16)
    weighted_grad = jnp.einsum(
        "cse,cde->csd", value_vecs, update_low, preferred_element_type=jnp.float32
    )
    value_grad = value_grad + jnp.einsum(
        "csd,cde->cse", weighted, update_low, preferred_element_type=jnp.float32
    )
    key_total = weighted_grad + end_norm[:, None, :]
    key_grad = key_grad + keep_weight[..., None] * key_total
    keep_grad = jnp.sum(key_vecs.astype(jnp.float32) * key_total, axis=-1) * keep_weight
    last_grad = last_grad + jnp.sum(keep_grad, axis=1)
    cum_grad = cum_grad - keep_grad
    in_grad = in_grad + keep_grad
    cum_grad = cum_grad.at[:, -1].add(last_grad)
    logf_grad = jnp.cumsum(cum_grad[:, ::-1], axis=1)[:, ::-1]
    forget_grad = logf_grad * jax.nn.sigmoid(-forget_pre)
    return (query_grad, key_grad, value_grad, in_grad, forget_grad)


def pass_state(decays, states, direction, seq_span, seq_stride):

    def relay_round(round_idx, incoming):
        return shifted(decays[:, None, None] * incoming + states, "dp", direction * seq_stride)

    return lax.fori_loop(0, seq_span - 1, relay_round, jnp.zeros_like(states))


def on_device(
    tokens,
    cotangent,
    ln_weight,
    up_inner,
    up_gate,
    conv_weight,
    conv_bias,
    query_weight,
    key_weight,
    value_weight,
    gate_weight,
    gate_bias,
    group_weight,
    skip_weight,
    down_weight,
):
    full_tokens, full_cot = (
        lax.all_gather(tokens, "tensor", axis=1, tiled=True),
        lax.all_gather(cotangent, "tensor", axis=1, tiled=True),
    )
    row_count = tokens.shape[0]
    local_width = up_inner.shape[1]
    model_width = full_tokens.shape[1]
    head_count = gate_bias.shape[0] // 2
    local_heads = local_width // DH
    block_count = row_count // BLOCK
    kernel_size = conv_weight.shape[0]
    seq_span = SEQ_LEN // row_count
    seq_stride = lax.axis_size("dp") // seq_span
    dp_place = lax.axis_index("dp")
    tensor_place = lax.axis_index("tensor")
    piece_pos = dp_place // seq_stride
    seq_first = piece_pos == 0
    seq_last = piece_pos == seq_span - 1
    normed_hat, inverse = layer_stats(full_tokens.astype(jnp.float32))
    normed = (normed_hat * ln_weight).astype(jnp.bfloat16)
    inner_act = matmul(normed, up_inner)
    gate_in = matmul(normed, up_gate)
    before = shifted(inner_act[row_count - kernel_size + 1 :], "dp", seq_stride)
    before = jnp.where(seq_first, 0.0, before)
    padded = jnp.concatenate([before, inner_act], axis=0)
    conv_out = conv_bias
    for tap_pos in range(kernel_size):
        conv_out = (
            conv_out
            + conv_weight[tap_pos]
            * padded[kernel_size - 1 - tap_pos : kernel_size - 1 - tap_pos + row_count]
        )
    active = jax.nn.silu(conv_out)
    queries = band_apply(active, query_weight).astype(jnp.bfloat16)
    key_vecs = band_apply(active, key_weight).astype(jnp.bfloat16)
    value_vecs = band_apply(inner_act, value_weight).astype(jnp.bfloat16)
    partial_pre = (
        matmul(queries, gate_weight[0])
        + matmul(key_vecs, gate_weight[1])
        + matmul(value_vecs, gate_weight[2])
    )
    gate_pre = lax.psum(partial_pre, "tensor") + gate_bias
    local_pre = lax.dynamic_slice_in_dim(
        gate_pre.reshape(row_count, 2, head_count), tensor_place * local_heads, local_heads, axis=2
    )

    def head_slices(head_pos):
        first_col = head_pos * DH
        return (
            queries[:, first_col : first_col + DH].reshape(block_count, BLOCK, DH),
            key_vecs[:, first_col : first_col + DH].reshape(block_count, BLOCK, DH),
            value_vecs[:, first_col : first_col + DH].reshape(block_count, BLOCK, DH),
            local_pre[:, 0, head_pos].reshape(block_count, BLOCK),
            local_pre[:, 1, head_pos].reshape(block_count, BLOCK),
        )

    slices = [head_slices(head_pos) for head_pos in range(local_heads)]
    summaries = [
        head_prepare(head_part[1], head_part[2], head_part[3], head_part[4]) for head_part in slices
    ]
    device_decay = jnp.stack([summary[1] for summary in summaries])
    device_state = jnp.stack([summary[2] for summary in summaries])
    incoming = pass_state(
        jnp.where(seq_last, 0.0, device_decay),
        jnp.where(seq_last, 0.0, device_state),
        1,
        seq_span,
        seq_stride,
    )
    head_mixed = []
    head_starts = []
    head_parts = []
    for head_pos in range(local_heads):
        head_part = slices[head_pos]
        mixed_head, starts, mixed_parts = head_outputs(
            head_part[0],
            head_part[1],
            head_part[2],
            head_part[3],
            summaries[head_pos][0],
            incoming[head_pos],
        )
        head_mixed.append(mixed_head)
        head_starts.append(starts)
        head_parts.append(mixed_parts)
    mixed = jnp.concatenate([piece.reshape(row_count, DH) for piece in head_mixed], axis=1)
    group_hat, group_inv = layer_stats(mixed.reshape(row_count, local_heads, DH))
    group_hat = group_hat.reshape(row_count, local_width)
    gated_state = group_hat * group_weight + skip_weight * active
    gate_act = jax.nn.silu(gate_in)
    gated = (gated_state * gate_act).astype(jnp.bfloat16)
    branch = lax.psum_scatter(matmul(gated, down_weight), "tensor", scatter_dimension=1, tiled=True)
    result = tokens.astype(jnp.float32) + branch
    square_sum = lax.psum(jnp.sum(result * result), ("dp", "tensor"))
    rms_single = jnp.sqrt(square_sum / (row_count * model_width * lax.axis_size("dp")))[None]
    dgated = outer_cols(full_cot, down_weight)
    grad_down = inner_rows(gated, full_cot)
    gate_sig = jax.nn.sigmoid(gate_in)
    state_grad = dgated * gate_act
    gate_in_grad = (dgated * gated_state * gate_sig * (1.0 + gate_in * (1.0 - gate_sig))).astype(
        jnp.bfloat16
    )
    grad_skip = jnp.sum(state_grad * active, axis=0)
    grad_group = jnp.sum(state_grad * group_hat, axis=0)
    active_grad = state_grad * skip_weight
    mixed_grad = layer_back(
        (state_grad * group_weight).reshape(row_count, local_heads, DH),
        group_hat.reshape(row_count, local_heads, DH),
        group_inv,
    ).reshape(row_count, local_width)
    head_grads = [
        mixed_grad[:, head_pos * DH : (head_pos + 1) * DH].reshape(block_count, BLOCK, DH)
        for head_pos in range(local_heads)
    ]
    first_list = []
    kept_list = []
    for head_pos in range(local_heads):
        first_grad, kept_grads = head_first(
            slices[head_pos][0], summaries[head_pos][0], head_parts[head_pos], head_grads[head_pos]
        )
        first_list.append(first_grad)
        kept_list.append(kept_grads)
    first_grads = jnp.stack(first_list)
    outgoing = pass_state(
        jnp.where(seq_first, 0.0, device_decay),
        jnp.where(seq_first, 0.0, first_grads),
        -1,
        seq_span,
        seq_stride,
    )
    found_list = []
    for head_pos in range(local_heads):
        head_part = slices[head_pos]
        found_list.append(
            head_rest(
                head_part[0],
                head_part[1],
                head_part[2],
                head_part[4],
                summaries[head_pos][0],
                head_starts[head_pos],
                head_parts[head_pos],
                kept_list[head_pos],
                outgoing[head_pos],
            )
        )
    query_grad = jnp.concatenate([found[0].reshape(row_count, DH) for found in found_list], axis=1)
    key_grad = jnp.concatenate([found[1].reshape(row_count, DH) for found in found_list], axis=1)
    value_grad = jnp.concatenate([found[2].reshape(row_count, DH) for found in found_list], axis=1)
    in_grad = jnp.stack([found[3].reshape(row_count) for found in found_list], axis=1)
    forget_grad = jnp.stack([found[4].reshape(row_count) for found in found_list], axis=1)
    pre_low = jnp.stack([in_grad, forget_grad], axis=1).astype(jnp.bfloat16)
    pre_grad = lax.all_gather(pre_low, "tensor", axis=2, tiled=True).reshape(
        row_count, 2 * head_count
    )
    grad_gate_bias = jnp.sum(pre_grad.astype(jnp.float32), axis=0)
    grad_gate_weight = jnp.stack(
        [
            inner_rows(queries, pre_grad),
            inner_rows(key_vecs, pre_grad),
            inner_rows(value_vecs, pre_grad),
        ]
    )
    query_grad = query_grad + outer_cols(pre_grad, gate_weight[0])
    key_grad = key_grad + outer_cols(pre_grad, gate_weight[1])
    value_grad = value_grad + outer_cols(pre_grad, gate_weight[2])
    block_size = query_weight.shape[1]
    grad_query = band_grad(query_grad, active, block_size)
    grad_key = band_grad(key_grad, active, block_size)
    grad_value = band_grad(value_grad, inner_act, block_size)
    active_grad = (
        active_grad
        + band_apply(query_grad, jnp.swapaxes(query_weight, 1, 2))
        + band_apply(key_grad, jnp.swapaxes(key_weight, 1, 2))
    )
    inner_grad = band_apply(value_grad, jnp.swapaxes(value_weight, 1, 2))
    conv_sig = jax.nn.sigmoid(conv_out)
    conv_grad = active_grad * conv_sig * (1.0 + conv_out * (1.0 - conv_sig))
    grad_conv_bias = jnp.sum(conv_grad, axis=0)
    grad_conv_weight = jnp.stack(
        [
            jnp.sum(
                conv_grad
                * padded[kernel_size - 1 - tap_pos : kernel_size - 1 - tap_pos + row_count],
                axis=0,
            )
            for tap_pos in range(kernel_size)
        ]
    )
    after_rows = shifted(conv_grad[: kernel_size - 1], "dp", -seq_stride)
    after_rows = jnp.where(seq_last, 0.0, after_rows)
    padded_grad = jnp.concatenate([conv_grad, after_rows], axis=0)
    for tap_pos in range(kernel_size):
        inner_grad = inner_grad + conv_weight[tap_pos] * padded_grad[tap_pos : tap_pos + row_count]
    inner_low = inner_grad.astype(jnp.bfloat16)
    normed_part = outer_cols(inner_low, up_inner) + outer_cols(gate_in_grad, up_gate)
    grad_up_inner = inner_rows(normed, inner_low)
    grad_up_gate = inner_rows(normed, gate_in_grad)
    width_share = model_width // lax.axis_size("tensor")
    column_start = tensor_place * width_share
    normed_grad = lax.psum(normed_part, "tensor")
    token_grad = lax.dynamic_slice_in_dim(
        layer_back(normed_grad * ln_weight, normed_hat, inverse), column_start, width_share, axis=1
    )
    grad_ln = lax.dynamic_slice_in_dim(
        jnp.sum(normed_grad * normed_hat, axis=0), column_start, width_share, axis=0
    )
    token_grad = token_grad + cotangent.astype(jnp.float32)
    summed = lax.psum(
        (
            grad_ln,
            grad_up_inner,
            grad_up_gate,
            grad_conv_weight,
            grad_conv_bias,
            grad_query,
            grad_key,
            grad_value,
            grad_gate_weight,
            grad_gate_bias,
            grad_group,
            grad_skip,
            grad_down,
        ),
        "dp",
    )
    return (result.astype(jnp.bfloat16), token_grad) + tuple(summed) + (rms_single,)


def solution(mesh):
    in_specs = (
        P("dp", "tensor"),
        P("dp", "tensor"),
        P(),
        P(None, "tensor"),
        P(None, "tensor"),
        P(None, "tensor"),
        P("tensor"),
        P("tensor", None, None),
        P("tensor", None, None),
        P("tensor", None, None),
        P(None, "tensor", None),
        P(),
        P("tensor"),
        P("tensor"),
        P("tensor", None),
    )
    out_specs = (
        P("dp", "tensor"),
        P("dp", "tensor"),
        P("tensor"),
        P(None, "tensor"),
        P(None, "tensor"),
        P(None, "tensor"),
        P("tensor"),
        P("tensor", None, None),
        P("tensor", None, None),
        P("tensor", None, None),
        P(None, "tensor", None),
        P(),
        P("tensor"),
        P("tensor"),
        P("tensor", None),
        P(),
    )
    return jax.shard_map(
        on_device, mesh=mesh, in_specs=in_specs, out_specs=out_specs, check_vma=False
    )
```

profile of v0, /device:TPU:0, one launch (start us, length us, event | category | flops | bytes accessed | tf_op | source)
XLA Modules:
  0.0 2474.9 jit_solution(7401666522847185554)
XLA Ops:
  89.1 11.2 fusion.40
  110.5 13.5 add_convert_fusion.1
  127.7 9.9 add_convert_fusion.2
  165.3 45.3 %while.136 = (s32[]{:T(128)}, f32[513,512]{1,0:T(8,128)S(1)}, f32[16]{0:T(128)S(1)}, f32[16,513,512]{2,1,0:T(8,128)}, s32[]{:T(128)}, /*index=5*/s32[]{:T(128)}) while((s32[]{:T(128)}, f32[513,512]{1,0:T(8,128)S(1)}, f32[16]{0:T(128)S(1)}, f32[16,513,512]{2,1,0:T(8,128)}, s32[]{:T(128)}, /*index=5*/s32[]{:T(128)}) %tuple.506), condition=%wide.region_8.9_spmd.clone, body=%wide.region_7.8_spmd.clone.sunk | while | flops 787971 | bytes 3151971 | solution.py:108
  224.1 64.0 %while.137 = (s32[]{:T(128)}, f32[513,512]{1,0:T(8,128)}, f32[16]{0:T(128)S(1)}, f32[16,513,512]{2,1,0:T(8,128)}, s32[]{:T(128)}, /*index=5*/s32[]{:T(128)}) while((s32[]{:T(128)}, f32[513,512]{1,0:T(8,128)}, f32[16]{0:T(128)S(1)}, f32[16,513,512]{2,1,0:T(8,128)}, s32[]{:T(128)}, /*index=5*/s32[]{:T(128)}) %tuple.503), condition=%wide.region_10.11_spmd.clone, body=%wide.region_9.10_spmd.clone.sunk | while | flops 787971 | bytes 3151971 | solution.py:108
  296.8 368.4 %while.130 = (s32[]{:T(128)}, f32[2,513,512]{2,0,1:T(2,128)}, f32[2]{0:T(128)S(1)}, f32[2,513,512]{2,0,1:T(2,128)}, s32[]{:T(128)}) while((s32[]{:T(128)}, f32[2,513,512]{2,0,1:T(2,128)}, f32[2]{0:T(128)S(1)}, f32[2,513,512]{2,0,1:T(2,128)}, s32[]{:T(128)}) %tuple.509), condition=%wide.region_12.13_spmd, body=%wide.region_11.12_spmd.sunk | while | flops 1050626 | bytes 14708845 | solution.py:269
  306.5 44.4 %collective-permute-done = f32[2,513,512]{2,0,1:T(2,128)} collective-permute-done((f32[2,513,512]{2,0,1:T(2,128)}, f32[2,513,512]{2,0,1:T(2,128)}, u32[]{:S(2)}, u32[]{:S(2)}) %collective-permute-start) | collective-permute-done | bytes 2101280 | tf_op jit(solution)/shard_map/while/body/eval_jaxpr/ppermute | solution.py:19
  361.4 43.6 %collective-permute-done = f32[2,513,512]{2,0,1:T(2,128)} collective-permute-done((f32[2,513,512]{2,0,1:T(2,128)}, f32[2,513,512]{2,0,1:T(2,128)}, u32[]{:S(2)}, u32[]{:S(2)}) %collective-permute-start) | collective-permute-done | bytes 2101280 | tf_op jit(solution)/shard_map/while/body/eval_jaxpr/ppermute | solution.py:19
  415.4 42.7 %collective-permute-done = f32[2,513,512]{2,0,1:T(2,128)} collective-permute-done((f32[2,513,512]{2,0,1:T(2,128)}, f32[2,513,512]{2,0,1:T(2,128)}, u32[]{:S(2)}, u32[]{:S(2)}) %collective-permute-start) | collective-permute-done | bytes 2101280 | tf_op jit(solution)/shard_map/while/body/eval_jaxpr/ppermute | solution.py:19
  469.4 41.8 %collective-permute-done = f32[2,513,512]{2,0,1:T(2,128)} collective-permute-done((f32[2,513,512]{2,0,1:T(2,128)}, f32[2,513,512]{2,0,1:T(2,128)}, u32[]{:S(2)}, u32[]{:S(2)}) %collective-permute-start) | collective-permute-done | bytes 2101280 | tf_op jit(solution)/shard_map/while/body/eval_jaxpr/ppermute | solution.py:19
  522.5 40.9 %collective-permute-done = f32[2,513,512]{2,0,1:T(2,128)} collective-permute-done((f32[2,513,512]{2,0,1:T(2,128)}, f32[2,513,512]{2,0,1:T(2,128)}, u32[]{:S(2)}, u32[]{:S(2)}) %collective-permute-start) | collective-permute-done | bytes 2101280 | tf_op jit(solution)/shard_map/while/body/eval_jaxpr/ppermute | solution.py:19
  574.7 39.9 %collective-permute-done = f32[2,513,512]{2,0,1:T(2,128)} collective-permute-done((f32[2,513,512]{2,0,1:T(2,128)}, f32[2,513,512]{2,0,1:T(2,128)}, u32[]{:S(2)}, u32[]{:S(2)}) %collective-permute-start) | collective-permute-done | bytes 2101280 | tf_op jit(solution)/shard_map/while/body/eval_jaxpr/ppermute | solution.py:19
  626.0 39.0 %collective-permute-done = f32[2,513,512]{2,0,1:T(2,128)} collective-permute-done((f32[2,513,512]{2,0,1:T(2,128)}, f32[2,513,512]{2,0,1:T(2,128)}, u32[]{:S(2)}, u32[]{:S(2)}) %collective-permute-start) | collective-permute-done | bytes 2101280 | tf_op jit(solution)/shard_map/while/body/eval_jaxpr/ppermute | solution.py:19
  676.8 95.4 %while.131 = (s32[]{:T(128)}, f32[513,512]{1,0:T(8,128)}, f32[16,513,512]{2,1,0:T(8,128)}, f32[16]{0:T(128)S(1)}, f32[16,513,512]{2,1,0:T(8,128)}, /*index=5*/s32[]{:T(128)}) while((s32[]{:T(128)}, f32[513,512]{1,0:T(8,128)}, f32[16,513,512]{2,1,0:T(8,128)}, f32[16]{0:T(128)S(1)}, f32[16,513,512]{2,1,0:T(8,128)}, ...), condition=%wide.region_14.15_spmd, body=%wide.region_13.14_spmd.sunk | while | flops 525314 | bytes 7369305 | solution.py:108
  772.2 11.0 copy.954
  791.8 9.1 fusion.44
  825.0 61.5 %while.132 = (s32[]{:T(128)}, f32[513,512]{1,0:T(8,128)S(1)}, f32[16,513,512]{2,1,0:T(8,128)}, f32[16]{0:T(128)S(1)}, f32[16,513,512]{2,1,0:T(8,128)}, /*index=5*/s32[]{:T(128)}) while((s32[]{:T(128)}, f32[513,512]{1,0:T(8,128)S(1)}, f32[16,513,512]{2,1,0:T(8,128)}, f32[16]{0:T(128)S(1)}, f32[16,513,512]{2,1,0:T(8,128)}, ...), condition=%wide.region_17.18_spmd, body=%wide.region_16.17_spmd.sunk | while | flops 525314 | bytes 7369305 | solution.py:108
  886.6 11.3 copy.962
  951.0 12.1 pad_maximum_fusion.2
  963.1 45.3 %while.138 = (s32[]{:T(128)}, f32[513,512]{1,0:T(8,128)S(1)}, f32[16,513,512]{2,1,0:T(8,128)}, f32[16]{0:T(128)S(1)}, s32[]{:T(128)}, /*index=5*/s32[]{:T(128)}, s32[]{:T(128)}) while((s32[]{:T(128)}, f32[513,512]{1,0:T(8,128)S(1)}, f32[16,513,512]{2,1,0:T(8,128)}, f32[16]{0:T(128)S(1)}, s32[]{:T(128)}, /*index=5*/s32[]{:T(128)}, ...), condition=%wide.region_26.27_spmd.clone, body=%wide.region_25.26_spmd.clone.sunk | while | flops 787972 | bytes 3151991 | solution.py:117
  1023.7 12.0 pad_maximum_fusion.3
  1035.8 45.3 %while.139 = (s32[]{:T(128)}, f32[513,512]{1,0:T(8,128)S(1)}, f32[16,513,512]{2,1,0:T(8,128)}, f32[16]{0:T(128)S(1)}, s32[]{:T(128)}, /*index=5*/s32[]{:T(128)}, s32[]{:T(128)}) while((s32[]{:T(128)}, f32[513,512]{1,0:T(8,128)S(1)}, f32[16,513,512]{2,1,0:T(8,128)}, f32[16]{0:T(128)S(1)}, s32[]{:T(128)}, /*index=5*/s32[]{:T(128)}, ...), condition=%wide.region_29.30_spmd.clone, body=%wide.region_28.29_spmd.clone.sunk | while | flops 787972 | bytes 3151991 | solution.py:117
  1087.4 331.1 %while.133 = (s32[]{:T(128)}, f32[2,513,512]{2,0,1:T(2,128)}, f32[2]{0:T(128)S(1)}, f32[2,513,512]{2,0,1:T(2,128)}, s32[]{:T(128)}) while((s32[]{:T(128)}, f32[2,513,512]{2,0,1:T(2,128)}, f32[2]{0:T(128)S(1)}, f32[2,513,512]{2,0,1:T(2,128)}, s32[]{:T(128)}) %tuple.555), condition=%wide.region_31.32_spmd, body=%wide.region_30.31_spmd.sunk | while | flops 1050626 | bytes 14708845 | solution.py:269
  1093.8 44.2 %collective-permute-done.1 = f32[2,513,512]{2,0,1:T(2,128)} collective-permute-done((f32[2,513,512]{2,0,1:T(2,128)}, f32[2,513,512]{2,0,1:T(2,128)}, u32[]{:S(2)}, u32[]{:S(2)}) %collective-permute-start.1) | collective-permute-done | bytes 2101280 | tf_op jit(solution)/shard_map/while/body/eval_jaxpr/ppermute | solution.py:19
  1144.0 43.6 %collective-permute-done.1 = f32[2,513,512]{2,0,1:T(2,128)} collective-permute-done((f32[2,513,512]{2,0,1:T(2,128)}, f32[2,513,512]{2,0,1:T(2,128)}, u32[]{:S(2)}, u32[]{:S(2)}) %collective-permute-start.1) | collective-permute-done | bytes 2101280 | tf_op jit(solution)/shard_map/while/body/eval_jaxpr/ppermute | solution.py:19
  1193.6 41.9 %collective-permute-done.1 = f32[2,513,512]{2,0,1:T(2,128)} collective-permute-done((f32[2,513,512]{2,0,1:T(2,128)}, f32[2,513,512]{2,0,1:T(2,128)}, u32[]{:S(2)}, u32[]{:S(2)}) %collective-permute-start.1) | collective-permute-done | bytes 2101280 | tf_op jit(solution)/shard_map/while/body/eval_jaxpr/ppermute | solution.py:19
  1241.4 41.0 %collective-permute-done.1 = f32[2,513,512]{2,0,1:T(2,128)} collective-permute-done((f32[2,513,512]{2,0,1:T(2,128)}, f32[2,513,512]{2,0,1:T(2,128)}, u32[]{:S(2)}, u32[]{:S(2)}) %collective-permute-start.1) | collective-permute-done | bytes 2101280 | tf_op jit(solution)/shard_map/while/body/eval_jaxpr/ppermute | solution.py:19
  1288.4 40.0 %collective-permute-done.1 = f32[2,513,512]{2,0,1:T(2,128)} collective-permute-done((f32[2,513,512]{2,0,1:T(2,128)}, f32[2,513,512]{2,0,1:T(2,128)}, u32[]{:S(2)}, u32[]{:S(2)}) %collective-permute-start.1) | collective-permute-done | bytes 2101280 | tf_op jit(solution)/shard_map/while/body/eval_jaxpr/ppermute | solution.py:19
  1334.4 39.9 %collective-permute-done.1 = f32[2,513,512]{2,0,1:T(2,128)} collective-permute-done((f32[2,513,512]{2,0,1:T(2,128)}, f32[2,513,512]{2,0,1:T(2,128)}, u32[]{:S(2)}, u32[]{:S(2)}) %collective-permute-start.1) | collective-permute-done | bytes 2101280 | tf_op jit(solution)/shard_map/while/body/eval_jaxpr/ppermute | solution.py:19
  1380.3 38.3 %collective-permute-done.1 = f32[2,513,512]{2,0,1:T(2,128)} collective-permute-done((f32[2,513,512]{2,0,1:T(2,128)}, f32[2,513,512]{2,0,1:T(2,128)}, u32[]{:S(2)}, u32[]{:S(2)}) %collective-permute-start.1) | collective-permute-done | bytes 2101280 | tf_op jit(solution)/shard_map/while/body/eval_jaxpr/ppermute | solution.py:19
  1429.8 96.1 %while.134 = (s32[]{:T(128)}, f32[513,512]{1,0:T(8,128)}, f32[16,513,512]{2,1,0:T(8,128)}, f32[16,513,512]{2,1,0:T(8,128)}, f32[16]{0:T(128)S(1)}, /*index=5*/s32[]{:T(128)}, s32[]{:T(128)}) while((s32[]{:T(128)}, f32[513,512]{1,0:T(8,128)}, f32[16,513,512]{2,1,0:T(8,128)}, f32[16,513,512]{2,1,0:T(8,128)}, f32[16]{0:T(128)S(1)}, ...), condition=%wide.region_33.34_spmd, body=%wide.region_32.33_spmd.sunk | while | flops 525315 | bytes 7368817 | solution.py:117
  1528.2 12.4 multiply_reduce_fusion.1
  1542.2 9.8 fusion.52
  1569.2 61.7 %while.135 = (s32[]{:T(128)}, f32[513,512]{1,0:T(8,128)S(1)}, f32[16,513,512]{2,1,0:T(8,128)}, f32[16,513,512]{2,1,0:T(8,128)}, f32[16]{0:T(128)S(1)}, /*index=5*/s32[]{:T(128)}, s32[]{:T(128)}) while((s32[]{:T(128)}, f32[513,512]{1,0:T(8,128)S(1)}, f32[16,513,512]{2,1,0:T(8,128)}, f32[16,513,512]{2,1,0:T(8,128)}, f32[16]{0:T(128)S(1)}, ...), condition=%wide.region_35.36_spmd, body=%wide.region_34.35_spmd.sunk | while | flops 525315 | bytes 7368817 | solution.py:117
  1633.3 12.4 multiply_reduce_fusion
  1647.2 9.9 fusion.54
  1659.8 9.0 fusion.48
  1712.2 13.3 multiply_reduce_fusion.7
  1738.6 10.4 fusion.43
  1749.0 10.6 fusion.45
  1790.9 17.9 multiply_reduce_fusion.13
  1838.8 33.3 %multiply_reduce_fusion.27 = (f32[1024]{0:T(1024)}, f32[1024]{0:T(1024)}, f32[1024]{0:T(1024)}, f32[1024]{0:T(1024)}, f32[1024]{0:T(1024)}, /*index=5*/f32[1024,1024]{0,1:T(8,128)}) fusion(f32[1024,1024]{0,1:T(8,128)} %copy-done.1, f32[3,1024]{0,1:T(8,128)S(1)} %copy-done.64, f32[1024,1024]{0,1:T(8,128)} %copy-done.6, f32[1024,3]{0,1:T(4,128)S(1)} %get-tuple-element.900, ...), kind=kLoop, calls=%fused_computation.144 | loop fusion | flops 63958016 | bytes 75591680 | tf_op jit(solution)/shard_map/reduce_sum | solution.py:470
  1879.8 10.2 collective-permute-done.3
  1890.2 16.2 fusion.6
  1924.7 10.9 multiply_reduce_fusion.12
  1983.1 41.8 %psum.127 = f32[]{:T(128)} all-reduce(f32[]{:T(128)} %get-tuple-element.937), channel_id=1, replica_groups=mesh['dp'=16,'tensor'=2] {'dp','tensor'}, use_global_device_ids=true, to_apply=%region_99.100 | all-reduce | flops 1 | bytes 8 | tf_op jit(solution)/shard_map/psum | solution.py:382
  2025.6 51.6 %all-reduce.8.cloned.1.call-done = (f32[512]{0:T(512)}, f32[4,1024]{1,0:T(4,128)}, f32[1024]{0:T(1024)}, f32[256,4,4]{0,2,1:T(4,128)}, f32[256,4,4]{0,2,1:T(4,12...) async-done(((f32[512]{0:T(512)}, f32[4,1024]{1,0:T(4,128)}, f32[1024]{0:T(1024)}, f32[256,4,4]{0,2,1:T(4,128)}, f32[256,4,4]{0,2,1:T(4,128)}, ...) | async-done | bytes 79920 | tf_op jit(solution)/shard_map/psum | solution.py:497
  2077.2 373.7 %all-reduce.10.cloned.1.call-done = (f32[1024,1024]{1,0:T(8,128)}, f32[1024,1024]{1,0:T(8,128)}, f32[3,1024,8]{1,2,0:T(8,128)}, f32[1024,1024]{1,0:T(8,128)}) async-done(((f32[1024,1024]{1,0:T(8,128)}, f32[1024,1024]{1,0:T(8,128)}, f32[3,1024,8]{1,2,0:T(8,128)}, f32[1024,1024]{1,0:T(8,128)}), (f32[1024,1024]{1,0:T(8,128)}, f32[1024,1024]{1,0:T(8,128)}, f32[3,1024,8]{1,2,0:T(8,128)}, ...) | async-done | bytes 12681232 | tf_op jit(solution)/shard_map/psum | solution.py:497
  (1291 shorter events, 1137.7 us)
Async XLA Ops:
  7.2 917.3 %copy-start = (bf16[1024,1024]{1,0:T(8,128)(2,1)S(1)}, bf16[1024,1024]{1,0:T(8,128)(2,1)}, u32[]{:S(2)}) copy-start(bf16[1024,1024]{1,0:T(8,128)(2,1)} %param.53) | copy-start | bytes 6291460
  7.2 38.1 %all-gather.3.cloned.1.call-start = ((), (), s32[]{:S(2)}) async-start(), calls=%async_computation.1 | async-start | bytes 3145728 | tf_op jit(solution)/shard_map/all_gather | solution.py:290
  7.9 916.6 %all-gather.5.cloned.1.call-start = ((), (), s32[]{:S(2)}) async-start(), calls=%async_computation.3 | async-start | bytes 3145728 | tf_op jit(solution)/shard_map/all_gather | solution.py:291
  8.7 1952.3 %all-reduce.6.cloned.1.call-start = ((), (), s32[]{:S(2)}) async-start(), calls=%async_computation.4 | async-start | bytes 8388608 | tf_op jit(solution)/shard_map/psum | solution.py:489
  22.8 66.3 %copy-start.123 = (f32[1,1024]{1,0:T(1,128)}, f32[1,1024]{1,0:T(1,128)S(1)}, u32[]{:S(2)}) copy-start(f32[1,1024]{1,0:T(1,128)S(1)} %get-tuple-element.1086) | copy-start | bytes 12292
  22.8 66.3 %copy-start.125 = (f32[1,1024]{1,0:T(1,128)}, f32[1,1024]{1,0:T(1,128)S(1)}, u32[]{:S(2)}) copy-start(f32[1,1024]{1,0:T(1,128)S(1)} %get-tuple-element.1087) | copy-start | bytes 12292
  22.8 66.3 %copy-start.127 = (f32[1,1024]{1,0:T(1,128)}, f32[1,1024]{1,0:T(1,128)S(1)}, u32[]{:S(2)}) copy-start(f32[1,1024]{1,0:T(1,128)S(1)} %get-tuple-element.1088) | copy-start | bytes 12292
  22.9 66.3 %copy-start.129 = (f32[1,1024]{1,0:T(1,128)}, f32[1,1024]{1,0:T(1,128)S(1)}, u32[]{:S(2)}) copy-start(f32[1,1024]{1,0:T(1,128)S(1)} %get-tuple-element.1089) | copy-start | bytes 12292
  32.5 17.2 copy-start.180
  47.4 30.6 %copy-start.121 = (f32[1024]{0:T(1024)}, f32[1024]{0:T(1024)S(1)}, u32[]{:S(2)}) copy-start(f32[1024]{0:T(1024)S(1)} %broadcast_multiply_fusion.6) | copy-start | bytes 12292
  49.8 28.3 %copy-start.119 = (f32[1024]{0:T(1024)}, f32[1024]{0:T(1024)S(1)}, u32[]{:S(2)}) copy-start(f32[1024]{0:T(1024)S(1)} %add_rsqrt_fusion.1) | copy-start | bytes 12292
  52.6 16.5 copy-start.1
  63.4 25.6 %collective-permute-start.2 = (f32[3,1024]{0,1:T(8,128)}, f32[3,1024]{0,1:T(8,128)}, u32[]{:S(2)}, u32[]{:S(2)}) collective-permute-start(f32[3,1024]{0,1:T(8,128)} %slice.1092), channel_id=1, source_target_pairs={{0,4},{2,6},{4,8},{6,10},{8,12},{10,14},{12,16},{14,18},{16,20},{1... | collective-permute-start | bytes 36872 | tf_op jit(solution)/shard_map/ppermute | solution.py:19
  100.4 26.2 %copy-start.6 = (f32[1024,1024]{0,1:T(8,128)}, f32[1024,1024]{0,1:T(8,128)S(1)}, u32[]{:S(2)}) copy-start(f32[1024,1024]{0,1:T(8,128)S(1)} %get-tuple-element.866) | copy-start | bytes 12582916
  110.4 16.2 copy-start.13
  110.4 16.2 copy-start.14
  110.4 16.1 copy-start.84
  110.4 16.1 copy-start.85
  110.5 16.1 copy-start.105
  110.5 16.1 copy-start.106
  110.5 16.1 copy-start.113
  110.5 16.1 copy-start.115
  110.5 16.1 copy-start.17
  213.1 591.1 %copy-start.19 = (bf16[1024,512]{1,0:T(8,128)(2,1)}, bf16[1024,512]{1,0:T(8,128)(2,1)S(1)}, u32[]{:S(2)}) copy-start(bf16[1024,512]{1,0:T(8,128)(2,1)S(1)} %copy.946) | copy-start | bytes 3145732
  301.5 49.5 %collective-permute-start = (f32[2,513,512]{2,0,1:T(2,128)}, f32[2,513,512]{2,0,1:T(2,128)}, u32[]{:S(2)}, u32[]{:S(2)}) collective-permute-start(f32[2,513,512]{2,0,1:T(2,128)} %multiply_add_fusion.11), channel_id=1, source_target_pairs={{0,4},{2,6},{4,8},{6,10},{8,12},{10,14},{12,16},{14,18},{16,20},{1... | collective-permute-start | bytes 6303752 | tf_op jit(solution)/shard_map/while/body/eval_jaxpr/ppermute | solution.py:19
  355.6 49.4 %collective-permute-start = (f32[2,513,512]{2,0,1:T(2,128)}, f32[2,513,512]{2,0,1:T(2,128)}, u32[]{:S(2)}, u32[]{:S(2)}) collective-permute-start(f32[2,513,512]{2,0,1:T(2,128)} %multiply_add_fusion.11), channel_id=1, source_target_pairs={{0,4},{2,6},{4,8},{6,10},{8,12},{10,14},{12,16},{14,18},{16,20},{1... | collective-permute-start | bytes 6303752 | tf_op jit(solution)/shard_map/while/body/eval_jaxpr/ppermute | solution.py:19
  409.7 48.4 %collective-permute-start = (f32[2,513,512]{2,0,1:T(2,128)}, f32[2,513,512]{2,0,1:T(2,128)}, u32[]{:S(2)}, u32[]{:S(2)}) collective-permute-start(f32[2,513,512]{2,0,1:T(2,128)} %multiply_add_fusion.11), channel_id=1, source_target_pairs={{0,4},{2,6},{4,8},{6,10},{8,12},{10,14},{12,16},{14,18},{16,20},{1... | collective-permute-start | bytes 6303752 | tf_op jit(solution)/shard_map/while/body/eval_jaxpr/ppermute | solution.py:19
  462.8 48.4 %collective-permute-start = (f32[2,513,512]{2,0,1:T(2,128)}, f32[2,513,512]{2,0,1:T(2,128)}, u32[]{:S(2)}, u32[]{:S(2)}) collective-permute-start(f32[2,513,512]{2,0,1:T(2,128)} %multiply_add_fusion.11), channel_id=1, source_target_pairs={{0,4},{2,6},{4,8},{6,10},{8,12},{10,14},{12,16},{14,18},{16,20},{1... | collective-permute-start | bytes 6303752 | tf_op jit(solution)/shard_map/while/body/eval_jaxpr/ppermute | solution.py:19
  515.9 47.5 %collective-permute-start = (f32[2,513,512]{2,0,1:T(2,128)}, f32[2,513,512]{2,0,1:T(2,128)}, u32[]{:S(2)}, u32[]{:S(2)}) collective-permute-start(f32[2,513,512]{2,0,1:T(2,128)} %multiply_add_fusion.11), channel_id=1, source_target_pairs={{0,4},{2,6},{4,8},{6,10},{8,12},{10,14},{12,16},{14,18},{16,20},{1... | collective-permute-start | bytes 6303752 | tf_op jit(solution)/shard_map/while/body/eval_jaxpr/ppermute | solution.py:19
  568.1 46.6 %collective-permute-start = (f32[2,513,512]{2,0,1:T(2,128)}, f32[2,513,512]{2,0,1:T(2,128)}, u32[]{:S(2)}, u32[]{:S(2)}) collective-permute-start(f32[2,513,512]{2,0,1:T(2,128)} %multiply_add_fusion.11), channel_id=1, source_target_pairs={{0,4},{2,6},{4,8},{6,10},{8,12},{10,14},{12,16},{14,18},{16,20},{1... | collective-permute-start | bytes 6303752 | tf_op jit(solution)/shard_map/while/body/eval_jaxpr/ppermute | solution.py:19
  619.3 45.7 %collective-permute-start = (f32[2,513,512]{2,0,1:T(2,128)}, f32[2,513,512]{2,0,1:T(2,128)}, u32[]{:S(2)}, u32[]{:S(2)}) collective-permute-start(f32[2,513,512]{2,0,1:T(2,128)} %multiply_add_fusion.11), channel_id=1, source_target_pairs={{0,4},{2,6},{4,8},{6,10},{8,12},{10,14},{12,16},{14,18},{16,20},{1... | collective-permute-start | bytes 6303752 | tf_op jit(solution)/shard_map/while/body/eval_jaxpr/ppermute | solution.py:19
  886.6 17.7 copy-start.27
  905.4 740.2 %copy-start.99 = (f32[16,64]{1,0:T(8,128)}, f32[16,64]{1,0:T(8,128)S(1)}, u32[]{:S(2)}) copy-start(f32[16,64]{1,0:T(8,128)S(1)} %copy.960) | copy-start | bytes 12292
  1092.5 45.5 %collective-permute-start.1 = (f32[2,513,512]{2,0,1:T(2,128)}, f32[2,513,512]{2,0,1:T(2,128)}, u32[]{:S(2)}, u32[]{:S(2)}) collective-permute-start(f32[2,513,512]{2,0,1:T(2,128)} %multiply_add_fusion.12), channel_id=1, source_target_pairs={{4,0},{6,2},{8,4},{10,6},{12,8},{14,10},{16,12},{18,14},{20,16},{2... | collective-permute-start | bytes 6303752 | tf_op jit(solution)/shard_map/while/body/eval_jaxpr/ppermute | solution.py:19
  1142.7 44.8 %collective-permute-start.1 = (f32[2,513,512]{2,0,1:T(2,128)}, f32[2,513,512]{2,0,1:T(2,128)}, u32[]{:S(2)}, u32[]{:S(2)}) collective-permute-start(f32[2,513,512]{2,0,1:T(2,128)} %multiply_add_fusion.12), channel_id=1, source_target_pairs={{4,0},{6,2},{8,4},{10,6},{12,8},{14,10},{16,12},{18,14},{20,16},{2... | collective-permute-start | bytes 6303752 | tf_op jit(solution)/shard_map/while/body/eval_jaxpr/ppermute | solution.py:19
  1192.3 43.2 %collective-permute-start.1 = (f32[2,513,512]{2,0,1:T(2,128)}, f32[2,513,512]{2,0,1:T(2,128)}, u32[]{:S(2)}, u32[]{:S(2)}) collective-permute-start(f32[2,513,512]{2,0,1:T(2,128)} %multiply_add_fusion.12), channel_id=1, source_target_pairs={{4,0},{6,2},{8,4},{10,6},{12,8},{14,10},{16,12},{18,14},{20,16},{2... | collective-permute-start | bytes 6303752 | tf_op jit(solution)/shard_map/while/body/eval_jaxpr/ppermute | solution.py:19
  1240.1 42.2 %collective-permute-start.1 = (f32[2,513,512]{2,0,1:T(2,128)}, f32[2,513,512]{2,0,1:T(2,128)}, u32[]{:S(2)}, u32[]{:S(2)}) collective-permute-start(f32[2,513,512]{2,0,1:T(2,128)} %multiply_add_fusion.12), channel_id=1, source_target_pairs={{4,0},{6,2},{8,4},{10,6},{12,8},{14,10},{16,12},{18,14},{20,16},{2... | collective-permute-start | bytes 6303752 | tf_op jit(solution)/shard_map/while/body/eval_jaxpr/ppermute | solution.py:19
  1287.1 41.3 %collective-permute-start.1 = (f32[2,513,512]{2,0,1:T(2,128)}, f32[2,513,512]{2,0,1:T(2,128)}, u32[]{:S(2)}, u32[]{:S(2)}) collective-permute-start(f32[2,513,512]{2,0,1:T(2,128)} %multiply_add_fusion.12), channel_id=1, source_target_pairs={{4,0},{6,2},{8,4},{10,6},{12,8},{14,10},{16,12},{18,14},{20,16},{2... | collective-permute-start | bytes 6303752 | tf_op jit(solution)/shard_map/while/body/eval_jaxpr/ppermute | solution.py:19
  1333.1 41.2 %collective-permute-start.1 = (f32[2,513,512]{2,0,1:T(2,128)}, f32[2,513,512]{2,0,1:T(2,128)}, u32[]{:S(2)}, u32[]{:S(2)}) collective-permute-start(f32[2,513,512]{2,0,1:T(2,128)} %multiply_add_fusion.12), channel_id=1, source_target_pairs={{4,0},{6,2},{8,4},{10,6},{12,8},{14,10},{16,12},{18,14},{20,16},{2... | collective-permute-start | bytes 6303752 | tf_op jit(solution)/shard_map/while/body/eval_jaxpr/ppermute | solution.py:19
  1379.0 39.6 %collective-permute-start.1 = (f32[2,513,512]{2,0,1:T(2,128)}, f32[2,513,512]{2,0,1:T(2,128)}, u32[]{:S(2)}, u32[]{:S(2)}) collective-permute-start(f32[2,513,512]{2,0,1:T(2,128)} %multiply_add_fusion.12), channel_id=1, source_target_pairs={{4,0},{6,2},{8,4},{10,6},{12,8},{14,10},{16,12},{18,14},{20,16},{2... | collective-permute-start | bytes 6303752 | tf_op jit(solution)/shard_map/while/body/eval_jaxpr/ppermute | solution.py:19
  1668.9 16.4 copy-start.77
  1668.9 22.6 copy-start.135
  1668.9 22.7 copy-start.79
  1873.2 16.8 collective-permute-start.3
  1890.2 17.5 copy-start.185
  1912.1 67.3 %reduce-scatter.2.cloned.1.call-start = ((), (), s32[]{:S(2)}) async-start(), calls=%async_computation.2 | async-start | bytes 6291456 | tf_op jit(solution)/shard_map/reduce_scatter | solution.py:380
  1918.9 158.3 %all-reduce.8.cloned.1.call-start = ((), (), s32[]{:S(2)}) async-start(), calls=%async_computation.5 | async-start | bytes 160768 | tf_op jit(solution)/shard_map/psum | solution.py:497
  1968.0 482.9 %all-reduce.10.cloned.1.call-start = ((), (), s32[]{:S(2)}) async-start(), calls=%async_computation.6 | async-start | bytes 25362432 | tf_op jit(solution)/shard_map/psum | solution.py:497
  (166 other events, 1264.9 us)
Sparse Core Ops, SparseCore 0:
  9.6 13.2 all-gather.2
  24.4 11.7 all-gather.4
  1912.3 29.7 all-reduce.5
  1944.8 13.1 reduce-scatter.1
  1968.1 109.0 all-reduce.7
  2085.2 365.6 all-reduce.9
where the time goes:
time: 2490 us; the launch traced here: 2470 us
  waiting for transfers between devices  1020 us (41%)
  other arithmetic  614 us (25%)
  local copies, waits for them, and re-layouts  477 us (19%)
  matrix products  236 us (9%)
  starting transfers between devices  59.6 us (2%)
  blocking collectives  47 us (2%)
    ppermute x16, waiting for transfers between devices, shifted(): return lax.ppermute(block, axis, route)  591 us
    psum x2, waiting for transfers between devices, on_device(): lax.psum((grad_ln, grad_up_inner, grad_up_gate, grad_conv_weight, grad_co...  425 us
    add x64, other arithmetic, advance(): return (decay_now * state_now + update_now, state_now)  174 us
    add x64, other arithmetic, retreat(): return (local_now + decay_now * grad_end, grad_end)  155 us
    another operation x72, local copies, waits for them, and re-layouts  77.5 us
    dynamic_slice x128, local copies, waits for them, and re-layouts, chain_forward(): return lax.scan(advance, initial, (decays, updates))  74.7 us
    dynamic_update_slice x64, local copies, waits for them, and re-layouts, chain_forward(): return lax.scan(advance, initial, (decays, updates))  68.1 us
    add x14, other arithmetic, relay_round(): decays[:, None, None] * incoming + states  65.8 us
  transfers between devices with their start and end apart: 22, of which 17 were waited for; matrix products, arithmetic and copies ran while one was open for 25% of the time, Pallas kernels for 0%

commit v1 on v0

v1 whole, which is shorter than its diff:
```python
import jax
import jax.numpy as jnp
from jax import lax
from jax.experimental import pallas as pl
from jax.experimental.pallas import tpu as pltpu
from jax.sharding import PartitionSpec as P

DH = 512
BLOCK = 64
QB = 4
SEQ_LEN = 8192
TILE = 256
GROUP = 256
HALO = 16
LANES = 128
NORM_EPS = 1e-05
PACK = DH + 16
WIDE = DH + 8
SMALL = 56

f32 = jnp.float32
bf16 = jnp.bfloat16
highest = lax.Precision.HIGHEST


def mm(left, right):
    return lax.dot_general(left, right, (((1,), (0,)), ((), ())), preferred_element_type=f32)


def mm_tn(left, right):
    return lax.dot_general(left, right, (((0,), (0,)), ((), ())), preferred_element_type=f32)


def mm_nt(left, right):
    return lax.dot_general(left, right, (((1,), (1,)), ((), ())), preferred_element_type=f32)


def split2(value):
    high = value.astype(bf16)
    return high, (value - high.astype(f32)).astype(bf16)


def split3(value):
    high = value.astype(bf16)
    rest = value - high.astype(f32)
    mid = rest.astype(bf16)
    return high, mid, (rest - mid.astype(f32)).astype(bf16)


def sigmoid(value):
    return 1.0 / (1.0 + jnp.exp(-value))


def params(vmem_mib):
    return pltpu.CompilerParams(
        dimension_semantics=("arbitrary",), vmem_limit_bytes=vmem_mib * 1024 * 1024
    )


def cost(flops, moved):
    return pl.CostEstimate(flops=flops, bytes_accessed=moved, transcendentals=0)


def rows(width, tile=TILE, flip=0):
    if flip:
        return pl.BlockSpec((tile, width), lambda i: (flip - 1 - i, 0))
    return pl.BlockSpec((tile, width), lambda i: (i, 0))


def whole(*shape):
    return pl.BlockSpec(shape, lambda i: (0,) * len(shape))


smem = pl.BlockSpec(memory_space=pltpu.MemorySpace.SMEM)


def shape_of(*dims, dtype=f32):
    return jax.ShapeDtypeStruct(dims, dtype)


def normed_rows(x, ln):
    centered = x - jnp.mean(x, axis=1, keepdims=True)
    inverse = lax.rsqrt(jnp.mean(centered * centered, axis=1, keepdims=True) + NORM_EPS)
    return (centered * inverse * ln).astype(bf16)


def band_sum(value, coefs, reach):
    sums = [coef[reach : reach + 1] * value for coef in coefs]
    for offset in range(-reach, reach + 1):
        if offset != 0:
            moved = pltpu.roll(value, -offset % value.shape[1], 1)
            sums = [
                total + coef[reach + offset : reach + offset + 1] * moved for total, coef in zip(sums, coefs)
            ]
    return sums


def first_kernel(
    flag, x_ref, halo_ref, ln_ref, up_ref, cw_ref, cb_ref, coef_ref, gw_ref,
    normed_ref, inner_ref, conv_ref, active_ref, q_ref, k_ref, v_ref, pre_ref, pad_ref,
):
    step = pl.program_id(0)
    tile = x_ref.shape[0]

    @pl.when(step == 0)
    def _():
        before = mm(normed_rows(halo_ref[...].astype(f32), ln_ref[...]), up_ref[...])
        pad_ref[0:8, :] = jnp.where(flag[0] == 1, 0.0, before[HALO - 8 :, :])

    normed = normed_rows(x_ref[...].astype(f32), ln_ref[...])
    normed_ref[...] = normed
    inner = mm(normed, up_ref[...])
    inner_ref[...] = inner
    pad_ref[8:, :] = inner
    conv = cb_ref[...] + cw_ref[0:1, :] * inner
    for j in range(1, cw_ref.shape[0]):
        conv = conv + cw_ref[j : j + 1, :] * pad_ref[8 - j : 8 - j + tile, :]
    conv_ref[...] = conv
    pad_ref[0:8, :] = pad_ref[tile : tile + 8, :]
    active_ref[...] = conv * sigmoid(conv)
    reach = QB - 1
    for g in range(inner.shape[1] // LANES):
        part = slice(g * LANES, (g + 1) * LANES)
        query, key = band_sum(active_ref[:, part], (coef_ref[0, :, part], coef_ref[1, :, part]), reach)
        q_ref[:, part] = query.astype(bf16)
        k_ref[:, part] = key.astype(bf16)
        v_ref[:, part] = band_sum(inner_ref[:, part], (coef_ref[2, :, part],), reach)[0].astype(bf16)
    pre = mm(q_ref[...], gw_ref[0]) + mm(k_ref[...], gw_ref[1]) + mm(v_ref[...], gw_ref[2])
    pre_ref[...] = jnp.transpose(pre)[0:8, :]


def first_stage(flag, full, halo, ln, up, cw, cb, coefs, gw):
    count, width = full.shape
    chan = up.shape[1]
    wide = (count, chan)
    return pl.pallas_call(
        first_kernel,
        grid=(count // TILE,),
        in_specs=[
            smem, rows(width), whole(*halo.shape), whole(*ln.shape), whole(*up.shape), whole(*cw.shape),
            whole(*cb.shape), whole(*coefs.shape), whole(*gw.shape),
        ],
        out_specs=[rows(width), rows(chan), rows(chan), rows(chan), rows(chan), rows(chan), rows(chan),
                   pl.BlockSpec((8, TILE), lambda i: (0, i))],
        out_shape=[shape_of(count, width, dtype=bf16), shape_of(*wide), shape_of(*wide), shape_of(*wide),
                   shape_of(*wide, dtype=bf16), shape_of(*wide, dtype=bf16), shape_of(*wide, dtype=bf16),
                   shape_of(8, count)],
        scratch_shapes=[pltpu.VMEM((TILE + 8, chan), f32)],
        compiler_params=params(48),
        cost_estimate=cost(2 * count * width * chan * 4, count * chan * 20),
        name="first",
    )(flag, full, halo, ln, up, cw, cb, coefs, gw)


def gates_kernel(place, own_ref, other_ref, bias_ref, row_ref, col_ref, total_ref):
    count = own_ref.shape[1]
    pre = own_ref[...] + other_ref[...] + bias_ref[...]
    low_half = place[0] == 0
    in_pre = jnp.where(low_half, pre[0:2], pre[2:4])
    forget = jnp.where(low_half, pre[4:6], pre[6:8])
    both = jnp.concatenate([in_pre, forget, in_pre, forget], axis=0)
    in8 = jnp.concatenate([in_pre] * 4, axis=0)
    f8 = jnp.concatenate([forget] * 4, axis=0)
    log_keep = jnp.minimum(f8, 0.0) - jnp.log1p(jnp.exp(-jnp.abs(f8)))
    lane = lax.broadcasted_iota(jnp.int32, f8.shape, 1)
    place_in = lane % BLOCK
    cum = log_keep
    dist = 1
    while dist < BLOCK:
        cum = cum + jnp.where(place_in >= dist, pltpu.roll(cum, dist, 1), 0.0)
        dist *= 2
    last = jnp.where(place_in == BLOCK - 1, cum, 0.0)
    dist = 1
    while dist < BLOCK:
        last = last + jnp.where(place_in < BLOCK - dist, pltpu.roll(last, count - dist, 1), 0.0)
        dist *= 2
    before = jnp.where(lane >= BLOCK, pltpu.roll(last, BLOCK, 1), 0.0)
    after = jnp.where(lane < count - BLOCK, pltpu.roll(last, count - BLOCK, 1), 0.0)
    dist = BLOCK
    while dist < count:
        before = before + jnp.where(lane >= dist, pltpu.roll(before, dist, 1), 0.0)
        after = after + jnp.where(lane < count - dist, pltpu.roll(after, count - dist, 1), 0.0)
        dist *= 2
    scale = DH ** (-0.5)
    keep = jnp.exp(last - cum + in8) * scale
    table = jnp.concatenate(
        [
            cum[0:2], jnp.exp(cum[0:2]), keep[0:2], jnp.exp(after[0:2]),
            jnp.exp(before[0:2]), jnp.exp(last[0:2]), in8[0:2], 1.0 / (1.0 + jnp.exp(f8[0:2])),
        ],
        axis=0,
    )
    tall = jnp.concatenate([table, jnp.zeros((LANES - 16, count), f32)], axis=0)
    col_ref[...] = jnp.transpose(tall)
    small = jnp.concatenate([cum[0:2], in8[0:2], cum[0:2], in8[0:2]], axis=0)
    for b in range(count // BLOCK):
        row_ref[b] = small[:, b * BLOCK : (b + 1) * BLOCK]
    total = (before + last)[:, count - 1 : count]
    total_ref[...] = jnp.broadcast_to(total, total_ref.shape)


def gates_stage(place, own, other, bias):
    count = own.shape[1]
    return pl.pallas_call(
        gates_kernel,
        grid=(1,),
        in_specs=[smem, whole(8, count), whole(8, count), whole(8, 1)],
        out_specs=[whole(count // BLOCK, 8, BLOCK), whole(count, LANES), whole(8, DH)],
        out_shape=[shape_of(count // BLOCK, 8, BLOCK), shape_of(count, LANES), shape_of(8, DH)],
        compiler_params=params(24),
        cost_estimate=cost(count * 1000, count * 600),
        name="gates",
    )(place, own, other, bias)


def write_pack(ref, state, vector, log_decay):
    ref[0:DH, :] = state.astype(bf16)
    terms = split3(vector) + split3(log_decay)
    tail = jnp.concatenate(
        [t.astype(f32) for t in terms] + [jnp.zeros((PACK - DH - 6, DH), f32)], axis=0
    )
    ref[DH:PACK, :] = tail.astype(bf16)


def write_wide(ref, state, vector, log_decay):
    ref[0:DH, :] = state
    ref[DH:WIDE, :] = jnp.concatenate([vector, log_decay, jnp.zeros((WIDE - DH - 2, DH), f32)], axis=0)


def read_pack(ref):
    tail = ref[DH:PACK, :].astype(f32)
    return (
        ref[0:DH, :].astype(f32), (tail[0:1] + tail[1:2]) + tail[2:3], (tail[3:4] + tail[4:5]) + tail[5:6]
    )


def read_wide(ref):
    return ref[0:DH, :], ref[DH : DH + 1, :], ref[DH + 1 : DH + 2, :]


def joined(first, second):
    decay = jnp.exp(second[2])
    return decay * first[0] + second[0], decay * first[1] + second[1], first[2] + second[2]


def chosen(which, yes, no):
    return tuple(jnp.where(which, a, b) for a, b in zip(yes, no))


def pair_kernel(flag, own_ref, got_ref, send_ref, total_ref, lead_ref):
    own, got = read_wide(own_ref), read_pack(got_ref)
    is_lead = flag[0] == 1
    lead = chosen(is_lead, own, got)
    total = joined(lead, chosen(is_lead, got, own))
    write_wide(lead_ref, *lead)
    write_wide(total_ref, *total)
    write_pack(send_ref, *total)


def step_kernel(flag, total_ref, got_ref, before_ref, send_ref, new_total_ref, new_before_ref):
    total, got, before = read_wide(total_ref), read_pack(got_ref), read_wide(before_ref)
    upper = flag[0] == 1
    both = joined(chosen(upper, got, total), chosen(upper, total, got))
    write_wide(new_total_ref, *both)
    write_pack(send_ref, *both)
    write_wide(new_before_ref, *chosen(upper, joined(got, before), before))


def last_kernel(flag, got_ref, before_ref, lead_ref, send_ref, mine_ref):
    before, got = read_wide(before_ref), read_pack(got_ref)
    upper = flag[0] == 1
    is_lead = flag[1] == 1
    found = chosen(upper, joined(got, before), before)
    after = joined(found, read_wide(lead_ref))
    write_pack(send_ref, *chosen(is_lead, after, found))
    write_wide(mine_ref, *chosen(is_lead, found, after))


def pack_spec(wide):
    return whole(WIDE if wide else PACK, DH)


def pack_shape(wide):
    return shape_of(WIDE if wide else PACK, DH, dtype=f32 if wide else bf16)


def small_call(kernel, name, ins, outs, flag, *packs):
    return pl.pallas_call(
        kernel,
        grid=(1,),
        in_specs=[smem] + [pack_spec(w) for w in ins],
        out_specs=[pack_spec(w) for w in outs],
        out_shape=[pack_shape(w) for w in outs],
        compiler_params=params(24),
        cost_estimate=cost(PACK * DH * 8, PACK * DH * 3 * (len(ins) + len(outs))),
        name=name,
    )(flag, *packs)


def pass_states(own, send, place, span, stride):
    devices = lax.axis_size("dp")

    def swap(value, bit):
        route = [((i // stride ^ bit) * stride + i % stride, i) for i in range(devices)]
        return lax.ppermute(value, "dp", route)

    def as_flag(*values):
        return jnp.stack([jnp.asarray(v).astype(jnp.int32) for v in values])

    is_lead = place % 2 == 0
    got = swap(send, 1)
    out, total, lead = small_call(pair_kernel, "pair", (1, 0), (0, 1, 1), as_flag(is_lead), own, got)
    before = jnp.zeros_like(own)
    bit = 2
    while bit < span:
        got = swap(out, bit)
        upper = (place // bit) % 2 == 1
        if bit * 2 < span:
            out, total, before = small_call(
                step_kernel, "step", (1, 0, 1), (0, 1, 1), as_flag(upper), total, got, before
            )
        bit *= 2
    out, mine = small_call(last_kernel, "last", (0, 1, 1), (0, 1), as_flag(upper, is_lead), got, before, lead)
    return mine, swap(out, 1)


def put_states(flag, mine_ref, came_ref, state_ref, vec_ref):
    mine, came = read_wide(mine_ref), read_pack(came_ref)
    for h in range(2):
        found = chosen((flag[0] == 1) == (h == 0), mine, came)
        state_ref[h] = found[0]
        vec_ref[h : h + 1, :] = found[1]


def ends_kernel(flag, k_ref, v_ref, col_ref, total_ref, own_ref, send_ref, state_ref, vec_ref):
    step = pl.program_id(0)

    @pl.when(step == 0)
    def _():
        state_ref[...] = jnp.zeros_like(state_ref)
        vec_ref[...] = jnp.zeros_like(vec_ref)

    col = col_ref[...]
    for h in range(2):
        part = slice(h * DH, (h + 1) * DH)
        wide = k_ref[:, part].astype(f32)
        keep = col[:, 4 + h : 5 + h]
        later = col[:, 6 + h : 7 + h]
        kept = wide * keep
        high, low = split2(kept.astype(bf16).astype(f32) * later)
        value = v_ref[:, part]
        state_ref[h] += mm_tn(high, value) + mm_tn(low, value)
        vec_ref[h : h + 1, :] += jnp.sum(kept * later, axis=0, keepdims=True)

    @pl.when(step == pl.num_programs(0) - 1)
    def _():
        write_two(flag, state_ref, vec_ref, total_ref, own_ref, send_ref)


def write_two(flag, state_ref, vec_ref, total_ref, own_ref, send_ref):
    for h in range(2):
        found = (state_ref[h], vec_ref[h : h + 1, :], total_ref[h : h + 1, :])

        @pl.when(flag[0] == 1 - h)
        def _():
            write_wide(own_ref, *found)

        @pl.when(flag[0] == h)
        def _():
            write_pack(send_ref, *found)


def ends_stage(flag, k, v, col, total):
    count, chan = k.shape
    return pl.pallas_call(
        ends_kernel,
        grid=(count // TILE,),
        in_specs=[smem, rows(chan), rows(chan), rows(LANES), whole(8, DH)],
        out_specs=[pack_spec(1), pack_spec(0)],
        out_shape=[pack_shape(1), pack_shape(0)],
        scratch_shapes=[pltpu.VMEM((2, DH, DH), f32), pltpu.VMEM((8, DH), f32)],
        compiler_params=params(32),
        cost_estimate=cost(4 * count * chan * DH, count * chan * 4),
        name="ends",
    )(flag, k, v, col, total)


def damping_of(col, row, h):
    t = lax.broadcasted_iota(jnp.int32, (BLOCK, BLOCK), 0)
    s = lax.broadcasted_iota(jnp.int32, (BLOCK, BLOCK), 1)
    expo = col[:, h : h + 1] - row[h : h + 1, :] + row[2 + h : 3 + h, :]
    return jnp.exp(jnp.where(t >= s, expo, -1e30))


def lanes_of(*columns):
    lane = lax.broadcasted_iota(jnp.int32, (columns[0].shape[0], LANES), 1)
    out = jnp.zeros(lane.shape, f32)
    for i, column in enumerate(columns):
        out = jnp.where(lane == i, column, out)
    return out


def inside_kernel(q_ref, k_ref, v_ref, col_ref, row_ref, inside_ref, norm_ref):
    scale = DH ** (-0.5)

    def body(b, carry):
        r0 = pl.multiple_of(b * BLOCK, BLOCK)
        here = pl.ds(r0, BLOCK)
        col = col_ref[here, :]
        row = row_ref[b]
        sums = []
        for h in range(2):
            part = slice(h * DH, (h + 1) * DH)
            scores = mm_nt(q_ref[here, part], k_ref[here, part])
            weights = scores * damping_of(col, row, h) * scale
            inside_ref[here, part] = mm(weights.astype(bf16), v_ref[here, part])
            sums.append(jnp.sum(weights, axis=1, keepdims=True))
        norm_ref[here, :] = lanes_of(*sums)
        return carry

    lax.fori_loop(0, q_ref.shape[0] // BLOCK, body, 0)


def inside_stage(q, k, v, col, row):
    count, chan = q.shape
    return pl.pallas_call(
        inside_kernel,
        grid=(count // TILE,),
        in_specs=[rows(chan), rows(chan), rows(chan), rows(LANES),
                  pl.BlockSpec((TILE // BLOCK, 8, BLOCK), lambda i: (i, 0, 0))],
        out_specs=[rows(chan), rows(LANES)],
        out_shape=[shape_of(count, chan), shape_of(count, LANES)],
        compiler_params=params(32),
        cost_estimate=cost(4 * count * chan * BLOCK, count * chan * 10),
        name="inside",
    )(q, k, v, col, row)


def middle_kernel(
    flag, mine_ref, came_ref, q_ref, k_ref, v_ref, inside_ref, norm_ref, col_ref, gate_ref, dgated_ref,
    active_ref, group_ref, skip_ref, total_ref,
    gated_ref, gig_ref, sgrad_ref, nlow_ref, clow_ref, start_ref, nvec_ref, stat_ref, ggroup_ref, gskip_ref,
    own_ref, send_ref,
    state_ref, vec_ref, back_ref, bvec_ref,
):
    step = pl.program_id(0)

    @pl.when(step == 0)
    def _():
        put_states(flag, mine_ref, came_ref, state_ref, vec_ref)
        back_ref[...] = jnp.zeros_like(back_ref)
        bvec_ref[...] = jnp.zeros_like(bvec_ref)
        ggroup_ref[...] = jnp.zeros_like(ggroup_ref)
        gskip_ref[...] = jnp.zeros_like(gskip_ref)

    def body(b, carry):
        r0 = pl.multiple_of(b * BLOCK, BLOCK)
        here = pl.ds(r0, BLOCK)
        col = col_ref[here, :]
        norms = norm_ref[here, :]
        nvec_ref[b] = vec_ref[...]
        stats = []
        for h in range(2):
            part = slice(h * DH, (h + 1) * DH)
            query = q_ref[here, part]
            state = state_ref[h]
            state_low = state.astype(bf16)
            start_ref[h, b] = state_low
            growth = col[:, 2 + h : 3 + h]
            carried = growth * mm(query, state_low)
            vec = vec_ref[h : h + 1, :]
            norm_cross = growth * jnp.sum(query.astype(f32) * vec, axis=1, keepdims=True)
            numer = inside_ref[here, part] + carried
            normal = norms[:, h : h + 1] + norm_cross
            over = 1.0 / jnp.maximum(jnp.abs(normal), 1.0)
            mixed = numer * over
            centered = mixed - jnp.mean(mixed, axis=1, keepdims=True)
            inverse = lax.rsqrt(jnp.mean(centered * centered, axis=1, keepdims=True) + NORM_EPS)
            ghat = centered * inverse
            active = active_ref[here, part]
            gate = gate_ref[here, part]
            sig = sigmoid(gate)
            gact = gate * sig
            gweight = group_ref[0:1, part]
            gstate = ghat * gweight + skip_ref[0:1, part] * active
            gated_ref[here, part] = (gstate * gact).astype(bf16)
            dgated = dgated_ref[here, part]
            sgrad = dgated * gact
            sgrad_ref[here, part] = sgrad
            gig_ref[here, part] = (dgated * gstate * sig * (1.0 + gate * (1.0 - sig))).astype(bf16)
            gskip_ref[0:1, part] += jnp.sum(sgrad * active, axis=0, keepdims=True)
            ggroup_ref[0:1, part] += jnp.sum(sgrad * ghat, axis=0, keepdims=True)
            g = sgrad * gweight
            mgrad = inverse * (
                g - jnp.mean(g, axis=1, keepdims=True) - ghat * jnp.mean(g * ghat, axis=1, keepdims=True)
            )
            ngrad = mgrad * over
            down = -jnp.sum(mgrad * mixed, axis=1, keepdims=True) * over
            normal_grad = jnp.where(normal > 1.0, down, jnp.where(normal < -1.0, -down, 0.0))
            nlow_ref[here, part] = ngrad.astype(bf16)
            clow_ref[here, part] = (growth * ngrad).astype(bf16)
            moved = jnp.sum(ngrad * carried, axis=1, keepdims=True) + normal_grad * norm_cross
            stats.append((normal_grad, moved))
            wide = k_ref[here, part].astype(f32)
            kept = wide * col[:, 4 + h : 5 + h]
            decay = col[0:1, 10 + h : 11 + h]
            state_ref[h] = decay * state + mm_tn(kept.astype(bf16), v_ref[here, part])
            vec_ref[h : h + 1, :] = decay * vec + jnp.sum(kept, axis=0, keepdims=True)
            scaled = col[:, 8 + h : 9 + h] * growth * normal_grad
            bvec_ref[h : h + 1, :] += jnp.sum(scaled * query.astype(f32), axis=0, keepdims=True)
        stat_ref[here, :] = lanes_of(stats[0][0], stats[1][0], stats[0][1], stats[1][1])
        return carry

    lax.fori_loop(0, q_ref.shape[0] // BLOCK, body, 0)
    for h in range(2):
        part = slice(h * DH, (h + 1) * DH)
        high, low = split2(clow_ref[:, part].astype(f32) * col_ref[:, 8 + h : 9 + h])
        query = q_ref[:, part]
        back_ref[h] += mm_tn(query, high) + mm_tn(query, low)

    @pl.when(step == pl.num_programs(0) - 1)
    def _():
        write_two(flag, back_ref, bvec_ref, total_ref, own_ref, send_ref)


def middle_stage(flag, mine, came, q, k, v, inside, norms, col, gate, dgated, active, group, skip, total):
    count, chan = q.shape
    blocks = count // BLOCK
    per = TILE // BLOCK
    return pl.pallas_call(
        middle_kernel,
        grid=(count // TILE,),
        in_specs=[smem, pack_spec(1), pack_spec(0), rows(chan), rows(chan), rows(chan), rows(chan), rows(LANES), rows(LANES),
                  rows(chan), rows(chan), rows(chan), whole(1, chan), whole(1, chan), whole(8, DH)],
        out_specs=[rows(chan), rows(chan), rows(chan), rows(chan), rows(chan),
                   pl.BlockSpec((2, per, DH, DH), lambda i: (0, i, 0, 0)),
                   pl.BlockSpec((per, 8, DH), lambda i: (i, 0, 0)),
                   rows(LANES), whole(8, chan), whole(8, chan), pack_spec(1), pack_spec(0)],
        out_shape=[shape_of(count, chan, dtype=bf16), shape_of(count, chan, dtype=bf16), shape_of(count, chan),
                   shape_of(count, chan, dtype=bf16), shape_of(count, chan, dtype=bf16),
                   shape_of(2, blocks, DH, DH, dtype=bf16), shape_of(blocks, 8, DH), shape_of(count, LANES),
                   shape_of(8, chan), shape_of(8, chan),
                   pack_shape(1), pack_shape(0)],
        scratch_shapes=[pltpu.VMEM((2, DH, DH), f32), pltpu.VMEM((8, DH), f32),
                        pltpu.VMEM((2, DH, DH), f32), pltpu.VMEM((8, DH), f32)],
        compiler_params=params(56),
        cost_estimate=cost(10 * count * chan * DH, count * chan * 40),
        name="middle",
    )(flag, mine, came, q, k, v, inside, norms, col, gate, dgated, active, group, skip, total)


def back_kernel(
    flag, mine_ref, came_ref, q_ref, k_ref, v_ref, nlow_ref, clow_ref, start_ref, nvec_ref, col_ref, row_ref,
    stat_ref,
    qg_ref, kg_ref, vg_ref, pre_ref,
    state_ref, vec_ref,
):
    scale = DH ** (-0.5)

    @pl.when(pl.program_id(0) == 0)
    def _():
        put_states(flag, mine_ref, came_ref, state_ref, vec_ref)

    u = lax.broadcasted_iota(jnp.int32, (BLOCK, BLOCK), 0)
    t = lax.broadcasted_iota(jnp.int32, (BLOCK, BLOCK), 1)
    from_here = jnp.where(t >= u, 1.0, 0.0)
    at_end = lax.broadcasted_iota(jnp.int32, (BLOCK, 1), 0) == BLOCK - 1
    per = q_ref.shape[0] // BLOCK

    def body(i, carry):
        b = per - 1 - i
        r0 = pl.multiple_of(b * BLOCK, BLOCK)
        here = pl.ds(r0, BLOCK)
        col = col_ref[here, :]
        row = row_ref[b]
        stat = stat_ref[here, :]
        starts = nvec_ref[b]
        in_cols, cum_cols = [], []
        for h in range(2):
            part = slice(h * DH, (h + 1) * DH)
            query, key, value = q_ref[here, part], k_ref[here, part], v_ref[here, part]
            numer_low, cross_low = nlow_ref[here, part], clow_ref[here, part]
            growth = col[:, 2 + h : 3 + h]
            keep = col[:, 4 + h : 5 + h]
            decay = col[0:1, 10 + h : 11 + h]
            normal_grad = stat[:, h : h + 1]
            moved = stat[:, 2 + h : 3 + h]
            end = state_ref[h]
            end_low = end.astype(bf16)
            end_vec = vec_ref[h : h + 1, :]
            start_low = start_ref[h, b]
            start_vec = starts[h : h + 1, :]
            damping = damping_of(col, row, h)
            scores = mm_nt(query, key)
            weights_low = (scores * damping * scale).astype(bf16)
            weights_grad = mm_nt(numer_low, value) + normal_grad
            damped = weights_grad * scale * damping
            scores_low = damped.astype(bf16)
            expo = damped * scores
            pull = growth * normal_grad
            qg_ref[here, part] = mm(scores_low, key) + mm_nt(cross_low, start_low) + pull * start_vec
            wide = key.astype(f32)
            kept_low = (wide * keep).astype(bf16)
            key_total = mm_nt(value, end_low) + end_vec
            kg_ref[here, part] = mm_tn(scores_low, query) + keep * key_total
            vg_ref[here, part] = mm_tn(weights_low, numer_low) + mm(kept_low, end_low)
            keep_grad = keep * jnp.sum(wide * key_total, axis=1, keepdims=True)
            held = jnp.sum(end * start_low.astype(f32), axis=0, keepdims=True) + end_vec * start_vec
            last_grad = decay * jnp.sum(held, axis=1, keepdims=True) + jnp.sum(keep_grad, axis=0, keepdims=True)
            over_t = jnp.sum(jnp.transpose(expo), axis=1, keepdims=True)
            cum_grad = jnp.sum(expo, axis=1, keepdims=True) - over_t + moved - keep_grad
            cum_cols.append(cum_grad + jnp.where(at_end, last_grad, 0.0))
            in_cols.append(over_t + keep_grad)
            state_ref[h] = decay * end + mm_tn(query, cross_low)
            vec_ref[h : h + 1, :] = decay * end_vec + jnp.sum(pull * query.astype(f32), axis=0, keepdims=True)
        sums = lax.dot_general(
            from_here, lanes_of(*cum_cols), (((1,), (0,)), ((), ())), precision=highest, preferred_element_type=f32
        )
        forget = [sums[:, h : h + 1] * col[:, 14 + h : 15 + h] for h in range(2)]
        pre_ref[here, :] = lanes_of(*in_cols, *forget).astype(bf16)
        return carry

    lax.fori_loop(0, per, body, 0)


def back_stage(flag, mine, came, q, k, v, nlow, clow, start, nvec, col, row, stat):
    count, chan = q.shape
    tiles = count // TILE
    per = TILE // BLOCK
    flip = rows(chan, flip=tiles)
    thin = rows(LANES, flip=tiles)
    return pl.pallas_call(
        back_kernel,
        grid=(tiles,),
        in_specs=[smem, pack_spec(1), pack_spec(0), flip, flip, flip, flip, flip,
                  pl.BlockSpec((2, per, DH, DH), lambda i: (0, tiles - 1 - i, 0, 0)),
                  pl.BlockSpec((per, 8, DH), lambda i: (tiles - 1 - i, 0, 0)), thin,
                  pl.BlockSpec((per, 8, BLOCK), lambda i: (tiles - 1 - i, 0, 0)), thin],
        out_specs=[flip, flip, flip, thin],
        out_shape=[shape_of(count, chan)] * 3 + [shape_of(count, LANES, dtype=bf16)],
        scratch_shapes=[pltpu.VMEM((2, DH, DH), f32), pltpu.VMEM((8, DH), f32)],
        compiler_params=params(56),
        cost_estimate=cost(14 * count * chan * DH, count * chan * 30),
        name="back",
    )(flag, mine, came, q, k, v, nlow, clow, start, nvec, col, row, stat)


def band_back(value, map_hi, map_lo):
    high, low = value
    found = []
    for g in range(high.shape[1] // GROUP):
        part = slice(g * GROUP, (g + 1) * GROUP)
        found.append(
            mm_nt(high[:, part], map_hi[g])
            + (mm_nt(low[:, part], map_hi[g]) + mm_nt(high[:, part], map_lo[g]))
        )
    return jnp.concatenate(found, axis=1)


def conv_grad_of(active_grad, conv):
    sig = sigmoid(conv)
    return active_grad * sig * (1.0 + conv * (1.0 - sig))


def edge_kernel(qg_ref, kg_ref, pre_ref, sgrad_ref, conv_ref, skip_ref, coef_ref, gwt_ref, out_ref):
    pre = pre_ref[...]
    query_all = qg_ref[...] + mm(pre, gwt_ref[0])
    key_all = kg_ref[...] + mm(pre, gwt_ref[1])
    reach = QB - 1
    for g in range(query_all.shape[1] // LANES):
        part = slice(g * LANES, (g + 1) * LANES)
        total = sgrad_ref[:, part] * skip_ref[:, part]
        for m, value in enumerate((query_all[:, part], key_all[:, part])):
            for offset in range(-reach, reach + 1):
                total = total + pltpu.roll(
                    coef_ref[m, reach - offset : reach - offset + 1, part] * value, -offset % LANES, 1
                )
        out_ref[:, part] = conv_grad_of(total, conv_ref[:, part])[0:8, :]


def edge_stage(qg, kg, pre8, sgrad, conv, skip, coefs, gwt):
    chan = qg.shape[1]
    top = rows(chan, HALO)
    return pl.pallas_call(
        edge_kernel,
        grid=(1,),
        in_specs=[top, top, rows(LANES, HALO), top, top, whole(*skip.shape), whole(*coefs.shape),
                  whole(*gwt.shape)],
        out_specs=whole(8, chan),
        out_shape=shape_of(8, chan),
        compiler_params=params(16),
        cost_estimate=cost(10**7, 10**6),
        name="edge",
    )(qg, kg, pre8, sgrad, conv, skip, coefs, gwt)


def maps_kernel(
    flag, qg_ref, kg_ref, vg_ref, pre_ref, sgrad_ref, conv_ref, inner_ref, q_ref, k_ref, v_ref, edge_ref,
    skip_ref, cw_ref, coef_ref, gwt_ref,
    low_ref, small_ref,
    pad_ref, hi_ref, lo_ref, gmap_ref,
):
    tile, chan = qg_ref.shape
    groups = chan // GROUP
    reach = QB - 1

    @pl.when(pl.program_id(0) == 0)
    def _():
        pad_ref[tile : tile + 8, :] = jnp.where(flag[0] == 1, 0.0, edge_ref[...])
        gmap_ref[...] = jnp.zeros_like(gmap_ref)
        small_ref[...] = jnp.zeros_like(small_ref)
        apart = lax.broadcasted_iota(jnp.int32, (GROUP, GROUP), 0) - lax.broadcasted_iota(
            jnp.int32, (GROUP, GROUP), 1
        )
        for m in range(3):
            for g in range(groups):
                dense = jnp.zeros((GROUP, GROUP), f32)
                for offset in range(-reach, reach + 1):
                    coef = coef_ref[m, reach + offset : reach + offset + 1, g * GROUP : (g + 1) * GROUP]
                    dense = jnp.where(apart == offset, coef, dense)
                hi_ref[m, g], lo_ref[m, g] = split2(dense)

    pre = pre_ref[...]
    conv = conv_ref[...]
    inner = inner_ref[...]
    query_all = split2(qg_ref[...] + mm(pre, gwt_ref[0]))
    key_all = split2(kg_ref[...] + mm(pre, gwt_ref[1]))
    value_all = split2(vg_ref[...] + mm(pre, gwt_ref[2]))
    active = split2(conv * sigmoid(conv))
    inner2 = split2(inner)
    for m, (grads, acts) in enumerate(((query_all, active), (key_all, active), (value_all, inner2))):
        for g in range(groups):
            part = slice(g * GROUP, (g + 1) * GROUP)
            gmap_ref[m, g] += mm_tn(grads[0][:, part], acts[0][:, part]) + (
                mm_tn(grads[1][:, part], acts[0][:, part]) + mm_tn(grads[0][:, part], acts[1][:, part])
            )
    active_grad = (
        sgrad_ref[...] * skip_ref[...]
        + band_back(query_all, hi_ref[0], lo_ref[0])
        + band_back(key_all, hi_ref[1], lo_ref[1])
    )
    grad = conv_grad_of(active_grad, conv)
    pad_ref[0:tile, :] = grad
    taps = cw_ref.shape[0]
    small_ref[taps : taps + 1, :] += jnp.sum(grad, axis=0, keepdims=True)
    inner_grad = band_back(value_all, hi_ref[2], lo_ref[2])
    for j in range(cw_ref.shape[0]):
        moved = pad_ref[j : j + tile, :]
        inner_grad = inner_grad + cw_ref[j : j + 1, :] * moved
        small_ref[j : j + 1, :] += jnp.sum(moved * inner, axis=0, keepdims=True)
    low_ref[...] = inner_grad.astype(bf16)
    pad_ref[tile : tile + 8, :] = pad_ref[0:8, :]
    for m, ref in enumerate((q_ref, k_ref, v_ref)):
        small_ref[8 * (m + 1) : 8 * (m + 2), :] += mm_tn(pre, ref[...])[0:8, :]
    small_ref[taps + 1 : taps + 2, 0:LANES] += jnp.sum(pre.astype(f32), axis=0, keepdims=True)

    @pl.when(pl.program_id(0) == pl.num_programs(0) - 1)
    def _():
        r = lax.broadcasted_iota(jnp.int32, (GROUP, GROUP), 0)
        c = lax.broadcasted_iota(jnp.int32, (GROUP, GROUP), 1)
        pick = jnp.where(
            lax.broadcasted_iota(jnp.int32, (8, GROUP), 1) % QB == lax.broadcasted_iota(jnp.int32, (8, GROUP), 0),
            1.0, 0.0,
        )
        for m in range(3):
            for g in range(groups):
                held = jnp.where(r // QB == c // QB, gmap_ref[m, g], 0.0)
                small_ref[8 * (m + 4) : 8 * (m + 5), g * GROUP : (g + 1) * GROUP] = lax.dot_general(
                    pick, held, (((1,), (1,)), ((), ())), precision=highest, preferred_element_type=f32
                )


def maps_stage(flag, qg, kg, vg, pre8, sgrad, conv, inner, q, k, v, edge, skip, cw, coefs, gwt):
    count, chan = qg.shape
    tiles = count // TILE
    flip = rows(chan, flip=tiles)
    groups = chan // GROUP
    return pl.pallas_call(
        maps_kernel,
        grid=(tiles,),
        in_specs=[smem, flip, flip, flip, rows(LANES, flip=tiles), flip, flip, flip, flip, flip, flip,
                  whole(8, chan), whole(*skip.shape), whole(*cw.shape), whole(*coefs.shape), whole(*gwt.shape)],
        out_specs=[flip, whole(SMALL, chan)],
        out_shape=[shape_of(count, chan, dtype=bf16), shape_of(SMALL, chan)],
        scratch_shapes=[pltpu.VMEM((TILE + 8, chan), f32), pltpu.VMEM((3, groups, GROUP, GROUP), bf16),
                        pltpu.VMEM((3, groups, GROUP, GROUP), bf16), pltpu.VMEM((3, groups, GROUP, GROUP), f32)],
        compiler_params=params(60),
        cost_estimate=cost(20 * count * chan * GROUP, count * chan * 32),
        name="maps",
    )(flag, qg, kg, vg, pre8, sgrad, conv, inner, q, k, v, edge, skip, cw, coefs, gwt)


def exchanged(value, bit):
    route = [(i ^ bit, i) for i in range(lax.axis_size("dp"))]
    return lax.ppermute(value, "dp", route)


def summed(value, bits):
    place = lax.axis_index("dp")
    width = value.shape[1]
    for bit in bits:
        mine = (place // bit) % 2
        size = value.shape[0] // 2
        send = lax.dynamic_slice(value, ((1 - mine) * size, 0), (size, width)).astype(bf16)
        keep = lax.dynamic_slice(value, (mine * size, 0), (size, width))
        value = keep + exchanged(send, bit).astype(f32)
    value = value.astype(bf16)
    for bit in reversed(bits):
        first = (place // bit) % 2 == 0
        other = exchanged(value, bit)
        value = jnp.concatenate([jnp.where(first, value, other), jnp.where(first, other, value)], axis=0)
    return value


def all_sum(value, bits):
    for bit in bits:
        value = value + exchanged(value, bit)
    return value


def band_rows(weight):
    size = weight.shape[1]
    found = []
    for offset in range(1 - size, size):
        pieces = [
            weight[:, o, o + offset] if 0 <= o + offset < size else jnp.zeros_like(weight[:, 0, 0])
            for o in range(size)
        ]
        found.append(jnp.stack(pieces, axis=1).reshape(-1))
    return jnp.stack(found + [jnp.zeros_like(found[0])])


def on_device(
    tokens, cotangent, ln_weight, up_inner, up_gate, conv_weight, conv_bias, query_weight, key_weight,
    value_weight, gate_weight, gate_bias, group_weight, skip_weight, down_weight,
):
    count = tokens.shape[0]
    chan = up_inner.shape[1]
    model = up_inner.shape[0]
    half = tokens.shape[1]
    band = query_weight.shape[1]
    span = SEQ_LEN // count
    devices = lax.axis_size("dp")
    stride = devices // span
    t_place = lax.axis_index("tensor")
    piece = lax.axis_index("dp") // stride
    low_half = t_place == 0

    def across(value):
        return lax.ppermute(value, "tensor", [(0, 1), (1, 0)])

    def side_by_side(own):
        other = across(own)
        return jnp.concatenate([jnp.where(low_half, own, other), jnp.where(low_half, other, own)], axis=1)

    def along(value, distance):
        route = [(i - distance, i) for i in range(devices) if 0 <= i - distance < devices]
        return lax.ppermute(value, "dp", route)

    def flag_of(value):
        return jnp.asarray(value).astype(jnp.int32)[None]

    halo = side_by_side(along(tokens[count - HALO :], stride))
    full = side_by_side(tokens)
    full_cot = side_by_side(cotangent)

    coefs = jnp.stack([band_rows(w) for w in (query_weight, key_weight, value_weight)])
    gw = jnp.pad(gate_weight, ((0, 0), (0, 0), (0, LANES - gate_weight.shape[2])))
    gwt = jnp.swapaxes(gw, 1, 2)

    normed, inner, conv, active, q, k, v, pre = first_stage(
        flag_of(piece == 0), full, halo, ln_weight[None], up_inner, conv_weight, conv_bias[None],
        coefs, gw,
    )
    row, col, total = gates_stage(flag_of(t_place), pre, across(pre), gate_bias[:, None])
    even = flag_of(piece % 2 == 0)
    own, send = ends_stage(even, k, v, col, total)
    mine, came = pass_states(own, send, piece, span, stride)
    gate_in = mm(normed, up_gate)
    dgated = mm_nt(full_cot, down_weight)
    inside, norms = inside_stage(q, k, v, col, row)
    (
        gated, gate_in_grad, sgrad, nlow, clow, start, nvec, stat, ggroup, gskip, own, send
    ) = middle_stage(
        even, mine, came, q, k, v, inside, norms, col, gate_in, dgated, active, group_weight[None],
        skip_weight[None], total,
    )
    mine, came = pass_states(own, send, span - 1 - piece, span, stride)

    bits = [1 << n for n in range(devices.bit_length() - 1)]
    early = summed(jnp.concatenate([mm_tn(gated, full_cot), mm_tn(normed, gate_in_grad)], axis=0), bits)
    branch = mm(gated, down_weight)
    keep_half = lax.dynamic_slice_in_dim(branch, t_place * half, half, axis=1)
    send_half = lax.dynamic_slice_in_dim(branch, (1 - t_place) * half, half, axis=1)
    result = tokens.astype(f32) + (keep_half + across(send_half))
    squares = jnp.sum(result * result)
    gate_part = mm_nt(gate_in_grad, up_gate)

    qg, kg, vg, pre_own = back_stage(even, mine, came, q, k, v, nlow, clow, start, nvec, col, row, stat)
    pre_other = across(pre_own)
    heads = gate_bias.shape[0] // 2
    local = heads // 2
    a = jnp.where(low_half, pre_own, pre_other)
    c = jnp.where(low_half, pre_other, pre_own)
    pre8 = jnp.concatenate(
        [a[:, 0:local], c[:, 0:local], a[:, local : 2 * local], c[:, local : 2 * local],
         jnp.zeros((count, LANES - 2 * heads), bf16)], axis=1,
    )
    skip = skip_weight[None]
    edge = along(edge_stage(qg, kg, pre8, sgrad, conv, skip, coefs, gwt), -stride)
    inner_low, small = maps_stage(
        flag_of(piece == span - 1), qg, kg, vg, pre8, sgrad, conv, inner, q, k, v, edge, skip, conv_weight,
        coefs, gwt,
    )
    grad_up_inner = mm_tn(normed, inner_low)
    other_bits = [bits[1], bits[0]] + bits[2:]
    late = jnp.concatenate(
        [summed(grad_up_inner[: model // 2], bits), summed(grad_up_inner[model // 2 :], other_bits)], axis=0
    )
    ones = jnp.pad((squares + across(squares))[None, None], ((0, 7), (0, chan - 1)))
    small = all_sum(jnp.concatenate([small, ggroup, gskip, ones], axis=0), bits)

    part = gate_part + mm_nt(inner_low, up_inner)
    wide = full.astype(f32)
    centered = wide - jnp.mean(wide, axis=1, keepdims=True)
    inverse = lax.rsqrt(jnp.mean(centered * centered, axis=1, keepdims=True) + NORM_EPS)
    xhat = centered * inverse
    scaled = part * ln_weight
    mean_h = jnp.mean(scaled, axis=1)
    mean_hx = jnp.mean(scaled * xhat, axis=1)
    means = jnp.stack([mean_h, mean_hx])
    means = means + across(means)
    own_part = lax.dynamic_slice_in_dim(part, t_place * half, half, axis=1)
    send_part = lax.dynamic_slice_in_dim(part, (1 - t_place) * half, half, axis=1)
    normed_grad = own_part + across(send_part)
    xhat_own = lax.dynamic_slice_in_dim(xhat, t_place * half, half, axis=1)
    ln_own = lax.dynamic_slice_in_dim(ln_weight, t_place * half, half, axis=0)
    token_grad = (
        inverse * (normed_grad * ln_own - means[0][:, None] - xhat_own * means[1][:, None])
        + cotangent.astype(f32)
    )
    grad_ln = jnp.sum(normed_grad * xhat_own, axis=0)

    grad_ln = all_sum(jnp.broadcast_to(grad_ln[None], (8, half)), bits)[0]
    taps = conv_weight.shape[0]
    folded = small[32:56].reshape(3, 8, chan)[:, :band].reshape(3, band, chan // band, band)
    folded = jnp.transpose(folded, (0, 2, 3, 1))
    gate_rows = jnp.swapaxes(small[8:32].reshape(3, 8, chan), 1, 2)
    rms = jnp.sqrt(small[72, 0:1] / (count * model * devices))
    return (
        result.astype(bf16), token_grad, grad_ln, late.astype(f32), early[model:].astype(f32), small[:taps],
        small[taps], folded[0], folded[1], folded[2], gate_rows, small[taps + 1, : 2 * heads], small[56],
        small[64], early[:model].astype(f32), rms,
    )


def solution(mesh):
    rows_spec = P("dp", "tensor")
    cols = P(None, "tensor")
    vec = P("tensor")
    blocks = P("tensor", None, None)
    gates = P(None, "tensor", None)
    in_specs = (
        rows_spec, rows_spec, P(), cols, cols, cols, vec, blocks, blocks, blocks, gates, P(), vec, vec,
        P("tensor", None),
    )
    out_specs = (
        rows_spec, rows_spec, vec, cols, cols, cols, vec, blocks, blocks, blocks, gates, P(), vec, vec,
        P("tensor", None), P(),
    )
    return jax.shard_map(on_device, mesh=mesh, in_specs=in_specs, out_specs=out_specs, check_vma=False)
```

time: 2490 us -> 575 us (0.23)
  waiting for transfers between devices: 1020 us -> 188 us
  other arithmetic: 614 us -> 41.5 us
  local copies, waits for them, and re-layouts: 477 us -> 69.6 us
  matrix products: 236 us -> 29.6 us
  Pallas kernels: 0 us -> 155 us
  blocking collectives: 47 us -> 0 us
    psum x3 -> x0, waiting for transfers between devices: 425 us -> none  [the longest x2 425 us: on_device(): lax.psum((grad_ln, grad_up_inner, grad_up_gate, grad_conv_weight, grad_co...]
    ppermute x16 -> x51, waiting for transfers between devices: 591 us -> 188 us  [the longest x32 96.5 us: exchanged(): return lax.ppermute(value, 'dp', route)]
    add x146 -> x18, other arithmetic: 401 us -> 8.53 us  [the longest x9 7.76 us: summed(): value = keep + exchanged(send, bit).astype(f32)]
    dot_general x48 -> x8, matrix products: 236 us -> 29.6 us  [the longest x3 11.6 us: mm_nt(): lax.dot_general(left, right, (((1,), (1,)), ((), ())), preferred_element_...]
    pallas_call x0 -> x14, Pallas kernels: none -> 155 us  [the longest x1 40.1 us: back_stage(): pl.pallas_call(back_kernel, grid=(tiles,), in_specs=[smem, pack_spec(1),...]
    slice x113 -> x9, local copies, waits for them, and re-layouts: 101 us -> 6.85 us  [the longest x1 1.4 us: on_device(): small[64]]
    reduce_sum x19 -> x4, other arithmetic: 96 us -> 8.29 us  [the longest x1 3.84 us: on_device(): squares = jnp.sum(result * result)]
    another operation x127 -> x52, local copies, waits for them, and re-layouts: 92.6 us -> 8.56 us  [the longest x24 5.56 us: band_rows(): found.append(jnp.stack(pieces, axis=1).reshape(-1))]
  transfers between devices with their start and end apart: 22 -> 51, of which waited for: 17 -> 22; matrix products, arithmetic and copies ran while one was open for 25% -> 17% of each run, Pallas kernels for 0% -> 20%
where the time goes in v1:
time: 575 us; the launch traced here: 566 us
  waiting for transfers between devices  188 us (33%)
  Pallas kernels  155 us (27%)
  starting transfers between devices  75.8 us (13%)
  local copies, waits for them, and re-layouts  69.6 us (12%)
  other arithmetic  41.5 us (7%)
  matrix products  29.6 us (5%)
  between operations  5.87 us (1%)
    ppermute x32, waiting for transfers between devices, exchanged(): return lax.ppermute(value, 'dp', route)  96.5 us
    ppermute x8, waiting for transfers between devices, swap(): return lax.ppermute(value, 'dp', route)  90.3 us
    ppermute x32, starting transfers between devices, exchanged(): return lax.ppermute(value, 'dp', route)  58.2 us
    pallas_call x1, Pallas kernels, back_stage(): pl.pallas_call(back_kernel, grid=(tiles,), in_specs=[smem, pack_spec(1),...  40.1 us
    pallas_call x1, Pallas kernels, middle_stage(): pl.pallas_call(middle_kernel, grid=(count // TILE,), in_specs=[smem, pack...  40 us
    unnamed x182, local copies, waits for them, and re-layouts  38.6 us
    pallas_call x1, Pallas kernels, maps_stage(): pl.pallas_call(maps_kernel, grid=(tiles,), in_specs=[smem, flip, flip, fl...  29.9 us
    pallas_call x1, Pallas kernels, first_stage(): pl.pallas_call(first_kernel, grid=(count // TILE,), in_specs=[smem, rows(...  23.9 us
  transfers between devices with their start and end apart: 51, of which 22 were waited for; matrix products, arithmetic and copies ran while one was open for 17% of the time, Pallas kernels for 20%

profile of v1, /device:TPU:0, one launch (start us, length us, event | category | flops | bytes accessed | tf_op | source)
XLA Modules:
  0.0 565.7 jit_solution(3739372692923658811)
XLA Ops:
  2.0 4.5 collective-permute-start.1
  21.9 23.9 %first.1 = (bf16[1024,1024]{1,0:T(8,128)(2,1)S(1)}, f32[1024,1024]{1,0:T(8,128)}, f32[1024,1024]{1,0:T(8,128)}, f32[1024,1024]{1,0:T(8,128)}, bf16[1024,1024]{1,...) custom-call(s32[1]{0:T(128)} %bitcast.3.flag, ...), custom_call_target="tpu_custom_call" | custom-call | flops 8589934592 | bytes 20971520 | tf_op jit(solution)/shard_map/first/pallas_call | solution.py:136
  54.5 4.6 ends.1
  60.7 12.8 %collective-permute-done.4.got_ref = bf16[528,512]{1,0:T(8,128)(2,1)S(1)} collective-permute-done((bf16[528,512]{1,0:T(8,128)(2,1)S(1)}, bf16[528,512]{1,0:T(8,128)(2,1)S(1)}, u32[]{:S(2)}, u32[]{:S(2)}) %collective-permute-start.4) | collective-permute-done | bytes 540704 | tf_op jit(solution)/shard_map/ppermute | solution.py:305
  80.1 10.2 %collective-permute-done.5.got_ref = bf16[528,512]{1,0:T(8,128)(2,1)S(1)} collective-permute-done((bf16[528,512]{1,0:T(8,128)(2,1)}, bf16[528,512]{1,0:T(8,128)(2,1)S(1)}, u32[]{:S(2)}, u32[]{:S(2)}) %collective-permute-start.5) | collective-permute-done | bytes 540704 | tf_op jit(solution)/shard_map/ppermute | solution.py:305
  93.6 2.6 collective-permute-start.6
  96.2 4.4 fusion.30.gate_ref
  100.6 18.0 %collective-permute-done.6.got_ref = bf16[528,512]{1,0:T(8,128)(2,1)S(1)} collective-permute-done((bf16[528,512]{1,0:T(8,128)(2,1)S(1)}, bf16[528,512]{1,0:T(8,128)(2,1)S(1)}, u32[]{:S(2)}, u32[]{:S(2)}) %collective-permute-start.6) | collective-permute-done | bytes 540704 | tf_op jit(solution)/shard_map/ppermute | solution.py:305
  121.2 4.3 fusion.8.dgated_ref
  125.6 7.6 %inside.1 = (f32[1024,1024]{1,0:T(8,128)S(1)}, f32[1024,128]{1,0:T(8,128)S(1)}) custom-call(bf16[1024,1024]{1,0:T(8,128)(2,1)S(1)} %copy-done.2, bf16[1024,1024]{1,0:T(8,128)(2,1)S(1)} %copy-done.4, bf16[1024,1024]{1,0:T(8,128)(2,1)S(1)} %copy-done.6, f32[1024,128]{1,0:T(8,128)S(1)} %copy-done.13, f32[16,8,64]{2,1,0:T(8,128)S(1)} %get-tuple-element.78.row_ref), custom_call_target="tpu_custom_call" | custom-call | flops 268435456 | bytes 10485760 | tf_op jit(solution)/shard_map/inside/pallas_call | solution.py:426
  136.9 40.0 %middle.1 = (bf16[1024,1024]{1,0:T(8,128)(2,1)}, bf16[1024,1024]{1,0:T(8,128)(2,1)}, f32[1024,1024]{1,0:T(8,128)}, bf16[1024,1024]{1,0:T(8,128)(2,1)}, bf16[1024...) custom-call(s32[1]{0:T(128)} %bitcast.flag, ...), custom_call_target="tpu_custom_call" | custom-call | flops 5368709120 | bytes 41943040 | tf_op jit(solution)/shard_map/middle/pallas_call | solution.py:530
  176.9 3.9 fusion.31
  184.5 2.5 fusion.34
  187.0 11.5 %collective-permute-done.10.got_ref = bf16[528,512]{1,0:T(8,128)(2,1)S(1)} collective-permute-done((bf16[528,512]{1,0:T(8,128)(2,1)S(1)}, bf16[528,512]{1,0:T(8,128)(2,1)S(1)}, u32[]{:S(2)}, u32[]{:S(2)}) %collective-permute-start.10) | collective-permute-done | bytes 540704 | tf_op jit(solution)/shard_map/ppermute | solution.py:305
  201.8 2.4 fusion.7
  204.3 3.1 fusion.4
  210.0 5.8 %collective-permute-done.11.got_ref = bf16[528,512]{1,0:T(8,128)(2,1)} collective-permute-done((bf16[528,512]{1,0:T(8,128)(2,1)}, bf16[528,512]{1,0:T(8,128)(2,1)}, u32[]{:S(2)}, u32[]{:S(2)}) %collective-permute-start.11) | collective-permute-done | bytes 540704 | tf_op jit(solution)/shard_map/ppermute | solution.py:305
  217.0 2.5 step.3
  222.4 22.6 %collective-permute-done.12.got_ref = bf16[528,512]{1,0:T(8,128)(2,1)S(1)} collective-permute-done((bf16[528,512]{1,0:T(8,128)(2,1)S(1)}, bf16[528,512]{1,0:T(8,128)(2,1)S(1)}, u32[]{:S(2)}, u32[]{:S(2)}) %collective-permute-start.12) | collective-permute-done | bytes 540704 | tf_op jit(solution)/shard_map/ppermute | solution.py:305
  246.6 3.8 multiply_reduce_fusion.2
  250.4 9.3 %collective-permute-done.13.came_ref = bf16[528,512]{1,0:T(8,128)(2,1)S(1)} collective-permute-done((bf16[528,512]{1,0:T(8,128)(2,1)S(1)}, bf16[528,512]{1,0:T(8,128)(2,1)S(1)}, u32[]{:S(2)}, u32[]{:S(2)}) %collective-permute-start.13) | collective-permute-done | bytes 540704 | tf_op jit(solution)/shard_map/ppermute | solution.py:305
  260.5 40.1 %back.1 = (f32[1024,1024]{1,0:T(8,128)}, f32[1024,1024]{1,0:T(8,128)}, f32[1024,1024]{1,0:T(8,128)}, bf16[1024,128]{1,0:T(8,128)(2,1)}) custom-call(s32[1]{0:T(128)} %bitcast.flag, f32[520,512]{1,0:T(8,128)} %copy-done.16, bf16[528,512]{1,0:T(8,128)(2,1)} %copy-done.74, bf16[1024,1024]{1,0:T(8,128)(2,1)} %copy-done.1, ...), custom_call_target="tpu_custom_call" | custom-call | flops 7516192768 | bytes 31457280 | tf_op jit(solution)/shard_map/back/pallas_call | solution.py:632
  300.7 5.5 fusion.6
  322.0 2.7 collective-permute-start.39
  326.6 29.9 %maps.1 = (bf16[1024,1024]{1,0:T(8,128)(2,1)}, f32[56,1024]{1,0:T(8,128)}) custom-call(s32[1]{0:T(128)} %bitcast.61.flag, f32[1024,1024]{1,0:T(8,128)} %get-tuple-element.99.qg_ref, f32[1024,1024]{1,0:T(8,128)} %get-tuple-element.100.kg_ref, f32[1024,1024]{1,0:T(8,128)} %get-tuple-element.101.vg_ref, bf16[1024,128]{1,0:T(8,128)(2,1)} %copy-done.15, ...), custom_call_target="tpu_custom_call" | custom-call | flops 5368709120 | bytes 33554432 | tf_op jit(solution)/shard_map/maps/pallas_call | solution.py:778
  356.5 4.8 fusion.33
  363.8 2.7 collective-permute-start.47
  368.7 4.9 multiply_reduce_fusion.1
  376.9 8.6 %collective-permute-done.22 = bf16[256,1024]{1,0:T(8,128)(2,1)S(1)} collective-permute-done((bf16[256,1024]{1,0:T(8,128)(2,1)S(1)}, bf16[256,1024]{1,0:T(8,128)(2,1)S(1)}, u32[]{:S(2)}, u32[]{:S(2)}) %collective-permute-start.22) | collective-permute-done | bytes 524320 | tf_op jit(solution)/shard_map/ppermute | solution.py:795
  395.7 16.3 %collective-permute-done.24 = bf16[64,1024]{1,0:T(8,128)(2,1)S(1)} collective-permute-done((bf16[64,1024]{1,0:T(8,128)(2,1)S(1)}, bf16[64,1024]{1,0:T(8,128)(2,1)S(1)}, u32[]{:S(2)}, u32[]{:S(2)}) %collective-permute-start.24) | collective-permute-done | bytes 131104 | tf_op jit(solution)/shard_map/ppermute | solution.py:795
  412.1 2.9 collective-permute-start.25
  416.5 2.6 collective-permute-done.25
  422.6 3.0 collective-permute-start.50
  427.8 9.4 %collective-permute-start.27 = (bf16[64,1024]{1,0:T(8,128)(2,1)S(1)}, bf16[64,1024]{1,0:T(8,128)(2,1)S(1)}, u32[]{:S(2)}, u32[]{:S(2)}) collective-permute-start(bf16[64,1024]{1,0:T(8,128)(2,1)S(1)} %pad_maximum_fusion.11), channel_id=1, source_target_pairs={{8,0},{10,2},{12,4},{14,6},{0,8},{2,10},{4,12},{6,14},{24,16},{26,... | collective-permute-start | bytes 393224 | tf_op jit(solution)/shard_map/ppermute | solution.py:795
  437.4 3.4 collective-permute-start.41
  441.0 9.4 %collective-permute-done.41 = bf16[128,1024]{1,0:T(8,128)(2,1)S(1)} collective-permute-done((bf16[128,1024]{1,0:T(8,128)(2,1)S(1)}, bf16[128,1024]{1,0:T(8,128)(2,1)S(1)}, u32[]{:S(2)}, u32[]{:S(2)}) %collective-permute-start.41) | collective-permute-done | bytes 262176 | tf_op jit(solution)/shard_map/ppermute | solution.py:795
  451.4 5.2 collective-permute-start.28
  456.6 3.5 collective-permute-done.42
  460.9 4.9 collective-permute-start.43
  466.7 2.6 collective-permute-start.36
  470.1 2.8 reshape.80
  493.5 4.4 collective-permute-done.44
  502.7 3.4 multiply_reduce_fusion.3
  509.1 37.6 %collective-permute-done.18 = f32[8,512]{1,0:T(8,128)S(1)} collective-permute-done((f32[8,512]{1,0:T(8,128)S(1)}, f32[8,512]{1,0:T(8,128)S(1)}, u32[]{:S(2)}, u32[]{:S(2)}) %collective-permute-start.18) | collective-permute-done | bytes 16416 | tf_op jit(solution)/shard_map/ppermute | solution.py:795
  547.4 3.0 collective-permute-done.19
  550.7 3.5 collective-permute-done.20
  555.7 2.5 maximum_convert_fusion
  559.6 4.6 select_convert_fusion
  (412 shorter events, 135.2 us)
Async XLA Ops:
  0.7 17.9 %collective-permute-start = (bf16[1024,512]{1,0:T(8,128)(2,1)}, bf16[1024,512]{1,0:T(8,128)(2,1)}, u32[]{:S(2)}, u32[]{:S(2)}) collective-permute-start(bf16[1024,512]{1,0:T(8,128)(2,1)} %param.15), channel_id=1, source_target_pairs={{0,1},{1,0},{2,3},{3,2},{4,5},{5,4},{6,7},{7,6},{8,9},{9,8},{10,11... | collective-permute-start | bytes 3145736 | tf_op jit(solution)/shard_map/ppermute | solution.py:850
  2.0 13.5 %collective-permute-start.1 = (bf16[16,512]{1,0:T(8,128)(2,1)S(1)}, bf16[16,512]{1,0:T(8,128)(2,1)S(1)}, u32[]{:S(2)}, u32[]{:S(2)}) collective-permute-start(bf16[16,512]{1,0:T(8,128)(2,1)S(1)} %slice.210), channel_id=1, source_target_pairs={{0,4},{2,6},{4,8},{6,10},{8,12},{10,14},{12,16},{14,18},{16,20},{1... | collective-permute-start | bytes 49160 | tf_op jit(solution)/shard_map/ppermute | solution.py:858
  6.5 71.7 %collective-permute-start.8 = (bf16[1024,512]{1,0:T(8,128)(2,1)}, bf16[1024,512]{1,0:T(8,128)(2,1)}, u32[]{:S(2)}, u32[]{:S(2)}) collective-permute-start(bf16[1024,512]{1,0:T(8,128)(2,1)} %param.16), channel_id=1, source_target_pairs={{0,1},{1,0},{2,3},{3,2},{4,5},{5,4},{6,7},{7,6},{8,9},{9,8},{10,11... | collective-permute-start | bytes 3145736 | tf_op jit(solution)/shard_map/ppermute | solution.py:850
  59.1 14.4 %collective-permute-start.4 = (bf16[528,512]{1,0:T(8,128)(2,1)S(1)}, bf16[528,512]{1,0:T(8,128)(2,1)S(1)}, u32[]{:S(2)}, u32[]{:S(2)}) collective-permute-start(bf16[528,512]{1,0:T(8,128)(2,1)S(1)} %get-tuple-element.69), channel_id=1, source_target_pairs={{4,0},{6,2},{0,4},{2,6},{12,8},{14,10},{8,12},{10,14},{20,16},{22,... | collective-permute-start | bytes 1622024 | tf_op jit(solution)/shard_map/ppermute | solution.py:305
  76.6 13.7 %collective-permute-start.5 = (bf16[528,512]{1,0:T(8,128)(2,1)}, bf16[528,512]{1,0:T(8,128)(2,1)S(1)}, u32[]{:S(2)}, u32[]{:S(2)}) collective-permute-start(bf16[528,512]{1,0:T(8,128)(2,1)} %get-tuple-element.71), channel_id=1, source_target_pairs={{8,0},{10,2},{12,4},{14,6},{0,8},{2,10},{4,12},{6,14},{24,16},{26,... | collective-permute-start | bytes 1622024 | tf_op jit(solution)/shard_map/ppermute | solution.py:305
  93.6 25.1 %collective-permute-start.6 = (bf16[528,512]{1,0:T(8,128)(2,1)S(1)}, bf16[528,512]{1,0:T(8,128)(2,1)S(1)}, u32[]{:S(2)}, u32[]{:S(2)}) collective-permute-start(bf16[528,512]{1,0:T(8,128)(2,1)S(1)} %get-tuple-element.72), channel_id=1, source_target_pairs={{16,0},{18,2},{20,4},{22,6},{24,8},{26,10},{28,12},{30,14},{0,16},... | collective-permute-start | bytes 1622024 | tf_op jit(solution)/shard_map/ppermute | solution.py:305
  119.6 16.4 %collective-permute-start.7 = (bf16[528,512]{1,0:T(8,128)(2,1)S(1)}, bf16[528,512]{1,0:T(8,128)(2,1)S(1)}, u32[]{:S(2)}, u32[]{:S(2)}) collective-permute-start(bf16[528,512]{1,0:T(8,128)(2,1)S(1)} %get-tuple-element.76), channel_id=1, source_target_pairs={{4,0},{6,2},{0,4},{2,6},{12,8},{14,10},{8,12},{10,14},{20,16},{22,... | collective-permute-start | bytes 1622024 | tf_op jit(solution)/shard_map/ppermute | solution.py:305
  183.8 62.7 %collective-permute-start.9 = (f32[1024,512]{1,0:T(8,128)}, f32[1024,512]{1,0:T(8,128)}, u32[]{:S(2)}, u32[]{:S(2)}) collective-permute-start(f32[1024,512]{1,0:T(8,128)} %constant_dynamic-slice_fusion.1), channel_id=1, source_target_pairs={{0,1},{1,0},{2,3},{3,2},{4,5},{5,4},{6,7},{7,6},{8,9},{9,8},{10,11... | collective-permute-start | bytes 6291464 | tf_op jit(solution)/shard_map/ppermute | solution.py:850
  183.8 14.7 %collective-permute-start.10 = (bf16[528,512]{1,0:T(8,128)(2,1)S(1)}, bf16[528,512]{1,0:T(8,128)(2,1)S(1)}, u32[]{:S(2)}, u32[]{:S(2)}) collective-permute-start(bf16[528,512]{1,0:T(8,128)(2,1)S(1)} %copy-done.88), channel_id=1, source_target_pairs={{4,0},{6,2},{0,4},{2,6},{12,8},{14,10},{8,12},{10,14},{20,16},{22,... | collective-permute-start | bytes 1622024 | tf_op jit(solution)/shard_map/ppermute | solution.py:305
  201.5 14.2 %collective-permute-start.11 = (bf16[528,512]{1,0:T(8,128)(2,1)}, bf16[528,512]{1,0:T(8,128)(2,1)}, u32[]{:S(2)}, u32[]{:S(2)}) collective-permute-start(bf16[528,512]{1,0:T(8,128)(2,1)} %get-tuple-element.88), channel_id=1, source_target_pairs={{8,0},{10,2},{12,4},{14,6},{0,8},{2,10},{4,12},{6,14},{24,16},{26,... | collective-permute-start | bytes 1622024 | tf_op jit(solution)/shard_map/ppermute | solution.py:305
  207.4 93.3 %collective-permute-start.38 = (bf16[1024,1024]{1,0:T(8,128)(2,1)}, bf16[1024,1024]{1,0:T(8,128)(2,1)}, u32[]{:S(2)}, u32[]{:S(2)}) collective-permute-start(bf16[1024,1024]{1,0:T(8,128)(2,1)} %fusion.4), channel_id=1, source_target_pairs={{2,0},{0,2},{6,4},{4,6},{10,8},{8,10},{14,12},{12,14},{18,16},{16,... | collective-permute-start | bytes 6291464 | tf_op jit(solution)/shard_map/ppermute | solution.py:795
  219.5 25.5 %collective-permute-start.12 = (bf16[528,512]{1,0:T(8,128)(2,1)S(1)}, bf16[528,512]{1,0:T(8,128)(2,1)S(1)}, u32[]{:S(2)}, u32[]{:S(2)}) collective-permute-start(bf16[528,512]{1,0:T(8,128)(2,1)S(1)} %get-tuple-element.89), channel_id=1, source_target_pairs={{16,0},{18,2},{20,4},{22,6},{24,8},{26,10},{28,12},{30,14},{0,16},... | collective-permute-start | bytes 1622024 | tf_op jit(solution)/shard_map/ppermute | solution.py:305
  245.9 13.8 %collective-permute-start.13 = (bf16[528,512]{1,0:T(8,128)(2,1)S(1)}, bf16[528,512]{1,0:T(8,128)(2,1)S(1)}, u32[]{:S(2)}, u32[]{:S(2)}) collective-permute-start(bf16[528,512]{1,0:T(8,128)(2,1)S(1)} %get-tuple-element.93), channel_id=1, source_target_pairs={{4,0},{6,2},{0,4},{2,6},{12,8},{14,10},{8,12},{10,14},{20,16},{22,... | collective-permute-start | bytes 1622024 | tf_op jit(solution)/shard_map/ppermute | solution.py:305
  250.4 74.3 %collective-permute-start.46 = (f32[]{:T(128)}, f32[]{:T(128)}, u32[]{:S(2)}, u32[]{:S(2)}) collective-permute-start(f32[]{:T(128)} %get-tuple-element.146), channel_id=1, source_target_pairs={{0,1},{1,0},{2,3},{3,2},{4,5},{5,4},{6,7},{7,6},{8,9},{9,8},{10,11... | collective-permute-start | bytes 20 | tf_op jit(solution)/shard_map/ppermute | solution.py:850
  300.6 5.6 collective-permute-start.14
  318.9 7.1 %collective-permute-start.15 = (f32[8,1024]{1,0:T(8,128)S(1)}, f32[8,1024]{1,0:T(8,128)S(1)}, u32[]{:S(2)}, u32[]{:S(2)}) collective-permute-start(f32[8,1024]{1,0:T(8,128)S(1)} %edge.1), channel_id=1, source_target_pairs={{4,0},{6,2},{8,4},{10,6},{12,8},{14,10},{16,12},{18,14},{20,16},{2... | collective-permute-start | bytes 98312 | tf_op jit(solution)/shard_map/ppermute | solution.py:858
  322.0 67.6 %collective-permute-start.39 = (bf16[512,1024]{1,0:T(8,128)(2,1)S(1)}, bf16[512,1024]{1,0:T(8,128)(2,1)}, u32[]{:S(2)}, u32[]{:S(2)}) collective-permute-start(bf16[512,1024]{1,0:T(8,128)(2,1)S(1)} %dynamic-slice_convert_fusion), channel_id=1, source_target_pairs={{4,0},{6,2},{0,4},{2,6},{12,8},{14,10},{8,12},{10,14},{20,16},{22,... | collective-permute-start | bytes 3145736 | tf_op jit(solution)/shard_map/ppermute | solution.py:795
  363.8 12.5 %collective-permute-start.47 = (f32[80,1024]{1,0:T(8,128)S(1)}, f32[80,1024]{1,0:T(8,128)S(1)}, u32[]{:S(2)}, u32[]{:S(2)}) collective-permute-start(f32[80,1024]{1,0:T(8,128)S(1)} %select_maximum_fusion), channel_id=1, source_target_pairs={{2,0},{0,2},{6,4},{4,6},{10,8},{8,10},{14,12},{12,14},{18,16},{16,... | collective-permute-start | bytes 983048 | tf_op jit(solution)/shard_map/ppermute | solution.py:795
  366.9 18.6 %collective-permute-start.22 = (bf16[256,1024]{1,0:T(8,128)(2,1)S(1)}, bf16[256,1024]{1,0:T(8,128)(2,1)S(1)}, u32[]{:S(2)}, u32[]{:S(2)}) collective-permute-start(bf16[256,1024]{1,0:T(8,128)(2,1)S(1)} %dynamic-slice_convert_fusion.3), channel_id=1, source_target_pairs={{2,0},{0,2},{6,4},{4,6},{10,8},{8,10},{14,12},{12,14},{18,16},{16,... | collective-permute-start | bytes 1572872 | tf_op jit(solution)/shard_map/ppermute | solution.py:795
  367.1 19.0 %collective-permute-start.30 = (bf16[256,1024]{1,0:T(8,128)(2,1)S(1)}, bf16[256,1024]{1,0:T(8,128)(2,1)S(1)}, u32[]{:S(2)}, u32[]{:S(2)}) collective-permute-start(bf16[256,1024]{1,0:T(8,128)(2,1)S(1)} %dynamic-slice_convert_fusion.2), channel_id=1, source_target_pairs={{4,0},{6,2},{0,4},{2,6},{12,8},{14,10},{8,12},{10,14},{20,16},{22,... | collective-permute-start | bytes 1572872 | tf_op jit(solution)/shard_map/ppermute | solution.py:795
  376.3 126.4 %collective-permute-start.16 = (f32[1024,512]{1,0:T(8,128)}, f32[1024,512]{1,0:T(8,128)}, u32[]{:S(2)}, u32[]{:S(2)}) collective-permute-start(f32[1024,512]{1,0:T(8,128)} %constant_dynamic-slice_fusion), channel_id=1, source_target_pairs={{0,1},{1,0},{2,3},{3,2},{4,5},{5,4},{6,7},{7,6},{8,9},{9,8},{10,11... | collective-permute-start | bytes 6291464 | tf_op jit(solution)/shard_map/ppermute | solution.py:850
  376.3 11.7 %collective-permute-start.48 = (f32[80,1024]{1,0:T(8,128)S(1)}, f32[80,1024]{1,0:T(8,128)S(1)}, u32[]{:S(2)}, u32[]{:S(2)}) collective-permute-start(f32[80,1024]{1,0:T(8,128)S(1)} %fusion.24), channel_id=1, source_target_pairs={{4,0},{6,2},{0,4},{2,6},{12,8},{14,10},{8,12},{10,14},{20,16},{22,... | collective-permute-start | bytes 983048 | tf_op jit(solution)/shard_map/ppermute | solution.py:795
  385.7 7.6 %collective-permute-start.23 = (bf16[128,1024]{1,0:T(8,128)(2,1)S(1)}, bf16[128,1024]{1,0:T(8,128)(2,1)S(1)}, u32[]{:S(2)}, u32[]{:S(2)}) collective-permute-start(bf16[128,1024]{1,0:T(8,128)(2,1)S(1)} %dynamic-slice_convert_fusion.6), channel_id=1, source_target_pairs={{4,0},{6,2},{0,4},{2,6},{12,8},{14,10},{8,12},{10,14},{20,16},{22,... | collective-permute-start | bytes 786440 | tf_op jit(solution)/shard_map/ppermute | solution.py:795
  386.3 7.8 %collective-permute-start.31 = (bf16[128,1024]{1,0:T(8,128)(2,1)S(1)}, bf16[128,1024]{1,0:T(8,128)(2,1)S(1)}, u32[]{:S(2)}, u32[]{:S(2)}) collective-permute-start(bf16[128,1024]{1,0:T(8,128)(2,1)S(1)} %dynamic-slice_convert_fusion.5), channel_id=1, source_target_pairs={{2,0},{0,2},{6,4},{4,6},{10,8},{8,10},{14,12},{12,14},{18,16},{16,... | collective-permute-start | bytes 786440 | tf_op jit(solution)/shard_map/ppermute | solution.py:795
  388.1 34.5 %collective-permute-start.49 = (f32[80,1024]{1,0:T(8,128)S(1)}, f32[80,1024]{1,0:T(8,128)S(1)}, u32[]{:S(2)}, u32[]{:S(2)}) collective-permute-start(f32[80,1024]{1,0:T(8,128)S(1)} %add.285), channel_id=1, source_target_pairs={{8,0},{10,2},{12,4},{14,6},{0,8},{2,10},{4,12},{6,14},{24,16},{26,... | collective-permute-start | bytes 983048 | tf_op jit(solution)/shard_map/ppermute | solution.py:795
  391.4 45.8 %collective-permute-start.40 = (bf16[256,1024]{1,0:T(8,128)(2,1)S(1)}, bf16[256,1024]{1,0:T(8,128)(2,1)S(1)}, u32[]{:S(2)}, u32[]{:S(2)}) collective-permute-start(bf16[256,1024]{1,0:T(8,128)(2,1)S(1)} %dynamic-slice_convert_fusion.1), channel_id=1, source_target_pairs={{8,0},{10,2},{12,4},{14,6},{0,8},{2,10},{4,12},{6,14},{24,16},{26,... | collective-permute-start | bytes 1572872 | tf_op jit(solution)/shard_map/ppermute | solution.py:795
  393.5 18.6 %collective-permute-start.24 = (bf16[64,1024]{1,0:T(8,128)(2,1)S(1)}, bf16[64,1024]{1,0:T(8,128)(2,1)S(1)}, u32[]{:S(2)}, u32[]{:S(2)}) collective-permute-start(bf16[64,1024]{1,0:T(8,128)(2,1)S(1)} %dynamic-slice_convert_fusion.8), channel_id=1, source_target_pairs={{8,0},{10,2},{12,4},{14,6},{0,8},{2,10},{4,12},{6,14},{24,16},{26,... | collective-permute-start | bytes 393224 | tf_op jit(solution)/shard_map/ppermute | solution.py:795
  394.2 20.9 %collective-permute-start.32 = (bf16[64,1024]{1,0:T(8,128)(2,1)S(1)}, bf16[64,1024]{1,0:T(8,128)(2,1)S(1)}, u32[]{:S(2)}, u32[]{:S(2)}) collective-permute-start(bf16[64,1024]{1,0:T(8,128)(2,1)S(1)} %dynamic-slice_convert_fusion.7), channel_id=1, source_target_pairs={{8,0},{10,2},{12,4},{14,6},{0,8},{2,10},{4,12},{6,14},{24,16},{26,... | collective-permute-start | bytes 393224 | tf_op jit(solution)/shard_map/ppermute | solution.py:795
  412.1 7.0 %collective-permute-start.25 = (bf16[32,1024]{1,0:T(8,128)(2,1)S(1)}, bf16[32,1024]{1,0:T(8,128)(2,1)S(1)}, u32[]{:S(2)}, u32[]{:S(2)}) collective-permute-start(bf16[32,1024]{1,0:T(8,128)(2,1)S(1)} %dynamic-slice_convert_fusion.10), channel_id=1, source_target_pairs={{16,0},{18,2},{20,4},{22,6},{24,8},{26,10},{28,12},{30,14},{0,16},... | collective-permute-start | bytes 196616 | tf_op jit(solution)/shard_map/ppermute | solution.py:795
  415.1 7.4 %collective-permute-start.33 = (bf16[32,1024]{1,0:T(8,128)(2,1)S(1)}, bf16[32,1024]{1,0:T(8,128)(2,1)S(1)}, u32[]{:S(2)}, u32[]{:S(2)}) collective-permute-start(bf16[32,1024]{1,0:T(8,128)(2,1)S(1)} %dynamic-slice_convert_fusion.9), channel_id=1, source_target_pairs={{16,0},{18,2},{20,4},{22,6},{24,8},{26,10},{28,12},{30,14},{0,16},... | collective-permute-start | bytes 196616 | tf_op jit(solution)/shard_map/ppermute | solution.py:795
  419.1 8.7 %collective-permute-start.26 = (bf16[32,1024]{1,0:T(8,128)(2,1)S(1)}, bf16[32,1024]{1,0:T(8,128)(2,1)S(1)}, u32[]{:S(2)}, u32[]{:S(2)}) collective-permute-start(bf16[32,1024]{1,0:T(8,128)(2,1)S(1)} %add_convert_fusion.2), channel_id=1, source_target_pairs={{16,0},{18,2},{20,4},{22,6},{24,8},{26,10},{28,12},{30,14},{0,16},... | collective-permute-start | bytes 196616 | tf_op jit(solution)/shard_map/ppermute | solution.py:795
  422.5 18.4 %collective-permute-start.34 = (bf16[32,1024]{1,0:T(8,128)(2,1)S(1)}, bf16[32,1024]{1,0:T(8,128)(2,1)S(1)}, u32[]{:S(2)}, u32[]{:S(2)}) collective-permute-start(bf16[32,1024]{1,0:T(8,128)(2,1)S(1)} %add_convert_fusion.1), channel_id=1, source_target_pairs={{16,0},{18,2},{20,4},{22,6},{24,8},{26,10},{28,12},{30,14},{0,16},... | collective-permute-start | bytes 196616 | tf_op jit(solution)/shard_map/ppermute | solution.py:795
  422.6 46.6 %collective-permute-start.50 = (f32[80,1024]{1,0:T(8,128)S(1)}, f32[80,1024]{1,0:T(8,128)S(1)}, u32[]{:S(2)}, u32[]{:S(2)}) collective-permute-start(f32[80,1024]{1,0:T(8,128)S(1)} %add.286), channel_id=1, source_target_pairs={{16,0},{18,2},{20,4},{22,6},{24,8},{26,10},{28,12},{30,14},{0,16},... | collective-permute-start | bytes 983048 | tf_op jit(solution)/shard_map/ppermute | solution.py:795
  427.8 22.7 %collective-permute-start.27 = (bf16[64,1024]{1,0:T(8,128)(2,1)S(1)}, bf16[64,1024]{1,0:T(8,128)(2,1)S(1)}, u32[]{:S(2)}, u32[]{:S(2)}) collective-permute-start(bf16[64,1024]{1,0:T(8,128)(2,1)S(1)} %pad_maximum_fusion.11), channel_id=1, source_target_pairs={{8,0},{10,2},{12,4},{14,6},{0,8},{2,10},{4,12},{6,14},{24,16},{26,... | collective-permute-start | bytes 393224 | tf_op jit(solution)/shard_map/ppermute | solution.py:795
  437.4 13.0 %collective-permute-start.41 = (bf16[128,1024]{1,0:T(8,128)(2,1)S(1)}, bf16[128,1024]{1,0:T(8,128)(2,1)S(1)}, u32[]{:S(2)}, u32[]{:S(2)}) collective-permute-start(bf16[128,1024]{1,0:T(8,128)(2,1)S(1)} %dynamic-slice_convert_fusion.4), channel_id=1, source_target_pairs={{16,0},{18,2},{20,4},{22,6},{24,8},{26,10},{28,12},{30,14},{0,16},... | collective-permute-start | bytes 786440 | tf_op jit(solution)/shard_map/ppermute | solution.py:795
  440.9 24.9 %collective-permute-start.35 = (bf16[64,1024]{1,0:T(8,128)(2,1)S(1)}, bf16[64,1024]{1,0:T(8,128)(2,1)S(1)}, u32[]{:S(2)}, u32[]{:S(2)}) collective-permute-start(bf16[64,1024]{1,0:T(8,128)(2,1)S(1)} %pad_maximum_fusion.12), channel_id=1, source_target_pairs={{8,0},{10,2},{12,4},{14,6},{0,8},{2,10},{4,12},{6,14},{24,16},{26,... | collective-permute-start | bytes 393224 | tf_op jit(solution)/shard_map/ppermute | solution.py:795
  450.5 9.6 %collective-permute-start.42 = (bf16[128,1024]{1,0:T(8,128)(2,1)S(1)}, bf16[128,1024]{1,0:T(8,128)(2,1)S(1)}, u32[]{:S(2)}, u32[]{:S(2)}) collective-permute-start(bf16[128,1024]{1,0:T(8,128)(2,1)S(1)} %add_convert_fusion), channel_id=1, source_target_pairs={{16,0},{18,2},{20,4},{22,6},{24,8},{26,10},{28,12},{30,14},{0,16},... | collective-permute-start | bytes 786440 | tf_op jit(solution)/shard_map/ppermute | solution.py:795
  451.4 39.6 %collective-permute-start.28 = (bf16[128,1024]{1,0:T(8,128)(2,1)}, bf16[128,1024]{1,0:T(8,128)(2,1)}, u32[]{:S(2)}, u32[]{:S(2)}) collective-permute-start(bf16[128,1024]{1,0:T(8,128)(2,1)} %pad_maximum_fusion.9), channel_id=1, source_target_pairs={{4,0},{6,2},{0,4},{2,6},{12,8},{14,10},{8,12},{10,14},{20,16},{22,... | collective-permute-start | bytes 786440 | tf_op jit(solution)/shard_map/ppermute | solution.py:795
  460.9 13.5 %collective-permute-start.43 = (bf16[256,1024]{1,0:T(8,128)(2,1)S(1)}, bf16[256,1024]{1,0:T(8,128)(2,1)}, u32[]{:S(2)}, u32[]{:S(2)}) collective-permute-start(bf16[256,1024]{1,0:T(8,128)(2,1)S(1)} %pad_maximum_fusion.8), channel_id=1, source_target_pairs={{8,0},{10,2},{12,4},{14,6},{0,8},{2,10},{4,12},{6,14},{24,16},{26,... | collective-permute-start | bytes 1572872 | tf_op jit(solution)/shard_map/ppermute | solution.py:795
  466.7 34.8 %collective-permute-start.36 = (bf16[128,1024]{1,0:T(8,128)(2,1)}, bf16[128,1024]{1,0:T(8,128)(2,1)}, u32[]{:S(2)}, u32[]{:S(2)}) collective-permute-start(bf16[128,1024]{1,0:T(8,128)(2,1)} %pad_maximum_fusion.10), channel_id=1, source_target_pairs={{2,0},{0,2},{6,4},{4,6},{10,8},{8,10},{14,12},{12,14},{18,16},{16,... | collective-permute-start | bytes 786440 | tf_op jit(solution)/shard_map/ppermute | solution.py:795
  476.8 21.1 %collective-permute-start.44 = (bf16[512,1024]{1,0:T(8,128)(2,1)}, bf16[512,1024]{1,0:T(8,128)(2,1)}, u32[]{:S(2)}, u32[]{:S(2)}) collective-permute-start(bf16[512,1024]{1,0:T(8,128)(2,1)} %pad_maximum_fusion.5), channel_id=1, source_target_pairs={{4,0},{6,2},{0,4},{2,6},{12,8},{14,10},{8,12},{10,14},{20,16},{22,... | collective-permute-start | bytes 3145736 | tf_op jit(solution)/shard_map/ppermute | solution.py:795
  492.2 55.0 %collective-permute-start.29 = (bf16[256,1024]{1,0:T(8,128)(2,1)S(1)}, bf16[256,1024]{1,0:T(8,128)(2,1)S(1)}, u32[]{:S(2)}, u32[]{:S(2)}) collective-permute-start(bf16[256,1024]{1,0:T(8,128)(2,1)S(1)} %pad_maximum_fusion.6), channel_id=1, source_target_pairs={{2,0},{0,2},{6,4},{4,6},{10,8},{8,10},{14,12},{12,14},{18,16},{16,... | collective-permute-start | bytes 1572872 | tf_op jit(solution)/shard_map/ppermute | solution.py:795
  500.0 59.6 %collective-permute-start.45 = (bf16[1024,1024]{1,0:T(8,128)(2,1)S(1)}, bf16[1024,1024]{1,0:T(8,128)(2,1)S(1)}, u32[]{:S(2)}, u32[]{:S(2)}) collective-permute-start(bf16[1024,1024]{1,0:T(8,128)(2,1)S(1)} %pad_maximum_fusion.2), channel_id=1, source_target_pairs={{2,0},{0,2},{6,4},{4,6},{10,8},{8,10},{14,12},{12,14},{18,16},{16,... | collective-permute-start | bytes 6291464 | tf_op jit(solution)/shard_map/ppermute | solution.py:795
  506.1 40.6 %collective-permute-start.18 = (f32[8,512]{1,0:T(8,128)S(1)}, f32[8,512]{1,0:T(8,128)S(1)}, u32[]{:S(2)}, u32[]{:S(2)}) collective-permute-start(f32[8,512]{1,0:T(8,128)S(1)} %broadcast_in_dim.63), channel_id=1, source_target_pairs={{2,0},{0,2},{6,4},{4,6},{10,8},{8,10},{14,12},{12,14},{18,16},{16,... | collective-permute-start | bytes 49160 | tf_op jit(solution)/shard_map/ppermute | solution.py:795
  507.3 43.2 %collective-permute-start.37 = (bf16[256,1024]{1,0:T(8,128)(2,1)S(1)}, bf16[256,1024]{1,0:T(8,128)(2,1)S(1)}, u32[]{:S(2)}, u32[]{:S(2)}) collective-permute-start(bf16[256,1024]{1,0:T(8,128)(2,1)S(1)} %pad_maximum_fusion.7), channel_id=1, source_target_pairs={{4,0},{6,2},{0,4},{2,6},{12,8},{14,10},{8,12},{10,14},{20,16},{22,... | collective-permute-start | bytes 1572872 | tf_op jit(solution)/shard_map/ppermute | solution.py:795
  546.7 3.7 collective-permute-start.19
  550.5 3.7 collective-permute-start.20
  554.2 4.8 collective-permute-start.21
  (92 other events, 1136.2 us)

commit v2 on v1

--- a/solution.py
+++ b/solution.py
@@ -16,7 +16,10 @@
 NORM_EPS = 1e-05
 PACK = DH + 16
 WIDE = DH + 8
-SMALL = 56
+SMALL = 48
+LIMIT = 60
+STRIP = 256
+UNROLL = 4
 
 f32 = jnp.float32
 bf16 = jnp.bfloat16
@@ -95,19 +98,51 @@
     return sums
 
 
+def spread_coefs(maps_ref, coef_ref):
+    count = maps_ref.shape[2]
+    chan = count * QB
+    column = lax.broadcasted_iota(jnp.int32, (count, chan), 1)
+    block = lax.broadcasted_iota(jnp.int32, (count, chan), 0)
+    apart = column - QB * block
+    zero = jnp.zeros((1, count), f32)
+    total = jnp.zeros((24, chan), f32)
+    for out in range(QB):
+        picked = []
+        for m in range(3):
+            for offset in range(1 - QB, QB + 1):
+                inside = 0 <= out + offset < QB and offset < QB
+                at = out * QB + out + offset
+                picked.append(maps_ref[m, at : at + 1, :] if inside else zero)
+        place = jnp.where(apart == out, 1.0, 0.0).astype(bf16)
+        for term in split3(jnp.concatenate(picked, axis=0)):
+            total = total + mm(term, place)
+    for m in range(3):
+        coef_ref[m] = total[8 * m : 8 * (m + 1)]
+
+
+def both_halves(flag, own, other):
+    is_low = flag[1] == 0
+    return jnp.concatenate([jnp.where(is_low, own, other), jnp.where(is_low, other, own)], axis=1)
+
+
 def first_kernel(
-    flag, x_ref, halo_ref, ln_ref, up_ref, cw_ref, cb_ref, coef_ref, gw_ref,
-    normed_ref, inner_ref, conv_ref, active_ref, q_ref, k_ref, v_ref, pre_ref, pad_ref,
+    flag, own_ref, other_ref, hown_ref, hother_ref, ln_ref, up_ref, cw_ref, cb_ref, maps_ref, gate_ref,
+    normed_ref, inner_ref, conv_ref, active_ref, q_ref, k_ref, v_ref, pre_ref, coef_ref, pad_ref, gw_ref,
 ):
     step = pl.program_id(0)
-    tile = x_ref.shape[0]
+    tile = own_ref.shape[0]
 
     @pl.when(step == 0)
     def _():
-        before = mm(normed_rows(halo_ref[...].astype(f32), ln_ref[...]), up_ref[...])
+        halo = both_halves(flag, hown_ref[...].astype(f32), hother_ref[...].astype(f32))
+        before = mm(normed_rows(halo, ln_ref[...]), up_ref[...])
         pad_ref[0:8, :] = jnp.where(flag[0] == 1, 0.0, before[HALO - 8 :, :])
-
-    normed = normed_rows(x_ref[...].astype(f32), ln_ref[...])
+        spread_coefs(maps_ref, coef_ref)
+        gw_ref[...] = jnp.zeros_like(gw_ref)
+        gw_ref[:, :, 0 : gate_ref.shape[2]] = gate_ref[...]
+
+    x = both_halves(flag, own_ref[...].astype(f32), other_ref[...].astype(f32))
+    normed = normed_rows(x, ln_ref[...])
     normed_ref[...] = normed
     inner = mm(normed, up_ref[...])
     inner_ref[...] = inner
@@ -129,27 +164,27 @@
     pre_ref[...] = jnp.transpose(pre)[0:8, :]
 
 
-def first_stage(flag, full, halo, ln, up, cw, cb, coefs, gw):
-    count, width = full.shape
-    chan = up.shape[1]
+def first_stage(flag, own, other, hown, hother, ln, up, cw, cb, maps, gate):
+    count, half = own.shape
+    model, chan = up.shape
     wide = (count, chan)
     return pl.pallas_call(
         first_kernel,
         grid=(count // TILE,),
         in_specs=[
-            smem, rows(width), whole(*halo.shape), whole(*ln.shape), whole(*up.shape), whole(*cw.shape),
-            whole(*cb.shape), whole(*coefs.shape), whole(*gw.shape),
+            smem, rows(half), rows(half), whole(*hown.shape), whole(*hown.shape), whole(*ln.shape),
+            whole(*up.shape), whole(*cw.shape), whole(*cb.shape), whole(*maps.shape), whole(*gate.shape),
         ],
-        out_specs=[rows(width), rows(chan), rows(chan), rows(chan), rows(chan), rows(chan), rows(chan),
-                   pl.BlockSpec((8, TILE), lambda i: (0, i))],
-        out_shape=[shape_of(count, width, dtype=bf16), shape_of(*wide), shape_of(*wide), shape_of(*wide),
+        out_specs=[rows(model), rows(chan), rows(chan), rows(chan), rows(chan), rows(chan), rows(chan),
+                   pl.BlockSpec((8, TILE), lambda i: (0, i)), whole(3, 8, chan)],
+        out_shape=[shape_of(count, model, dtype=bf16), shape_of(*wide), shape_of(*wide), shape_of(*wide),
                    shape_of(*wide, dtype=bf16), shape_of(*wide, dtype=bf16), shape_of(*wide, dtype=bf16),
-                   shape_of(8, count)],
-        scratch_shapes=[pltpu.VMEM((TILE + 8, chan), f32)],
-        compiler_params=params(48),
-        cost_estimate=cost(2 * count * width * chan * 4, count * chan * 20),
+                   shape_of(8, count), shape_of(3, 8, chan)],
+        scratch_shapes=[pltpu.VMEM((TILE + 8, chan), f32), pltpu.VMEM((3, chan, LANES), bf16)],
+        compiler_params=params(LIMIT),
+        cost_estimate=cost(2 * count * model * chan * 4, count * chan * 20),
         name="first",
-    )(flag, full, halo, ln, up, cw, cb, coefs, gw)
+    )(flag, own, other, hown, hother, ln, up, cw, cb, maps, gate)
 
 
 def gates_kernel(place, own_ref, other_ref, bias_ref, row_ref, col_ref, total_ref):
@@ -207,7 +242,7 @@
         in_specs=[smem, whole(8, count), whole(8, count), whole(8, 1)],
         out_specs=[whole(count // BLOCK, 8, BLOCK), whole(count, LANES), whole(8, DH)],
         out_shape=[shape_of(count // BLOCK, 8, BLOCK), shape_of(count, LANES), shape_of(8, DH)],
-        compiler_params=params(24),
+        compiler_params=params(LIMIT),
         cost_estimate=cost(count * 1000, count * 600),
         name="gates",
     )(place, own, other, bias)
@@ -291,13 +326,13 @@
         in_specs=[smem] + [pack_spec(w) for w in ins],
         out_specs=[pack_spec(w) for w in outs],
         out_shape=[pack_shape(w) for w in outs],
-        compiler_params=params(24),
+        compiler_params=params(LIMIT),
         cost_estimate=cost(PACK * DH * 8, PACK * DH * 3 * (len(ins) + len(outs))),
         name=name,
     )(flag, *packs)
 
 
-def pass_states(own, send, place, span, stride):
+def pass_states(own, send, place, span, stride, fillers=((), (), ())):
     devices = lax.axis_size("dp")
 
     def swap(value, bit):
@@ -309,11 +344,16 @@
 
     is_lead = place % 2 == 0
     got = swap(send, 1)
+    done = []
+    got, filler = lax.optimization_barrier((got, fillers[0]))
+    done.append(filler)
     out, total, lead = small_call(pair_kernel, "pair", (1, 0), (0, 1, 1), as_flag(is_lead), own, got)
     before = jnp.zeros_like(own)
     bit = 2
     while bit < span:
         got = swap(out, bit)
+        got, filler = lax.optimization_barrier((got, fillers[min(len(done), len(fillers) - 1)]))
+        done.append(filler)
         upper = (place // bit) % 2 == 1
         if bit * 2 < span:
             out, total, before = small_call(
@@ -321,7 +361,7 @@
             )
         bit *= 2
     out, mine = small_call(last_kernel, "last", (0, 1, 1), (0, 1), as_flag(upper, is_lead), got, before, lead)
-    return mine, swap(out, 1)
+    return mine, swap(out, 1), done
 
 
 def put_states(flag, mine_ref, came_ref, state_ref, vec_ref):
@@ -379,7 +419,7 @@
         out_specs=[pack_spec(1), pack_spec(0)],
         out_shape=[pack_shape(1), pack_shape(0)],
         scratch_shapes=[pltpu.VMEM((2, DH, DH), f32), pltpu.VMEM((8, DH), f32)],
-        compiler_params=params(32),
+        compiler_params=params(LIMIT),
         cost_estimate=cost(4 * count * chan * DH, count * chan * 4),
         name="ends",
     )(flag, k, v, col, total)
@@ -392,8 +432,8 @@
     return jnp.exp(jnp.where(t >= s, expo, -1e30))
 
 
-def lanes_of(*columns):
-    lane = lax.broadcasted_iota(jnp.int32, (columns[0].shape[0], LANES), 1)
+def lanes_of(*columns, offset=0):
+    lane = lax.broadcasted_iota(jnp.int32, (columns[0].shape[0], LANES), 1) - offset
     out = jnp.zeros(lane.shape, f32)
     for i, column in enumerate(columns):
         out = jnp.where(lane == i, column, out)
@@ -430,7 +470,7 @@
                   pl.BlockSpec((TILE // BLOCK, 8, BLOCK), lambda i: (i, 0, 0))],
         out_specs=[rows(chan), rows(LANES)],
         out_shape=[shape_of(count, chan), shape_of(count, LANES)],
-        compiler_params=params(32),
+        compiler_params=params(LIMIT),
         cost_estimate=cost(4 * count * chan * BLOCK, count * chan * 10),
         name="inside",
     )(q, k, v, col, row)
@@ -441,7 +481,7 @@
     active_ref, group_ref, skip_ref, total_ref,
     gated_ref, gig_ref, sgrad_ref, nlow_ref, clow_ref, start_ref, nvec_ref, stat_ref, ggroup_ref, gskip_ref,
     own_ref, send_ref,
-    state_ref, vec_ref, back_ref, bvec_ref,
+    state_ref, vec_ref, back_ref, bvec_ref, cross_ref, ncross_ref,
 ):
     step = pl.program_id(0)
 
@@ -457,19 +497,36 @@
         r0 = pl.multiple_of(b * BLOCK, BLOCK)
         here = pl.ds(r0, BLOCK)
         col = col_ref[here, :]
-        norms = norm_ref[here, :]
         nvec_ref[b] = vec_ref[...]
-        stats = []
+        crosses = []
         for h in range(2):
             part = slice(h * DH, (h + 1) * DH)
             query = q_ref[here, part]
             state = state_ref[h]
             state_low = state.astype(bf16)
             start_ref[h, b] = state_low
+            cross_ref[here, part] = mm(query, state_low)
+            vec = vec_ref[h : h + 1, :]
+            crosses.append(jnp.sum(query.astype(f32) * vec, axis=1, keepdims=True))
+            kept = k_ref[here, part].astype(f32) * col[:, 4 + h : 5 + h]
+            decay = col[0:1, 10 + h : 11 + h]
+            state_ref[h] = decay * state + mm_tn(kept.astype(bf16), v_ref[here, part])
+            vec_ref[h : h + 1, :] = decay * vec + jnp.sum(kept, axis=0, keepdims=True)
+        ncross_ref[here, :] = lanes_of(*crosses)
+        return carry
+
+    lax.fori_loop(0, q_ref.shape[0] // BLOCK, body, 0, unroll=UNROLL)
+
+    def strip(i, carry):
+        here = pl.ds(pl.multiple_of(i * STRIP, STRIP), STRIP)
+        col = col_ref[here, :]
+        norms = norm_ref[here, :]
+        stats = []
+        for h in range(2):
+            part = slice(h * DH, (h + 1) * DH)
             growth = col[:, 2 + h : 3 + h]
-            carried = growth * mm(query, state_low)
-            vec = vec_ref[h : h + 1, :]
-            norm_cross = growth * jnp.sum(query.astype(f32) * vec, axis=1, keepdims=True)
+            carried = growth * cross_ref[here, part]
+            norm_cross = growth * ncross_ref[here, h : h + 1]
             numer = inside_ref[here, part] + carried
             normal = norms[:, h : h + 1] + norm_cross
             over = 1.0 / jnp.maximum(jnp.abs(normal), 1.0)
@@ -501,17 +558,12 @@
             clow_ref[here, part] = (growth * ngrad).astype(bf16)
             moved = jnp.sum(ngrad * carried, axis=1, keepdims=True) + normal_grad * norm_cross
             stats.append((normal_grad, moved))
-            wide = k_ref[here, part].astype(f32)
-            kept = wide * col[:, 4 + h : 5 + h]
-            decay = col[0:1, 10 + h : 11 + h]
-            state_ref[h] = decay * state + mm_tn(kept.astype(bf16), v_ref[here, part])
-            vec_ref[h : h + 1, :] = decay * vec + jnp.sum(kept, axis=0, keepdims=True)
             scaled = col[:, 8 + h : 9 + h] * growth * normal_grad
-            bvec_ref[h : h + 1, :] += jnp.sum(scaled * query.astype(f32), axis=0, keepdims=True)
+            bvec_ref[h : h + 1, :] += jnp.sum(scaled * q_ref[here, part].astype(f32), axis=0, keepdims=True)
         stat_ref[here, :] = lanes_of(stats[0][0], stats[1][0], stats[0][1], stats[1][1])
         return carry
 
-    lax.fori_loop(0, q_ref.shape[0] // BLOCK, body, 0)
+    lax.fori_loop(0, q_ref.shape[0] // STRIP, strip, 0)
     for h in range(2):
         part = slice(h * DH, (h + 1) * DH)
         high, low = split2(clow_ref[:, part].astype(f32) * col_ref[:, 8 + h : 9 + h])
@@ -542,8 +594,9 @@
                    shape_of(8, chan), shape_of(8, chan),
                    pack_shape(1), pack_shape(0)],
         scratch_shapes=[pltpu.VMEM((2, DH, DH), f32), pltpu.VMEM((8, DH), f32),
-                        pltpu.VMEM((2, DH, DH), f32), pltpu.VMEM((8, DH), f32)],
-        compiler_params=params(56),
+                        pltpu.VMEM((2, DH, DH), f32), pltpu.VMEM((8, DH), f32),
+                        pltpu.VMEM((TILE, chan), f32), pltpu.VMEM((TILE, LANES), f32)],
+        compiler_params=params(LIMIT),
         cost_estimate=cost(10 * count * chan * DH, count * chan * 40),
         name="middle",
     )(flag, mine, came, q, k, v, inside, norms, col, gate, dgated, active, group, skip, total)
@@ -617,10 +670,10 @@
             from_here, lanes_of(*cum_cols), (((1,), (0,)), ((), ())), precision=highest, preferred_element_type=f32
         )
         forget = [sums[:, h : h + 1] * col[:, 14 + h : 15 + h] for h in range(2)]
-        pre_ref[here, :] = lanes_of(*in_cols, *forget).astype(bf16)
+        pre_ref[here, :] = lanes_of(*in_cols, *forget, offset=4 * flag[1]).astype(bf16)
         return carry
 
-    lax.fori_loop(0, per, body, 0)
+    lax.fori_loop(0, per, body, 0, unroll=2)
 
 
 def back_stage(flag, mine, came, q, k, v, nlow, clow, start, nvec, col, row, stat):
@@ -639,7 +692,7 @@
         out_specs=[flip, flip, flip, thin],
         out_shape=[shape_of(count, chan)] * 3 + [shape_of(count, LANES, dtype=bf16)],
         scratch_shapes=[pltpu.VMEM((2, DH, DH), f32), pltpu.VMEM((8, DH), f32)],
-        compiler_params=params(56),
+        compiler_params=params(LIMIT),
         cost_estimate=cost(14 * count * chan * DH, count * chan * 30),
         name="back",
     )(flag, mine, came, q, k, v, nlow, clow, start, nvec, col, row, stat)
@@ -662,8 +715,8 @@
     return active_grad * sig * (1.0 + conv * (1.0 - sig))
 
 
-def edge_kernel(qg_ref, kg_ref, pre_ref, sgrad_ref, conv_ref, skip_ref, coef_ref, gwt_ref, out_ref):
-    pre = pre_ref[...]
+def edge_kernel(qg_ref, kg_ref, pre_ref, other_ref, sgrad_ref, conv_ref, skip_ref, coef_ref, gwt_ref, out_ref):
+    pre = pre_ref[...] + other_ref[...]
     query_all = qg_ref[...] + mm(pre, gwt_ref[0])
     key_all = kg_ref[...] + mm(pre, gwt_ref[1])
     reach = QB - 1
@@ -678,25 +731,25 @@
         out_ref[:, part] = conv_grad_of(total, conv_ref[:, part])[0:8, :]
 
 
-def edge_stage(qg, kg, pre8, sgrad, conv, skip, coefs, gwt):
+def edge_stage(qg, kg, pre, other, sgrad, conv, skip, coefs, gwt):
     chan = qg.shape[1]
     top = rows(chan, HALO)
     return pl.pallas_call(
         edge_kernel,
         grid=(1,),
-        in_specs=[top, top, rows(LANES, HALO), top, top, whole(*skip.shape), whole(*coefs.shape),
+        in_specs=[top, top, rows(LANES, HALO), rows(LANES, HALO), top, top, whole(*skip.shape), whole(*coefs.shape),
                   whole(*gwt.shape)],
         out_specs=whole(8, chan),
         out_shape=shape_of(8, chan),
-        compiler_params=params(16),
+        compiler_params=params(LIMIT),
         cost_estimate=cost(10**7, 10**6),
         name="edge",
-    )(qg, kg, pre8, sgrad, conv, skip, coefs, gwt)
+    )(qg, kg, pre, other, sgrad, conv, skip, coefs, gwt)
 
 
 def maps_kernel(
-    flag, qg_ref, kg_ref, vg_ref, pre_ref, sgrad_ref, conv_ref, inner_ref, q_ref, k_ref, v_ref, edge_ref,
-    skip_ref, cw_ref, coef_ref, gwt_ref,
+    flag, qg_ref, kg_ref, vg_ref, mine_ref, other_ref, sgrad_ref, conv_ref, inner_ref, q_ref, k_ref, v_ref, edge_ref,
+    skip_ref, cw_ref, coef_ref, gwt_ref, ggroup_ref, gskip_ref,
     low_ref, small_ref,
     pad_ref, hi_ref, lo_ref, gmap_ref,
 ):
@@ -720,7 +773,7 @@
                     dense = jnp.where(apart == offset, coef, dense)
                 hi_ref[m, g], lo_ref[m, g] = split2(dense)
 
-    pre = pre_ref[...]
+    pre = mine_ref[...] + other_ref[...]
     conv = conv_ref[...]
     inner = inner_ref[...]
     query_all = split2(qg_ref[...] + mm(pre, gwt_ref[0]))
@@ -765,12 +818,15 @@
         for m in range(3):
             for g in range(groups):
                 held = jnp.where(r // QB == c // QB, gmap_ref[m, g], 0.0)
-                small_ref[8 * (m + 4) : 8 * (m + 5), g * GROUP : (g + 1) * GROUP] = lax.dot_general(
+                found = lax.dot_general(
                     pick, held, (((1,), (1,)), ((), ())), precision=highest, preferred_element_type=f32
                 )
-
-
-def maps_stage(flag, qg, kg, vg, pre8, sgrad, conv, inner, q, k, v, edge, skip, cw, coefs, gwt):
+                small_ref[32 + QB * m : 32 + QB * (m + 1), g * GROUP : (g + 1) * GROUP] = found[0:QB]
+        small_ref[taps + 2 : taps + 3, :] = ggroup_ref[0:1, :]
+        small_ref[taps + 3 : taps + 4, :] = gskip_ref[0:1, :]
+
+
+def maps_stage(flag, qg, kg, vg, pre, other, sgrad, conv, inner, q, k, v, edge, skip, cw, coefs, gwt, ggroup, gskip):
     count, chan = qg.shape
     tiles = count // TILE
     flip = rows(chan, flip=tiles)
@@ -778,16 +834,18 @@
     return pl.pallas_call(
         maps_kernel,
         grid=(tiles,),
-        in_specs=[smem, flip, flip, flip, rows(LANES, flip=tiles), flip, flip, flip, flip, flip, flip,
-                  whole(8, chan), whole(*skip.shape), whole(*cw.shape), whole(*coefs.shape), whole(*gwt.shape)],
+        in_specs=[smem, flip, flip, flip, rows(LANES, flip=tiles), rows(LANES, flip=tiles), flip, flip, flip, flip,
+                  flip, flip,
+                  whole(8, chan), whole(*skip.shape), whole(*cw.shape), whole(*coefs.shape), whole(*gwt.shape),
+                  whole(8, chan), whole(8, chan)],
         out_specs=[flip, whole(SMALL, chan)],
         out_shape=[shape_of(count, chan, dtype=bf16), shape_of(SMALL, chan)],
         scratch_shapes=[pltpu.VMEM((TILE + 8, chan), f32), pltpu.VMEM((3, groups, GROUP, GROUP), bf16),
                         pltpu.VMEM((3, groups, GROUP, GROUP), bf16), pltpu.VMEM((3, groups, GROUP, GROUP), f32)],
-        compiler_params=params(60),
+        compiler_params=params(LIMIT),
         cost_estimate=cost(20 * count * chan * GROUP, count * chan * 32),
         name="maps",
-    )(flag, qg, kg, vg, pre8, sgrad, conv, inner, q, k, v, edge, skip, cw, coefs, gwt)
+    )(flag, qg, kg, vg, pre, other, sgrad, conv, inner, q, k, v, edge, skip, cw, coefs, gwt, ggroup, gskip)
 
 
 def exchanged(value, bit):
@@ -795,21 +853,52 @@
     return lax.ppermute(value, "dp", route)
 
 
-def summed(value, bits):
-    place = lax.axis_index("dp")
+def halved(value, bit):
+    mine = (lax.axis_index("dp") // bit) % 2
     width = value.shape[1]
-    for bit in bits:
-        mine = (place // bit) % 2
-        size = value.shape[0] // 2
-        send = lax.dynamic_slice(value, ((1 - mine) * size, 0), (size, width)).astype(bf16)
-        keep = lax.dynamic_slice(value, (mine * size, 0), (size, width))
-        value = keep + exchanged(send, bit).astype(f32)
+    size = value.shape[0] // 2
+    send = lax.dynamic_slice(value, ((1 - mine) * size, 0), (size, width)).astype(bf16)
+    keep = lax.dynamic_slice(value, (mine * size, 0), (size, width))
+    return keep + exchanged(send, bit).astype(f32)
+
+
+def joined_halves(value, bit):
+    first = (lax.axis_index("dp") // bit) % 2 == 0
+    other = exchanged(value, bit)
+    return jnp.concatenate([jnp.where(first, value, other), jnp.where(first, other, value)], axis=0)
+
+
+def finished(pair, bits):
+    value = jnp.concatenate(pair, axis=0)
+    for bit in bits[2:]:
+        value = halved(value, bit)
     value = value.astype(bf16)
-    for bit in reversed(bits):
-        first = (place // bit) % 2 == 0
-        other = exchanged(value, bit)
-        value = jnp.concatenate([jnp.where(first, value, other), jnp.where(first, other, value)], axis=0)
-    return value
+    for bit in reversed(bits[2:]):
+        value = joined_halves(value, bit)
+    size = value.shape[0] // 2
+    one, two = joined_halves(value[:size], bits[1]), joined_halves(value[size:], bits[0])
+    return jnp.concatenate([joined_halves(one, bits[0]), joined_halves(two, bits[1])], axis=0)
+
+
+def half_products(pairs, side):
+    found = []
+    for left, right in pairs:
+        size = left.shape[1] // 2
+        found.append(mm_tn(lax.dynamic_slice_in_dim(left, side * size, size, axis=1), right))
+    return found
+
+
+def shares(value):
+    devices = lax.axis_size("dp")
+    groups = [[i for i in range(devices) if i & 5 == low] for low in (0, 1, 4, 5)]
+    return lax.psum_scatter(value, "dp", scatter_dimension=0, axis_index_groups=groups, tiled=True)
+
+
+def from_shares(every):
+    devices = lax.axis_size("dp")
+    size, width = every.shape[0] // devices, every.shape[1]
+    every = every.reshape(devices // 8, 2, 2, 2, size, width)
+    return [jnp.transpose(every[:, i], (2, 0, 1, 3, 4)).reshape(-1, width).astype(f32) for i in range(2)]
 
 
 def all_sum(value, bits):
@@ -818,16 +907,8 @@
     return value
 
 
-def band_rows(weight):
-    size = weight.shape[1]
-    found = []
-    for offset in range(1 - size, size):
-        pieces = [
-            weight[:, o, o + offset] if 0 <= o + offset < size else jnp.zeros_like(weight[:, 0, 0])
-            for o in range(size)
-        ]
-        found.append(jnp.stack(pieces, axis=1).reshape(-1))
-    return jnp.stack(found + [jnp.zeros_like(found[0])])
+def map_rows(weight):
+    return weight.reshape(weight.shape[0], -1).T
 
 
 def on_device(
@@ -849,77 +930,85 @@
     def across(value):
         return lax.ppermute(value, "tensor", [(0, 1), (1, 0)])
 
-    def side_by_side(own):
-        other = across(own)
+    def side_by_side(own, other):
         return jnp.concatenate([jnp.where(low_half, own, other), jnp.where(low_half, other, own)], axis=1)
 
     def along(value, distance):
         route = [(i - distance, i) for i in range(devices) if 0 <= i - distance < devices]
         return lax.ppermute(value, "dp", route)
 
-    def flag_of(value):
-        return jnp.asarray(value).astype(jnp.int32)[None]
-
-    halo = side_by_side(along(tokens[count - HALO :], stride))
-    full = side_by_side(tokens)
-    full_cot = side_by_side(cotangent)
-
-    coefs = jnp.stack([band_rows(w) for w in (query_weight, key_weight, value_weight)])
-    gw = jnp.pad(gate_weight, ((0, 0), (0, 0), (0, LANES - gate_weight.shape[2])))
-    gwt = jnp.swapaxes(gw, 1, 2)
-
-    normed, inner, conv, active, q, k, v, pre = first_stage(
-        flag_of(piece == 0), full, halo, ln_weight[None], up_inner, conv_weight, conv_bias[None],
-        coefs, gw,
-    )
-    row, col, total = gates_stage(flag_of(t_place), pre, across(pre), gate_bias[:, None])
-    even = flag_of(piece % 2 == 0)
+    def flags(*values):
+        return jnp.stack([jnp.asarray(v).astype(jnp.int32) for v in values])
+
+    halo = along(tokens[count - HALO :], stride)
+    other_tokens = across(tokens)
+    full = side_by_side(tokens, other_tokens)
+    full_cot = side_by_side(cotangent, across(cotangent))
+
+    maps = jnp.stack([map_rows(w) for w in (query_weight, key_weight, value_weight)])
+    heads = gate_bias.shape[0] // 2
+    local = heads // 2
+    order = [kind * heads + t * local + j for t in range(2) for kind in range(2) for j in range(local)]
+    gwt = jnp.pad(
+        jnp.swapaxes(gate_weight, 1, 2)[:, jnp.array(order)], ((0, 0), (0, LANES - 2 * heads), (0, 0))
+    )
+
+    normed, inner, conv, active, q, k, v, pre, coefs = first_stage(
+        flags(piece == 0, t_place), tokens, other_tokens, halo, across(halo), ln_weight[None], up_inner,
+        conv_weight, conv_bias[None], maps, gate_weight,
+    )
+    row, col, total = gates_stage(flags(t_place), pre, across(pre), gate_bias[:, None])
+    even = flags(piece % 2 == 0)
     own, send = ends_stage(even, k, v, col, total)
-    mine, came = pass_states(own, send, piece, span, stride)
     gate_in = mm(normed, up_gate)
     dgated = mm_nt(full_cot, down_weight)
     inside, norms = inside_stage(q, k, v, col, row)
+    mine, came, done = pass_states(
+        own, send, piece, span, stride, ((inside, norms), (dgated,), (gate_in,))
+    )
+    (inside, norms), (dgated,), (gate_in,) = done
     (
         gated, gate_in_grad, sgrad, nlow, clow, start, nvec, stat, ggroup, gskip, own, send
     ) = middle_stage(
         even, mine, came, q, k, v, inside, norms, col, gate_in, dgated, active, group_weight[None],
         skip_weight[None], total,
     )
-    mine, came = pass_states(own, send, span - 1 - piece, span, stride)
+    pairs = ((gated, full_cot), (normed, gate_in_grad))
+    lowest = lax.axis_index("dp") % 2
+    sends = [value.astype(bf16) for value in half_products(pairs, 1 - lowest)]
+    keeps = [
+        value + exchanged(sent, 1).astype(f32) for value, sent in zip(half_products(pairs, lowest), sends)
+    ]
+    both = jnp.concatenate(keeps, axis=0)
+    branch = mm(gated, down_weight)
+    second = (lax.axis_index("dp") // 4) % 2
+    away = lax.dynamic_slice_in_dim(both, (1 - second) * (model // 2), model // 2, axis=0).astype(bf16)
+    mine, came, done = pass_states(own, send, span - 1 - piece, span, stride, (sends, (branch,), (both, away)))
+    _, (branch,), (both, away) = done
+    both = lax.dynamic_slice_in_dim(both, second * (model // 2), model // 2, axis=0)
+    both = both + exchanged(away, 4).astype(f32)
+    mine, came, both = lax.optimization_barrier((mine, came, both))
+    share = shares(both)
 
     bits = [1 << n for n in range(devices.bit_length() - 1)]
-    early = summed(jnp.concatenate([mm_tn(gated, full_cot), mm_tn(normed, gate_in_grad)], axis=0), bits)
-    branch = mm(gated, down_weight)
     keep_half = lax.dynamic_slice_in_dim(branch, t_place * half, half, axis=1)
     send_half = lax.dynamic_slice_in_dim(branch, (1 - t_place) * half, half, axis=1)
     result = tokens.astype(f32) + (keep_half + across(send_half))
     squares = jnp.sum(result * result)
     gate_part = mm_nt(gate_in_grad, up_gate)
 
-    qg, kg, vg, pre_own = back_stage(even, mine, came, q, k, v, nlow, clow, start, nvec, col, row, stat)
+    qg, kg, vg, pre_own = back_stage(flags(piece % 2 == 0, t_place), mine, came, q, k, v, nlow, clow, start, nvec, col, row, stat)
     pre_other = across(pre_own)
-    heads = gate_bias.shape[0] // 2
-    local = heads // 2
-    a = jnp.where(low_half, pre_own, pre_other)
-    c = jnp.where(low_half, pre_other, pre_own)
-    pre8 = jnp.concatenate(
-        [a[:, 0:local], c[:, 0:local], a[:, local : 2 * local], c[:, local : 2 * local],
-         jnp.zeros((count, LANES - 2 * heads), bf16)], axis=1,
-    )
     skip = skip_weight[None]
-    edge = along(edge_stage(qg, kg, pre8, sgrad, conv, skip, coefs, gwt), -stride)
+    edge = along(edge_stage(qg, kg, pre_own, pre_other, sgrad, conv, skip, coefs, gwt), -stride)
+    edge, share = lax.optimization_barrier((edge, share.astype(bf16)))
+    every = lax.all_gather(share, "dp", axis=0, tiled=True)
     inner_low, small = maps_stage(
-        flag_of(piece == span - 1), qg, kg, vg, pre8, sgrad, conv, inner, q, k, v, edge, skip, conv_weight,
-        coefs, gwt,
-    )
-    grad_up_inner = mm_tn(normed, inner_low)
-    other_bits = [bits[1], bits[0]] + bits[2:]
-    late = jnp.concatenate(
-        [summed(grad_up_inner[: model // 2], bits), summed(grad_up_inner[model // 2 :], other_bits)], axis=0
-    )
-    ones = jnp.pad((squares + across(squares))[None, None], ((0, 7), (0, chan - 1)))
-    small = all_sum(jnp.concatenate([small, ggroup, gskip, ones], axis=0), bits)
-
+        flags(piece == span - 1), qg, kg, vg, pre_own, pre_other, sgrad, conv, inner, q, k, v, edge, skip, conv_weight,
+        coefs, gwt, ggroup, gskip,
+    )
+    grad_up_inner, inner_low = lax.optimization_barrier((mm_tn(normed, inner_low), inner_low))
+    late = [halved(grad_up_inner[: model // 2], bits[0]), halved(grad_up_inner[model // 2 :], bits[1])]
     part = gate_part + mm_nt(inner_low, up_inner)
     wide = full.astype(f32)
     centered = wide - jnp.mean(wide, axis=1, keepdims=True)
@@ -929,6 +1018,8 @@
     mean_h = jnp.mean(scaled, axis=1)
     mean_hx = jnp.mean(scaled * xhat, axis=1)
     means = jnp.stack([mean_h, mean_hx])
+    late, part, means = lax.optimization_barrier((late, part, means))
+    late = [halved(late[0], bits[1]), halved(late[1], bits[0])]
     means = means + across(means)
     own_part = lax.dynamic_slice_in_dim(part, t_place * half, half, axis=1)
     send_part = lax.dynamic_slice_in_dim(part, (1 - t_place) * half, half, axis=1)
@@ -941,16 +1032,22 @@
     )
     grad_ln = jnp.sum(normed_grad * xhat_own, axis=0)
 
-    grad_ln = all_sum(jnp.broadcast_to(grad_ln[None], (8, half)), bits)[0]
+    late, grad_ln, token_grad, every = lax.optimization_barrier((late, grad_ln, token_grad, every))
+    last = jnp.concatenate([grad_ln, jnp.broadcast_to(squares + across(squares), (LANES,))])
+    small = all_sum(small + jnp.pad(last[None], ((SMALL - 1, 0), (0, chan - half - LANES))), bits)
+    grad_ln = small[SMALL - 1, :half]
+    late = finished(late, bits)
+    early = from_shares(every)
     taps = conv_weight.shape[0]
-    folded = small[32:56].reshape(3, 8, chan)[:, :band].reshape(3, band, chan // band, band)
+    folded = small[32 : 32 + 3 * band].reshape(3, band, chan // band, band)
     folded = jnp.transpose(folded, (0, 2, 3, 1))
-    gate_rows = jnp.swapaxes(small[8:32].reshape(3, 8, chan), 1, 2)
-    rms = jnp.sqrt(small[72, 0:1] / (count * model * devices))
+    back_order = jnp.array([order.index(c) for c in range(2 * heads)])
+    gate_rows = jnp.swapaxes(small[8:32].reshape(3, 8, chan)[:, back_order], 1, 2)
+    rms = jnp.sqrt(small[SMALL - 1, half : half + 1] / (count * model * devices))
     return (
-        result.astype(bf16), token_grad, grad_ln, late.astype(f32), early[model:].astype(f32), small[:taps],
-        small[taps], folded[0], folded[1], folded[2], gate_rows, small[taps + 1, : 2 * heads], small[56],
-        small[64], early[:model].astype(f32), rms,
+        result.astype(bf16), token_grad, grad_ln, late.astype(f32), early[1], small[:taps],
+        small[taps], folded[0], folded[1], folded[2], gate_rows, small[taps + 1, : 2 * heads][back_order], small[taps + 2],
+        small[taps + 3], early[0], rms,
     )
 
 

time: 575 us -> 492 us (0.86)
  waiting for transfers between devices: 188 us -> 128 us
  starting transfers between devices: 75.8 us -> 37.9 us
  local copies, waits for them, and re-layouts: 69.6 us -> 48.7 us
  Pallas kernels: 155 us -> 168 us
  matrix products: 29.6 us -> 42.2 us
  between operations: 5.87 us -> 18 us
    ppermute x8, waiting for transfers between devices: 90.3 us -> 41.9 us  [swap(): return lax.ppermute(value, 'dp', route)]
    ppermute x32 -> x19, starting transfers between devices: 58.2 us -> 17.4 us  [exchanged(): return lax.ppermute(value, 'dp', route)]
    ppermute x32 -> x19, waiting for transfers between devices: 96.5 us -> 73.6 us  [exchanged(): return lax.ppermute(value, 'dp', route)]
    unnamed x182 -> x83, local copies, waits for them, and re-layouts: 38.6 us -> 18.4 us
    pallas_call x6, Pallas kernels: 7.67 us -> 19.6 us  [small_call(): pl.pallas_call(kernel, grid=(1,), in_specs=[smem] + [pack_spec(w) for w i...]
    reduce_scatter x0 -> x1, waiting for transfers between devices: none -> 10.3 us  [shares(): lax.psum_scatter(value, 'dp', scatter_dimension=0, axis_index_groups=grou...]
    pallas_call x1, Pallas kernels: 40 us -> 30.7 us  [middle_stage(): pl.pallas_call(middle_kernel, grid=(count // TILE,), in_specs=[smem, pack...]
    dot_general x3 -> x5, matrix products: 9.7 us -> 18.2 us  [mm_tn(): lax.dot_general(left, right, (((0,), (0,)), ((), ())), preferred_element_...]
  transfers between devices with their start and end apart: 51 -> 40, of which waited for: 22 -> 24; matrix products, arithmetic and copies ran while one was open for 17% -> 25% of each run, Pallas kernels for 20% -> 27%
where the time goes in v2:
time: 492 us; the launch traced here: 484 us
  Pallas kernels  168 us (34%)
  waiting for transfers between devices  128 us (26%)
  local copies, waits for them, and re-layouts  48.7 us (10%)
  matrix products  42.2 us (9%)
  other arithmetic  41.4 us (8%)
  starting transfers between devices  37.9 us (8%)
  between operations  18 us (4%)
    ppermute x19, waiting for transfers between devices, exchanged(): return lax.ppermute(value, 'dp', route)  73.6 us
    ppermute x8, waiting for transfers between devices, swap(): return lax.ppermute(value, 'dp', route)  41.9 us
    pallas_call x1, Pallas kernels, back_stage(): pl.pallas_call(back_kernel, grid=(tiles,), in_specs=[smem, pack_spec(1),...  37.8 us
    pallas_call x1, Pallas kernels, maps_stage(): pl.pallas_call(maps_kernel, grid=(tiles,), in_specs=[smem, flip, flip, fl...  30.8 us
    pallas_call x1, Pallas kernels, middle_stage(): pl.pallas_call(middle_kernel, grid=(count // TILE,), in_specs=[smem, pack...  30.7 us
    pallas_call x1, Pallas kernels, first_stage(): pl.pallas_call(first_kernel, grid=(count // TILE,), in_specs=[smem, rows(...  25.7 us
    pallas_call x6, Pallas kernels, small_call(): pl.pallas_call(kernel, grid=(1,), in_specs=[smem] + [pack_spec(w) for w i...  19.6 us
    unnamed x83, local copies, waits for them, and re-layouts  18.4 us
  transfers between devices with their start and end apart: 40, of which 24 were waited for; matrix products, arithmetic and copies ran while one was open for 25% of the time, Pallas kernels for 27%

profile of v2, /device:TPU:0, one launch (start us, length us, event | category | flops | bytes accessed | tf_op | source)
XLA Modules:
  0.0 483.8 jit_solution(15585201269149106813)
XLA Ops:
  8.5 4.5 collective-permute-start.1
  20.0 25.7 %first.1 = (bf16[1024,1024]{1,0:T(8,128)(2,1)}, f32[1024,1024]{1,0:T(8,128)}, f32[1024,1024]{1,0:T(8,128)}, f32[1024,1024]{1,0:T(8,128)}, bf16[1024,1024]{1,0:T(...) custom-call(s32[2]{0:T(128)} %pad_add_fusion.2.flag, ...), custom_call_target="tpu_custom_call" | custom-call | flops 8589934592 | bytes 20971520 | tf_op jit(solution)/shard_map/first/pallas_call | solution.py:171
  47.8 2.9 gates.1
  50.8 7.1 %ends.1 = (f32[520,512]{1,0:T(8,128)}, bf16[528,512]{1,0:T(8,128)(2,1)}) custom-call(s32[1]{0:T(128)} %bitcast.1.flag, bf16[1024,1024]{1,0:T(8,128)(2,1)} %get-tuple-element.93.k_ref, bf16[1024,1024]{1,0:T(8,128)(2,1)} %get-tuple-element.94.v_ref, f32[1024,128]{1,0:T(8,128)} %get-tuple-element.96.col_ref, f32[8,512]{1,0:T(8,128)} %get-tuple-element.97.total_ref), custom_call_target="tpu_custom_call" | custom-call | flops 2147483648 | bytes 4194304 | tf_op jit(solution)/shard_map/ends/pallas_call | solution.py:415
  60.0 10.6 %inside.1 = (f32[1024,1024]{1,0:T(8,128)}, f32[1024,128]{1,0:T(8,128)}) custom-call(bf16[1024,1024]{1,0:T(8,128)(2,1)} %get-tuple-element.100.q_ref, bf16[1024,1024]{1,0:T(8,128)(2,1)} %get-tuple-element.93.k_ref, bf16[1024,1024]{1,0:T(8,128)(2,1)} %get-tuple-element.94.v_ref, f32[1024,128]{1,0:T(8,128)} %get-tuple-element.96.col_ref, ...), custom_call_target="tpu_custom_call" | custom-call | flops 268435456 | bytes 10485760 | tf_op jit(solution)/shard_map/inside/pallas_call | solution.py:466
  73.2 3.1 pair.2
  79.4 4.5 fusion.9.dgated_ref
  83.9 6.2 %collective-permute-done.5.got_ref = bf16[528,512]{1,0:T(8,128)(2,1)S(1)} collective-permute-done((bf16[528,512]{1,0:T(8,128)(2,1)}, bf16[528,512]{1,0:T(8,128)(2,1)S(1)}, u32[]{:S(2)}, u32[]{:S(2)}) %collective-permute-start.5) | collective-permute-done | bytes 540704 | tf_op jit(solution)/shard_map/ppermute | solution.py:340
  91.3 3.5 step.2
  94.8 2.7 collective-permute-start.7
  97.5 5.9 %fusion.21.gate_ref = f32[1024,1024]{1,0:T(8,128)} fusion(bf16[1024,1024]{1,0:T(8,128)(2,1)} %get-tuple-element.109, bf16[1024,1024]{1,0:T(8,128)(2,1)S(1)} %copy-done), kind=kOutput, calls=%fused_computation.103 | convolution fusion | flops 2147483648 | bytes 8388608 | tf_op jit(solution)/shard_map/dot_general | solution.py:30
  103.4 16.8 %collective-permute-done.7.got_ref = bf16[528,512]{1,0:T(8,128)(2,1)S(1)} collective-permute-done((bf16[528,512]{1,0:T(8,128)(2,1)}, bf16[528,512]{1,0:T(8,128)(2,1)S(1)}, u32[]{:S(2)}, u32[]{:S(2)}) %collective-permute-start.7) | collective-permute-done | bytes 540704 | tf_op jit(solution)/shard_map/ppermute | solution.py:340
  121.0 3.2 last.2
  125.5 11.8 %collective-permute-done.8.came_ref = bf16[528,512]{1,0:T(8,128)(2,1)S(1)} collective-permute-done((bf16[528,512]{1,0:T(8,128)(2,1)}, bf16[528,512]{1,0:T(8,128)(2,1)S(1)}, u32[]{:S(2)}, u32[]{:S(2)}) %collective-permute-start.8) | collective-permute-done | bytes 540704 | tf_op jit(solution)/shard_map/ppermute | solution.py:340
  138.2 30.7 %middle.1 = (bf16[1024,1024]{1,0:T(8,128)(2,1)}, bf16[1024,1024]{1,0:T(8,128)(2,1)}, f32[1024,1024]{1,0:T(8,128)}, bf16[1024,1024]{1,0:T(8,128)(2,1)}, bf16[1024...) custom-call(s32[1]{0:T(128)} %bitcast.1.flag, ...), custom_call_target="tpu_custom_call" | custom-call | flops 5368709120 | bytes 41943040 | tf_op jit(solution)/shard_map/middle/pallas_call | solution.py:582
  170.4 4.3 convolution_convert_fusion
  181.3 3.1 pair.3
  184.4 3.4 collective-permute-start.10
  187.8 6.6 %fusion.22 = f32[1024,1024]{1,0:T(8,128)} fusion(bf16[1024,1024]{1,0:T(8,128)(2,1)} %get-tuple-element.122, bf16[1024,1024]{1,0:T(8,128)(2,1)} %param.31), kind=kOutput, calls=%fused_computation.104 | convolution fusion | flops 2147483648 | bytes 8388608 | tf_op jit(solution)/shard_map/dot_general | solution.py:30
  194.3 6.8 %collective-permute-done.14 = bf16[512,1024]{1,0:T(8,128)(2,1)} collective-permute-done((bf16[512,1024]{1,0:T(8,128)(2,1)}, bf16[512,1024]{1,0:T(8,128)(2,1)}, u32[]{:S(2)}, u32[]{:S(2)}) %collective-permute-start.14) | collective-permute-done | bytes 1048608 | tf_op jit(solution)/shard_map/ppermute | solution.py:853
  201.2 3.8 convert_add_fusion.2
  205.9 3.5 step.3
  209.3 11.0 %collective-permute-done.13 = bf16[512,1024]{1,0:T(8,128)(2,1)} collective-permute-done((bf16[512,1024]{1,0:T(8,128)(2,1)}, bf16[512,1024]{1,0:T(8,128)(2,1)}, u32[]{:S(2)}, u32[]{:S(2)}) %collective-permute-start.13) | collective-permute-done | bytes 1048608 | tf_op jit(solution)/shard_map/ppermute | solution.py:853
  220.3 3.1 convert_add_fusion.3
  224.3 2.6 pad_maximum_fusion
  226.9 3.0 collective-permute-done.12.got_ref
  230.5 3.2 last.3
  234.4 17.9 %collective-permute-done.16 = bf16[512,1024]{1,0:T(8,128)(2,1)} collective-permute-done((bf16[512,1024]{1,0:T(8,128)(2,1)S(1)}, bf16[512,1024]{1,0:T(8,128)(2,1)}, u32[]{:S(2)}, u32[]{:S(2)}) %collective-permute-start.16) | collective-permute-done | bytes 1048608 | tf_op jit(solution)/shard_map/ppermute | solution.py:853
  252.3 3.7 convert_add_fusion.1
  256.6 37.8 %back.1 = (f32[1024,1024]{1,0:T(8,128)}, f32[1024,1024]{1,0:T(8,128)}, f32[1024,1024]{1,0:T(8,128)}, bf16[1024,128]{1,0:T(8,128)(2,1)}) custom-call(s32[2]{0:T(128)} %pad_add_fusion.3.flag, f32[520,512]{1,0:T(8,128)} %get-tuple-element.137.mine_ref, bf16[528,512]{1,0:T(8,128)(2,1)} %collective-permute-done.15.came_ref, ...), custom_call_target="tpu_custom_call" | custom-call | flops 7516192768 | bytes 31457280 | tf_op jit(solution)/shard_map/back/pallas_call | solution.py:685
  300.5 10.3 %reduce-scatter.2.cloned.1.call-done = f32[128,1024]{1,0:T(8,128)} async-done(((f32[512,1024]{1,0:T(8,128)}), f32[128,1024]{1,0:T(8,128)}) %reduce-scatter.2.cloned.1.call-update) | async-done | bytes 524304 | tf_op jit(solution)/shard_map/reduce_scatter | solution.py:894
  315.5 30.8 %maps.1 = (bf16[1024,1024]{1,0:T(8,128)(2,1)}, f32[48,1024]{1,0:T(8,128)}) custom-call(s32[1]{0:T(128)} %bitcast.17.flag, f32[1024,1024]{1,0:T(8,128)} %get-tuple-element.144.qg_ref, f32[1024,1024]{1,0:T(8,128)} %get-tuple-element.145.kg_ref, f32[1024,1024]{1,0:T(8,128)} %get-tuple-element.146.vg_ref, bf16[1024,128]{1,0:T(8,128)(2,1)} %get-tuple-element.147.pre_ref.mine_ref, ...), custom_call_target="tpu_custom_call" | custom-call | flops 5368709120 | bytes 33554432 | tf_op jit(solution)/shard_map/maps/pallas_call | solution.py:834
  346.3 4.6 fusion.23
  356.1 4.8 multiply_reduce_fusion.1
  360.9 8.1 %collective-permute-done.20 = bf16[256,1024]{1,0:T(8,128)(2,1)S(1)} collective-permute-done((bf16[256,1024]{1,0:T(8,128)(2,1)S(1)}, bf16[256,1024]{1,0:T(8,128)(2,1)S(1)}, u32[]{:S(2)}, u32[]{:S(2)}) %collective-permute-start.20) | collective-permute-done | bytes 524320 | tf_op jit(solution)/shard_map/ppermute | solution.py:853
  378.0 2.5 collective-permute-start.22
  382.6 4.5 collective-permute-done.22
  390.6 4.5 convert_add_fusion
  399.1 4.4 multiply_reduce_fusion.2
  409.4 3.7 collective-permute-done.26
  414.1 3.5 collective-permute-done.31
  421.5 4.3 collective-permute-done.32
  427.9 3.2 convert_bitcast_fusion
  435.8 2.9 collective-permute-done.29
  438.7 2.8 reshape.101
  443.2 2.5 slice_bitcast_fusion.2
  450.7 4.3 collective-permute-done.36
  473.1 2.5 maximum_convert_fusion
  (221 shorter events, 108.4 us)
Async XLA Ops:
  7.2 90.3 %copy-start = (bf16[1024,1024]{1,0:T(8,128)(2,1)S(1)}, bf16[1024,1024]{1,0:T(8,128)(2,1)}, u32[]{:S(2)}) copy-start(bf16[1024,1024]{1,0:T(8,128)(2,1)} %param.21) | copy-start | bytes 6291460
  7.2 303.6 %reduce-scatter.2.cloned.1.call-start = ((), (), s32[]{:S(2)}) async-start(), calls=%async_computation.1 | async-start | bytes 2621440 | tf_op jit(solution)/shard_map/reduce_scatter | solution.py:894
  7.2 11.8 %collective-permute-start = (bf16[1024,512]{1,0:T(8,128)(2,1)}, bf16[1024,512]{1,0:T(8,128)(2,1)S(1)}, u32[]{:S(2)}, u32[]{:S(2)}) collective-permute-start(bf16[1024,512]{1,0:T(8,128)(2,1)} %own_ref.1), channel_id=1, source_target_pairs={{0,1},{1,0},{2,3},{3,2},{4,5},{5,4},{6,7},{7,6},{8,9},{9,8},{10,11... | collective-permute-start | bytes 3145736 | tf_op jit(solution)/shard_map/ppermute | solution.py:931
  8.5 7.4 %collective-permute-start.1 = (bf16[16,512]{1,0:T(8,128)(2,1)S(1)}, bf16[16,512]{1,0:T(8,128)(2,1)S(1)}, u32[]{:S(2)}, u32[]{:S(2)}) collective-permute-start(bf16[16,512]{1,0:T(8,128)(2,1)S(1)} %slice.57), channel_id=1, source_target_pairs={{0,4},{2,6},{4,8},{6,10},{8,12},{10,14},{12,16},{14,18},{16,20},{1... | collective-permute-start | bytes 49160 | tf_op jit(solution)/shard_map/ppermute | solution.py:938
  13.0 65.0 %collective-permute-start.6 = (bf16[1024,512]{1,0:T(8,128)(2,1)}, bf16[1024,512]{1,0:T(8,128)(2,1)}, u32[]{:S(2)}, u32[]{:S(2)}) collective-permute-start(bf16[1024,512]{1,0:T(8,128)(2,1)} %param.18), channel_id=1, source_target_pairs={{0,1},{1,0},{2,3},{3,2},{4,5},{5,4},{6,7},{7,6},{8,9},{9,8},{10,11... | collective-permute-start | bytes 3145736 | tf_op jit(solution)/shard_map/ppermute | solution.py:931
  16.0 3.0 collective-permute-start.2
  20.0 25.9 %copy-start.30 = (f32[8]{0:T(128)S(1)}, f32[8]{0:T(128)}, u32[]{:S(2)}) copy-start(f32[8]{0:T(128)} %param.28) | copy-start | bytes 100
  45.7 1.5 collective-permute-start.3
  57.9 14.6 %collective-permute-start.4 = (bf16[528,512]{1,0:T(8,128)(2,1)}, bf16[528,512]{1,0:T(8,128)(2,1)S(1)}, u32[]{:S(2)}, u32[]{:S(2)}) collective-permute-start(bf16[528,512]{1,0:T(8,128)(2,1)} %get-tuple-element.99), channel_id=1, source_target_pairs={{4,0},{6,2},{0,4},{2,6},{12,8},{14,10},{8,12},{10,14},{20,16},{22,... | collective-permute-start | bytes 1622024 | tf_op jit(solution)/shard_map/ppermute | solution.py:340
  76.4 13.7 %collective-permute-start.5 = (bf16[528,512]{1,0:T(8,128)(2,1)}, bf16[528,512]{1,0:T(8,128)(2,1)S(1)}, u32[]{:S(2)}, u32[]{:S(2)}) collective-permute-start(bf16[528,512]{1,0:T(8,128)(2,1)} %get-tuple-element.106), channel_id=1, source_target_pairs={{8,0},{10,2},{12,4},{14,6},{0,8},{2,10},{4,12},{6,14},{24,16},{26,... | collective-permute-start | bytes 1622024 | tf_op jit(solution)/shard_map/ppermute | solution.py:340
  94.8 25.4 %collective-permute-start.7 = (bf16[528,512]{1,0:T(8,128)(2,1)}, bf16[528,512]{1,0:T(8,128)(2,1)S(1)}, u32[]{:S(2)}, u32[]{:S(2)}) collective-permute-start(bf16[528,512]{1,0:T(8,128)(2,1)} %get-tuple-element.108), channel_id=1, source_target_pairs={{16,0},{18,2},{20,4},{22,6},{24,8},{26,10},{28,12},{30,14},{0,16},... | collective-permute-start | bytes 1622024 | tf_op jit(solution)/shard_map/ppermute | solution.py:340
  124.2 13.2 %collective-permute-start.8 = (bf16[528,512]{1,0:T(8,128)(2,1)}, bf16[528,512]{1,0:T(8,128)(2,1)S(1)}, u32[]{:S(2)}, u32[]{:S(2)}) collective-permute-start(bf16[528,512]{1,0:T(8,128)(2,1)} %get-tuple-element.114), channel_id=1, source_target_pairs={{4,0},{6,2},{0,4},{2,6},{12,8},{14,10},{8,12},{10,14},{20,16},{22,... | collective-permute-start | bytes 1622024 | tf_op jit(solution)/shard_map/ppermute | solution.py:340
  168.9 12.4 %collective-permute-start.9 = (bf16[528,512]{1,0:T(8,128)(2,1)}, bf16[528,512]{1,0:T(8,128)(2,1)}, u32[]{:S(2)}, u32[]{:S(2)}) collective-permute-start(bf16[528,512]{1,0:T(8,128)(2,1)} %get-tuple-element.121), channel_id=1, source_target_pairs={{4,0},{6,2},{0,4},{2,6},{12,8},{14,10},{8,12},{10,14},{20,16},{22,... | collective-permute-start | bytes 1622024 | tf_op jit(solution)/shard_map/ppermute | solution.py:340
  174.7 26.4 %collective-permute-start.14 = (bf16[512,1024]{1,0:T(8,128)(2,1)}, bf16[512,1024]{1,0:T(8,128)(2,1)}, u32[]{:S(2)}, u32[]{:S(2)}) collective-permute-start(bf16[512,1024]{1,0:T(8,128)(2,1)} %convolution_convert_fusion), channel_id=1, source_target_pairs={{2,0},{0,2},{6,4},{4,6},{10,8},{8,10},{14,12},{12,14},{18,16},{16,... | collective-permute-start | bytes 3145736 | tf_op jit(solution)/shard_map/ppermute | solution.py:853
  178.6 41.8 %collective-permute-start.13 = (bf16[512,1024]{1,0:T(8,128)(2,1)}, bf16[512,1024]{1,0:T(8,128)(2,1)}, u32[]{:S(2)}, u32[]{:S(2)}) collective-permute-start(bf16[512,1024]{1,0:T(8,128)(2,1)} %convolution_convert_fusion.1), channel_id=1, source_target_pairs={{2,0},{0,2},{6,4},{4,6},{10,8},{8,10},{14,12},{12,14},{18,16},{16,... | collective-permute-start | bytes 3145736 | tf_op jit(solution)/shard_map/ppermute | solution.py:853
  184.4 16.8 %copy-start.4 = (bf16[1024,1024]{1,0:T(8,128)(2,1)S(1)}, bf16[1024,1024]{1,0:T(8,128)(2,1)}, u32[]{:S(2)}) copy-start(bf16[1024,1024]{1,0:T(8,128)(2,1)} %get-tuple-element.123) | copy-start | bytes 6291460
  184.4 16.8 %copy-start.12 = (bf16[1024,1024]{1,0:T(8,128)(2,1)S(1)}, bf16[1024,1024]{1,0:T(8,128)(2,1)}, u32[]{:S(2)}) copy-start(bf16[1024,1024]{1,0:T(8,128)(2,1)} %get-tuple-element.109) | copy-start | bytes 6291460
  184.4 20.6 %collective-permute-start.10 = (bf16[528,512]{1,0:T(8,128)(2,1)}, bf16[528,512]{1,0:T(8,128)(2,1)S(1)}, u32[]{:S(2)}, u32[]{:S(2)}) collective-permute-start(bf16[528,512]{1,0:T(8,128)(2,1)} %get-tuple-element.125), channel_id=1, source_target_pairs={{8,0},{10,2},{12,4},{14,6},{0,8},{2,10},{4,12},{6,14},{24,16},{26,... | collective-permute-start | bytes 1622024 | tf_op jit(solution)/shard_map/ppermute | solution.py:340
  209.3 14.1 %copy-start.1 = (f32[512,1024]{1,0:T(8,128)S(1)}, f32[512,1024]{1,0:T(8,128)}, u32[]{:S(2)}) copy-start(f32[512,1024]{1,0:T(8,128)} %convert_add_fusion.2) | copy-start | bytes 6291460
  209.3 20.5 %collective-permute-start.12 = (bf16[528,512]{1,0:T(8,128)(2,1)}, bf16[528,512]{1,0:T(8,128)(2,1)}, u32[]{:S(2)}, u32[]{:S(2)}) collective-permute-start(bf16[528,512]{1,0:T(8,128)(2,1)} %get-tuple-element.129), channel_id=1, source_target_pairs={{16,0},{18,2},{20,4},{22,6},{24,8},{26,10},{28,12},{30,14},{0,16},... | collective-permute-start | bytes 1622024 | tf_op jit(solution)/shard_map/ppermute | solution.py:340
  229.9 22.4 %collective-permute-start.16 = (bf16[512,1024]{1,0:T(8,128)(2,1)S(1)}, bf16[512,1024]{1,0:T(8,128)(2,1)}, u32[]{:S(2)}, u32[]{:S(2)}) collective-permute-start(bf16[512,1024]{1,0:T(8,128)(2,1)S(1)} %fusion.4), channel_id=1, source_target_pairs={{8,0},{10,2},{12,4},{14,6},{0,8},{2,10},{4,12},{6,14},{24,16},{26,... | collective-permute-start | bytes 3145736 | tf_op jit(solution)/shard_map/ppermute | solution.py:853
  233.7 22.3 %collective-permute-start.15 = (bf16[528,512]{1,0:T(8,128)(2,1)}, bf16[528,512]{1,0:T(8,128)(2,1)}, u32[]{:S(2)}, u32[]{:S(2)}) collective-permute-start(bf16[528,512]{1,0:T(8,128)(2,1)} %get-tuple-element.134), channel_id=1, source_target_pairs={{4,0},{6,2},{0,4},{2,6},{12,8},{14,10},{8,12},{10,14},{20,16},{22,... | collective-permute-start | bytes 1622024 | tf_op jit(solution)/shard_map/ppermute | solution.py:340
  256.0 139.1 %all-gather.2.cloned.1.call-start = ((), (), s32[]{:S(2)}) async-start(), calls=%async_computation.2 | async-start | bytes 4456448 | tf_op jit(solution)/shard_map/all_gather | solution.py:1005
  256.6 37.9 %copy-start.26 = (bf16[3,1024,8]{1,2,0:T(8,128)(2,1)S(1)}, bf16[3,1024,8]{1,2,0:T(8,128)(2,1)}, u32[]{:S(2)}) copy-start(bf16[3,1024,8]{1,2,0:T(8,128)(2,1)} %param.27) | copy-start | bytes 147460
  256.6 37.9 %copy-start.31 = (s32[8]{0:T(128)S(1)}, s32[8]{0:T(128)}, u32[]{:S(2)}) copy-start(s32[8]{0:T(128)} %constant.216) | copy-start | bytes 100
  294.4 1.8 collective-permute-start.17
  299.2 13.4 %collective-permute-start.18 = (f32[8,1024]{1,0:T(8,128)}, f32[8,1024]{1,0:T(8,128)S(1)}, u32[]{:S(2)}, u32[]{:S(2)}) collective-permute-start(f32[8,1024]{1,0:T(8,128)} %edge.1), channel_id=1, source_target_pairs={{4,0},{6,2},{8,4},{10,6},{12,8},{14,10},{16,12},{18,14},{20,16},{2... | collective-permute-start | bytes 98312 | tf_op jit(solution)/shard_map/ppermute | solution.py:938
  351.3 17.7 %collective-permute-start.20 = (bf16[256,1024]{1,0:T(8,128)(2,1)S(1)}, bf16[256,1024]{1,0:T(8,128)(2,1)S(1)}, u32[]{:S(2)}, u32[]{:S(2)}) collective-permute-start(bf16[256,1024]{1,0:T(8,128)(2,1)S(1)} %dynamic-slice_convert_fusion), channel_id=1, source_target_pairs={{4,0},{6,2},{0,4},{2,6},{12,8},{14,10},{8,12},{10,14},{20,16},{22,... | collective-permute-start | bytes 1572872 | tf_op jit(solution)/shard_map/ppermute | solution.py:853
  352.2 18.5 %collective-permute-start.19 = (bf16[256,1024]{1,0:T(8,128)(2,1)S(1)}, bf16[256,1024]{1,0:T(8,128)(2,1)S(1)}, u32[]{:S(2)}, u32[]{:S(2)}) collective-permute-start(bf16[256,1024]{1,0:T(8,128)(2,1)S(1)} %dynamic-slice_convert_fusion.1), channel_id=1, source_target_pairs={{2,0},{0,2},{6,4},{4,6},{10,8},{8,10},{14,12},{12,14},{18,16},{16,... | collective-permute-start | bytes 1572872 | tf_op jit(solution)/shard_map/ppermute | solution.py:853
  373.3 17.2 %collective-permute-start.23 = (f32[1024,512]{1,0:T(8,128)}, f32[1024,512]{1,0:T(8,128)}, u32[]{:S(2)}, u32[]{:S(2)}) collective-permute-start(f32[1024,512]{1,0:T(8,128)} %constant_dynamic-slice_fusion), channel_id=1, source_target_pairs={{0,1},{1,0},{2,3},{3,2},{4,5},{5,4},{6,7},{7,6},{8,9},{9,8},{10,11... | collective-permute-start | bytes 6291464 | tf_op jit(solution)/shard_map/ppermute | solution.py:931
  376.3 14.3 %copy-start.8 = (bf16[1024,512]{1,0:T(8,128)(2,1)S(1)}, bf16[1024,512]{1,0:T(8,128)(2,1)}, u32[]{:S(2)}) copy-start(bf16[1024,512]{1,0:T(8,128)(2,1)} %param.18) | copy-start | bytes 3145732
  376.3 22.8 %collective-permute-start.11 = (f32[1024,512]{1,0:T(8,128)}, f32[1024,512]{1,0:T(8,128)}, u32[]{:S(2)}, u32[]{:S(2)}) collective-permute-start(f32[1024,512]{1,0:T(8,128)} %constant_dynamic-slice_fusion.1), channel_id=1, source_target_pairs={{0,1},{1,0},{2,3},{3,2},{4,5},{5,4},{6,7},{7,6},{8,9},{9,8},{10,11... | collective-permute-start | bytes 6291464 | tf_op jit(solution)/shard_map/ppermute | solution.py:931
  376.4 6.2 %collective-permute-start.24 = (f32[2,1024]{1,0:T(2,128)S(1)}, f32[2,1024]{1,0:T(2,128)S(1)}, u32[]{:S(2)}, u32[]{:S(2)}) collective-permute-start(f32[2,1024]{1,0:T(2,128)S(1)} %pad_maximum_fusion.10), channel_id=1, source_target_pairs={{0,1},{1,0},{2,3},{3,2},{4,5},{5,4},{6,7},{7,6},{8,9},{9,8},{10,11... | collective-permute-start | bytes 24584 | tf_op jit(solution)/shard_map/ppermute | solution.py:931
  378.0 9.1 %collective-permute-start.22 = (bf16[128,1024]{1,0:T(8,128)(2,1)S(1)}, bf16[128,1024]{1,0:T(8,128)(2,1)S(1)}, u32[]{:S(2)}, u32[]{:S(2)}) collective-permute-start(bf16[128,1024]{1,0:T(8,128)(2,1)S(1)} %dynamic-slice_convert_fusion.3), channel_id=1, source_target_pairs={{2,0},{0,2},{6,4},{4,6},{10,8},{8,10},{14,12},{12,14},{18,16},{16,... | collective-permute-start | bytes 786440 | tf_op jit(solution)/shard_map/ppermute | solution.py:853
  381.6 8.1 %collective-permute-start.21 = (bf16[128,1024]{1,0:T(8,128)(2,1)S(1)}, bf16[128,1024]{1,0:T(8,128)(2,1)S(1)}, u32[]{:S(2)}, u32[]{:S(2)}) collective-permute-start(bf16[128,1024]{1,0:T(8,128)(2,1)S(1)} %dynamic-slice_convert_fusion.4), channel_id=1, source_target_pairs={{4,0},{6,2},{0,4},{2,6},{12,8},{14,10},{8,12},{10,14},{20,16},{22,... | collective-permute-start | bytes 786440 | tf_op jit(solution)/shard_map/ppermute | solution.py:853
  399.0 8.2 %collective-permute-start.30 = (bf16[128,1024]{1,0:T(8,128)(2,1)}, bf16[128,1024]{1,0:T(8,128)(2,1)}, u32[]{:S(2)}, u32[]{:S(2)}) collective-permute-start(bf16[128,1024]{1,0:T(8,128)(2,1)} %dynamic-slice_convert_fusion.2), channel_id=1, source_target_pairs={{8,0},{10,2},{12,4},{14,6},{0,8},{2,10},{4,12},{6,14},{24,16},{26,... | collective-permute-start | bytes 786440 | tf_op jit(solution)/shard_map/ppermute | solution.py:853
  403.5 1.2 collective-permute-start.25
  406.0 7.1 %collective-permute-start.26 = (f32[48,1024]{1,0:T(8,128)S(1)}, f32[48,1024]{1,0:T(8,128)S(1)}, u32[]{:S(2)}, u32[]{:S(2)}) collective-permute-start(f32[48,1024]{1,0:T(8,128)S(1)} %pad_add_fusion), channel_id=1, source_target_pairs={{2,0},{0,2},{6,4},{4,6},{10,8},{8,10},{14,12},{12,14},{18,16},{16,... | collective-permute-start | bytes 589832 | tf_op jit(solution)/shard_map/ppermute | solution.py:853
  408.4 9.1 %collective-permute-start.31 = (bf16[64,1024]{1,0:T(8,128)(2,1)S(1)}, bf16[64,1024]{1,0:T(8,128)(2,1)S(1)}, u32[]{:S(2)}, u32[]{:S(2)}) collective-permute-start(bf16[64,1024]{1,0:T(8,128)(2,1)S(1)} %dynamic-slice_convert_fusion.5), channel_id=1, source_target_pairs={{16,0},{18,2},{20,4},{22,6},{24,8},{26,10},{28,12},{30,14},{0,16},... | collective-permute-start | bytes 393224 | tf_op jit(solution)/shard_map/ppermute | solution.py:853
  413.2 6.3 %collective-permute-start.27 = (f32[48,1024]{1,0:T(8,128)S(1)}, f32[48,1024]{1,0:T(8,128)S(1)}, u32[]{:S(2)}, u32[]{:S(2)}) collective-permute-start(f32[48,1024]{1,0:T(8,128)S(1)} %fusion.38), channel_id=1, source_target_pairs={{4,0},{6,2},{0,4},{2,6},{12,8},{14,10},{8,12},{10,14},{20,16},{22,... | collective-permute-start | bytes 589832 | tf_op jit(solution)/shard_map/ppermute | solution.py:853
  417.6 8.2 %collective-permute-start.32 = (bf16[64,1024]{1,0:T(8,128)(2,1)S(1)}, bf16[64,1024]{1,0:T(8,128)(2,1)S(1)}, u32[]{:S(2)}, u32[]{:S(2)}) collective-permute-start(bf16[64,1024]{1,0:T(8,128)(2,1)S(1)} %add_convert_fusion), channel_id=1, source_target_pairs={{16,0},{18,2},{20,4},{22,6},{24,8},{26,10},{28,12},{30,14},{0,16},... | collective-permute-start | bytes 393224 | tf_op jit(solution)/shard_map/ppermute | solution.py:853
  419.5 8.3 %collective-permute-start.28 = (f32[48,1024]{1,0:T(8,128)S(1)}, f32[48,1024]{1,0:T(8,128)S(1)}, u32[]{:S(2)}, u32[]{:S(2)}) collective-permute-start(f32[48,1024]{1,0:T(8,128)S(1)} %add.239), channel_id=1, source_target_pairs={{8,0},{10,2},{12,4},{14,6},{0,8},{2,10},{4,12},{6,14},{24,16},{26,... | collective-permute-start | bytes 589832 | tf_op jit(solution)/shard_map/ppermute | solution.py:853
  425.8 16.3 %collective-permute-start.33 = (bf16[128,1024]{1,0:T(8,128)(2,1)S(1)}, bf16[128,1024]{1,0:T(8,128)(2,1)S(1)}, u32[]{:S(2)}, u32[]{:S(2)}) collective-permute-start(bf16[128,1024]{1,0:T(8,128)(2,1)S(1)} %pad_maximum_fusion.8), channel_id=1, source_target_pairs={{8,0},{10,2},{12,4},{14,6},{0,8},{2,10},{4,12},{6,14},{24,16},{26,... | collective-permute-start | bytes 786440 | tf_op jit(solution)/shard_map/ppermute | solution.py:853
  427.8 10.8 %collective-permute-start.29 = (f32[48,1024]{1,0:T(8,128)S(1)}, f32[48,1024]{1,0:T(8,128)S(1)}, u32[]{:S(2)}, u32[]{:S(2)}) collective-permute-start(f32[48,1024]{1,0:T(8,128)S(1)} %add.240), channel_id=1, source_target_pairs={{16,0},{18,2},{20,4},{22,6},{24,8},{26,10},{28,12},{30,14},{0,16},... | collective-permute-start | bytes 589832 | tf_op jit(solution)/shard_map/ppermute | solution.py:853
  442.3 6.4 %collective-permute-start.34 = (bf16[128,1024]{1,0:T(8,128)(2,1)S(1)}, bf16[128,1024]{1,0:T(8,128)(2,1)S(1)}, u32[]{:S(2)}, u32[]{:S(2)}) collective-permute-start(bf16[128,1024]{1,0:T(8,128)(2,1)S(1)} %get-tuple-element.210), channel_id=1, source_target_pairs={{4,0},{6,2},{0,4},{2,6},{12,8},{14,10},{8,12},{10,14},{20,16},{22,... | collective-permute-start | bytes 786440 | tf_op jit(solution)/shard_map/ppermute | solution.py:853
  445.7 9.2 %collective-permute-start.36 = (bf16[128,1024]{1,0:T(8,128)(2,1)S(1)}, bf16[128,1024]{1,0:T(8,128)(2,1)S(1)}, u32[]{:S(2)}, u32[]{:S(2)}) collective-permute-start(bf16[128,1024]{1,0:T(8,128)(2,1)S(1)} %get-tuple-element.211), channel_id=1, source_target_pairs={{2,0},{0,2},{6,4},{4,6},{10,8},{8,10},{14,12},{12,14},{18,16},{16,... | collective-permute-start | bytes 786440 | tf_op jit(solution)/shard_map/ppermute | solution.py:853
  449.6 20.9 %collective-permute-start.35 = (bf16[256,1024]{1,0:T(8,128)(2,1)}, bf16[256,1024]{1,0:T(8,128)(2,1)}, u32[]{:S(2)}, u32[]{:S(2)}) collective-permute-start(bf16[256,1024]{1,0:T(8,128)(2,1)} %pad_maximum_fusion.6), channel_id=1, source_target_pairs={{2,0},{0,2},{6,4},{4,6},{10,8},{8,10},{14,12},{12,14},{18,16},{16,... | collective-permute-start | bytes 1572872 | tf_op jit(solution)/shard_map/ppermute | solution.py:853
  455.8 16.0 %collective-permute-start.37 = (bf16[256,1024]{1,0:T(8,128)(2,1)}, bf16[256,1024]{1,0:T(8,128)(2,1)}, u32[]{:S(2)}, u32[]{:S(2)}) collective-permute-start(bf16[256,1024]{1,0:T(8,128)(2,1)} %pad_maximum_fusion.7), channel_id=1, source_target_pairs={{4,0},{6,2},{0,4},{2,6},{12,8},{14,10},{8,12},{10,14},{20,16},{22,... | collective-permute-start | bytes 1572872 | tf_op jit(solution)/shard_map/ppermute | solution.py:853
  (30 other events, 106.5 us)
Sparse Core Ops, SparseCore 0:
  256.1 54.6 reduce-scatter.1
  314.0 78.5 all-gather.1

commit v3 on v2

--- a/solution.py
+++ b/solution.py
@@ -18,6 +18,8 @@
 WIDE = DH + 8
 SMALL = 48
 LIMIT = 60
+FORTH = 2
+BACK = 1
 STRIP = 256
 UNROLL = 4
 
@@ -242,7 +244,7 @@
         in_specs=[smem, whole(8, count), whole(8, count), whole(8, 1)],
         out_specs=[whole(count // BLOCK, 8, BLOCK), whole(count, LANES), whole(8, DH)],
         out_shape=[shape_of(count // BLOCK, 8, BLOCK), shape_of(count, LANES), shape_of(8, DH)],
-        compiler_params=params(LIMIT),
+        compiler_params=params(24),
         cost_estimate=cost(count * 1000, count * 600),
         name="gates",
     )(place, own, other, bias)
@@ -252,14 +254,16 @@
     ref[0:DH, :] = state.astype(bf16)
     terms = split3(vector) + split3(log_decay)
     tail = jnp.concatenate(
-        [t.astype(f32) for t in terms] + [jnp.zeros((PACK - DH - 6, DH), f32)], axis=0
+        [t.astype(f32) for t in terms] + [jnp.zeros((PACK - DH - 6, vector.shape[1]), f32)], axis=0
     )
     ref[DH:PACK, :] = tail.astype(bf16)
 
 
 def write_wide(ref, state, vector, log_decay):
     ref[0:DH, :] = state
-    ref[DH:WIDE, :] = jnp.concatenate([vector, log_decay, jnp.zeros((WIDE - DH - 2, DH), f32)], axis=0)
+    ref[DH:WIDE, :] = jnp.concatenate(
+        [vector, log_decay, jnp.zeros((WIDE - DH - 2, vector.shape[1]), f32)], axis=0
+    )
 
 
 def read_pack(ref):
@@ -311,22 +315,31 @@
     write_wide(mine_ref, *chosen(is_lead, found, after))
 
 
-def pack_spec(wide):
-    return whole(WIDE if wide else PACK, DH)
-
-
-def pack_shape(wide):
-    return shape_of(WIDE if wide else PACK, DH, dtype=f32 if wide else bf16)
+def pack_spec(wide, streams):
+    return whole(WIDE if wide else PACK, DH // streams)
+
+
+def pack_shape(wide, streams):
+    return shape_of(WIDE if wide else PACK, DH // streams, dtype=f32 if wide else bf16)
+
+
+def pack_specs(streams):
+    return [pack_spec(1, streams)] * streams + [pack_spec(0, streams)] * streams
+
+
+def pack_shapes(streams):
+    return [pack_shape(1, streams)] * streams + [pack_shape(0, streams)] * streams
 
 
 def small_call(kernel, name, ins, outs, flag, *packs):
+    streams = DH // packs[0].shape[1]
     return pl.pallas_call(
         kernel,
         grid=(1,),
-        in_specs=[smem] + [pack_spec(w) for w in ins],
-        out_specs=[pack_spec(w) for w in outs],
-        out_shape=[pack_shape(w) for w in outs],
-        compiler_params=params(LIMIT),
+        in_specs=[smem] + [pack_spec(w, streams) for w in ins],
+        out_specs=[pack_spec(w, streams) for w in outs],
+        out_shape=[pack_shape(w, streams) for w in outs],
+        compiler_params=params(24),
         cost_estimate=cost(PACK * DH * 8, PACK * DH * 3 * (len(ins) + len(outs))),
         name=name,
     )(flag, *packs)
@@ -343,36 +356,59 @@
         return jnp.stack([jnp.asarray(v).astype(jnp.int32) for v in values])
 
     is_lead = place % 2 == 0
-    got = swap(send, 1)
+    streams = range(len(own))
     done = []
-    got, filler = lax.optimization_barrier((got, fillers[0]))
-    done.append(filler)
-    out, total, lead = small_call(pair_kernel, "pair", (1, 0), (0, 1, 1), as_flag(is_lead), own, got)
-    before = jnp.zeros_like(own)
+
+    def exchange(packs, bit):
+        got = [swap(pack, bit) for pack in packs]
+        if bit < span and len(done) < len(fillers):
+            got[-1], filler = lax.optimization_barrier((got[-1], fillers[len(done)]))
+            done.append(filler)
+        return got
+
+    got = exchange(send, 1)
+    found = [
+        small_call(pair_kernel, "pair", (1, 0), (0, 1, 1), as_flag(is_lead), own[n], got[n]) for n in streams
+    ]
+    out, total, lead = zip(*found)
+    before = [jnp.zeros_like(pack) for pack in own]
     bit = 2
     while bit < span:
-        got = swap(out, bit)
-        got, filler = lax.optimization_barrier((got, fillers[min(len(done), len(fillers) - 1)]))
-        done.append(filler)
+        got = exchange(out, bit)
         upper = (place // bit) % 2 == 1
         if bit * 2 < span:
-            out, total, before = small_call(
-                step_kernel, "step", (1, 0, 1), (0, 1, 1), as_flag(upper), total, got, before
-            )
+            found = [
+                small_call(
+                    step_kernel, "step", (1, 0, 1), (0, 1, 1), as_flag(upper), total[n], got[n], before[n]
+                )
+                for n in streams
+            ]
+            out, total, before = zip(*found)
         bit *= 2
-    out, mine = small_call(last_kernel, "last", (0, 1, 1), (0, 1), as_flag(upper, is_lead), got, before, lead)
-    return mine, swap(out, 1), done
-
-
-def put_states(flag, mine_ref, came_ref, state_ref, vec_ref):
-    mine, came = read_wide(mine_ref), read_pack(came_ref)
-    for h in range(2):
-        found = chosen((flag[0] == 1) == (h == 0), mine, came)
-        state_ref[h] = found[0]
-        vec_ref[h : h + 1, :] = found[1]
-
-
-def ends_kernel(flag, k_ref, v_ref, col_ref, total_ref, own_ref, send_ref, state_ref, vec_ref):
+    found = [
+        small_call(
+            last_kernel, "last", (0, 1, 1), (0, 1), as_flag(upper, is_lead), got[n], before[n], lead[n]
+        )
+        for n in streams
+    ]
+    out, mine = zip(*found)
+    return mine + tuple(swap(pack, 1) for pack in out), done
+
+
+def put_states(flag, packs, state_ref, vec_ref):
+    streams = len(packs) // 2
+    size = DH // streams
+    for n in range(streams):
+        mine, came = read_wide(packs[n]), read_pack(packs[streams + n])
+        part = slice(n * size, (n + 1) * size)
+        for h in range(2):
+            found = chosen((flag[0] == 1) == (h == 0), mine, came)
+            state_ref[h, :, part] = found[0]
+            vec_ref[h : h + 1, part] = found[1]
+
+
+def ends_kernel(flag, k_ref, v_ref, col_ref, total_ref, *refs):
+    packs, (state_ref, vec_ref) = refs[: 2 * FORTH], refs[2 * FORTH :]
     step = pl.program_id(0)
 
     @pl.when(step == 0)
@@ -394,20 +430,24 @@
 
     @pl.when(step == pl.num_programs(0) - 1)
     def _():
-        write_two(flag, state_ref, vec_ref, total_ref, own_ref, send_ref)
-
-
-def write_two(flag, state_ref, vec_ref, total_ref, own_ref, send_ref):
-    for h in range(2):
-        found = (state_ref[h], vec_ref[h : h + 1, :], total_ref[h : h + 1, :])
-
-        @pl.when(flag[0] == 1 - h)
-        def _():
-            write_wide(own_ref, *found)
-
-        @pl.when(flag[0] == h)
-        def _():
-            write_pack(send_ref, *found)
+        write_two(flag, state_ref, vec_ref, total_ref, packs)
+
+
+def write_two(flag, state_ref, vec_ref, total_ref, packs):
+    streams = len(packs) // 2
+    size = DH // streams
+    for n in range(streams):
+        part = slice(n * size, (n + 1) * size)
+        for h in range(2):
+            found = (state_ref[h, :, part], vec_ref[h : h + 1, part], total_ref[h : h + 1, part])
+
+            @pl.when(flag[0] == 1 - h)
+            def _():
+                write_wide(packs[n], *found)
+
+            @pl.when(flag[0] == h)
+            def _():
+                write_pack(packs[streams + n], *found)
 
 
 def ends_stage(flag, k, v, col, total):
@@ -416,8 +456,8 @@
         ends_kernel,
         grid=(count // TILE,),
         in_specs=[smem, rows(chan), rows(chan), rows(LANES), whole(8, DH)],
-        out_specs=[pack_spec(1), pack_spec(0)],
-        out_shape=[pack_shape(1), pack_shape(0)],
+        out_specs=pack_specs(FORTH),
+        out_shape=pack_shapes(FORTH),
         scratch_shapes=[pltpu.VMEM((2, DH, DH), f32), pltpu.VMEM((8, DH), f32)],
         compiler_params=params(LIMIT),
         cost_estimate=cost(4 * count * chan * DH, count * chan * 4),
@@ -470,24 +510,26 @@
                   pl.BlockSpec((TILE // BLOCK, 8, BLOCK), lambda i: (i, 0, 0))],
         out_specs=[rows(chan), rows(LANES)],
         out_shape=[shape_of(count, chan), shape_of(count, LANES)],
-        compiler_params=params(LIMIT),
+        compiler_params=params(32),
         cost_estimate=cost(4 * count * chan * BLOCK, count * chan * 10),
         name="inside",
     )(q, k, v, col, row)
 
 
-def middle_kernel(
-    flag, mine_ref, came_ref, q_ref, k_ref, v_ref, inside_ref, norm_ref, col_ref, gate_ref, dgated_ref,
-    active_ref, group_ref, skip_ref, total_ref,
-    gated_ref, gig_ref, sgrad_ref, nlow_ref, clow_ref, start_ref, nvec_ref, stat_ref, ggroup_ref, gskip_ref,
-    own_ref, send_ref,
-    state_ref, vec_ref, back_ref, bvec_ref, cross_ref, ncross_ref,
-):
+def middle_kernel(flag, *refs):
+    states, refs = refs[: 2 * FORTH], refs[2 * FORTH :]
+    (
+        q_ref, k_ref, v_ref, inside_ref, norm_ref, col_ref, gate_ref, dgated_ref, active_ref, group_ref,
+        skip_ref, total_ref,
+        gated_ref, gig_ref, sgrad_ref, nlow_ref, clow_ref, start_ref, nvec_ref, stat_ref, ggroup_ref, gskip_ref,
+    ) = refs[:22]
+    packs = refs[22 : 22 + 2 * BACK]
+    state_ref, vec_ref, back_ref, bvec_ref, cross_ref, ncross_ref = refs[22 + 2 * BACK :]
     step = pl.program_id(0)
 
     @pl.when(step == 0)
     def _():
-        put_states(flag, mine_ref, came_ref, state_ref, vec_ref)
+        put_states(flag, states, state_ref, vec_ref)
         back_ref[...] = jnp.zeros_like(back_ref)
         bvec_ref[...] = jnp.zeros_like(bvec_ref)
         ggroup_ref[...] = jnp.zeros_like(ggroup_ref)
@@ -572,47 +614,48 @@
 
     @pl.when(step == pl.num_programs(0) - 1)
     def _():
-        write_two(flag, back_ref, bvec_ref, total_ref, own_ref, send_ref)
-
-
-def middle_stage(flag, mine, came, q, k, v, inside, norms, col, gate, dgated, active, group, skip, total):
+        write_two(flag, back_ref, bvec_ref, total_ref, packs)
+
+
+def middle_stage(flag, states, q, k, v, inside, norms, col, gate, dgated, active, group, skip, total):
     count, chan = q.shape
     blocks = count // BLOCK
     per = TILE // BLOCK
     return pl.pallas_call(
         middle_kernel,
         grid=(count // TILE,),
-        in_specs=[smem, pack_spec(1), pack_spec(0), rows(chan), rows(chan), rows(chan), rows(chan), rows(LANES), rows(LANES),
-                  rows(chan), rows(chan), rows(chan), whole(1, chan), whole(1, chan), whole(8, DH)],
+        in_specs=[smem, *pack_specs(FORTH), rows(chan), rows(chan), rows(chan),
+                  rows(chan), rows(LANES), rows(LANES), rows(chan), rows(chan), rows(chan), whole(1, chan), whole(1, chan), whole(8, DH)],
         out_specs=[rows(chan), rows(chan), rows(chan), rows(chan), rows(chan),
                    pl.BlockSpec((2, per, DH, DH), lambda i: (0, i, 0, 0)),
                    pl.BlockSpec((per, 8, DH), lambda i: (i, 0, 0)),
-                   rows(LANES), whole(8, chan), whole(8, chan), pack_spec(1), pack_spec(0)],
+                   rows(LANES), whole(8, chan), whole(8, chan), *pack_specs(BACK)],
         out_shape=[shape_of(count, chan, dtype=bf16), shape_of(count, chan, dtype=bf16), shape_of(count, chan),
                    shape_of(count, chan, dtype=bf16), shape_of(count, chan, dtype=bf16),
                    shape_of(2, blocks, DH, DH, dtype=bf16), shape_of(blocks, 8, DH), shape_of(count, LANES),
                    shape_of(8, chan), shape_of(8, chan),
-                   pack_shape(1), pack_shape(0)],
+                   *pack_shapes(BACK)],
         scratch_shapes=[pltpu.VMEM((2, DH, DH), f32), pltpu.VMEM((8, DH), f32),
                         pltpu.VMEM((2, DH, DH), f32), pltpu.VMEM((8, DH), f32),
                         pltpu.VMEM((TILE, chan), f32), pltpu.VMEM((TILE, LANES), f32)],
         compiler_params=params(LIMIT),
         cost_estimate=cost(10 * count * chan * DH, count * chan * 40),
         name="middle",
-    )(flag, mine, came, q, k, v, inside, norms, col, gate, dgated, active, group, skip, total)
-
-
-def back_kernel(
-    flag, mine_ref, came_ref, q_ref, k_ref, v_ref, nlow_ref, clow_ref, start_ref, nvec_ref, col_ref, row_ref,
-    stat_ref,
-    qg_ref, kg_ref, vg_ref, pre_ref,
-    state_ref, vec_ref,
-):
+    )(flag, *states, q, k, v, inside, norms, col, gate, dgated, active, group, skip, total)
+
+
+def back_kernel(flag, *refs):
+    states, refs = refs[: 2 * BACK], refs[2 * BACK :]
+    (
+        q_ref, k_ref, v_ref, nlow_ref, clow_ref, start_ref, nvec_ref, col_ref, row_ref, stat_ref,
+        qg_ref, kg_ref, vg_ref, pre_ref,
+        state_ref, vec_ref,
+    ) = refs
     scale = DH ** (-0.5)
 
     @pl.when(pl.program_id(0) == 0)
     def _():
-        put_states(flag, mine_ref, came_ref, state_ref, vec_ref)
+        put_states(flag, states, state_ref, vec_ref)
 
     u = lax.broadcasted_iota(jnp.int32, (BLOCK, BLOCK), 0)
     t = lax.broadcasted_iota(jnp.int32, (BLOCK, BLOCK), 1)
@@ -676,7 +719,7 @@
     lax.fori_loop(0, per, body, 0, unroll=2)
 
 
-def back_stage(flag, mine, came, q, k, v, nlow, clow, start, nvec, col, row, stat):
+def back_stage(flag, states, q, k, v, nlow, clow, start, nvec, col, row, stat):
     count, chan = q.shape
     tiles = count // TILE
     per = TILE // BLOCK
@@ -685,7 +728,7 @@
     return pl.pallas_call(
         back_kernel,
         grid=(tiles,),
-        in_specs=[smem, pack_spec(1), pack_spec(0), flip, flip, flip, flip, flip,
+        in_specs=[smem, *pack_specs(BACK), flip, flip, flip, flip, flip,
                   pl.BlockSpec((2, per, DH, DH), lambda i: (0, tiles - 1 - i, 0, 0)),
                   pl.BlockSpec((per, 8, DH), lambda i: (tiles - 1 - i, 0, 0)), thin,
                   pl.BlockSpec((per, 8, BLOCK), lambda i: (tiles - 1 - i, 0, 0)), thin],
@@ -695,7 +738,7 @@
         compiler_params=params(LIMIT),
         cost_estimate=cost(14 * count * chan * DH, count * chan * 30),
         name="back",
-    )(flag, mine, came, q, k, v, nlow, clow, start, nvec, col, row, stat)
+    )(flag, *states, q, k, v, nlow, clow, start, nvec, col, row, stat)
 
 
 def band_back(value, map_hi, map_lo):
@@ -959,18 +1002,18 @@
     )
     row, col, total = gates_stage(flags(t_place), pre, across(pre), gate_bias[:, None])
     even = flags(piece % 2 == 0)
-    own, send = ends_stage(even, k, v, col, total)
+    packs = ends_stage(even, k, v, col, total)
     gate_in = mm(normed, up_gate)
     dgated = mm_nt(full_cot, down_weight)
     inside, norms = inside_stage(q, k, v, col, row)
-    mine, came, done = pass_states(
-        own, send, piece, span, stride, ((inside, norms), (dgated,), (gate_in,))
+    states, done = pass_states(
+        packs[:FORTH], packs[FORTH:], piece, span, stride, ((inside, norms), (dgated,), (gate_in,))
     )
     (inside, norms), (dgated,), (gate_in,) = done
     (
-        gated, gate_in_grad, sgrad, nlow, clow, start, nvec, stat, ggroup, gskip, own, send
+        gated, gate_in_grad, sgrad, nlow, clow, start, nvec, stat, ggroup, gskip, *packs
     ) = middle_stage(
-        even, mine, came, q, k, v, inside, norms, col, gate_in, dgated, active, group_weight[None],
+        even, states, q, k, v, inside, norms, col, gate_in, dgated, active, group_weight[None],
         skip_weight[None], total,
     )
     pairs = ((gated, full_cot), (normed, gate_in_grad))
@@ -983,11 +1026,12 @@
     branch = mm(gated, down_weight)
     second = (lax.axis_index("dp") // 4) % 2
     away = lax.dynamic_slice_in_dim(both, (1 - second) * (model // 2), model // 2, axis=0).astype(bf16)
-    mine, came, done = pass_states(own, send, span - 1 - piece, span, stride, (sends, (branch,), (both, away)))
+    states, done = pass_states(
+        packs[:BACK], packs[BACK:], span - 1 - piece, span, stride, (sends, (branch,), (both, away)))
     _, (branch,), (both, away) = done
     both = lax.dynamic_slice_in_dim(both, second * (model // 2), model // 2, axis=0)
     both = both + exchanged(away, 4).astype(f32)
-    mine, came, both = lax.optimization_barrier((mine, came, both))
+    states, both = lax.optimization_barrier((states, both))
     share = shares(both)
 
     bits = [1 << n for n in range(devices.bit_length() - 1)]
@@ -997,7 +1041,7 @@
     squares = jnp.sum(result * result)
     gate_part = mm_nt(gate_in_grad, up_gate)
 
-    qg, kg, vg, pre_own = back_stage(flags(piece % 2 == 0, t_place), mine, came, q, k, v, nlow, clow, start, nvec, col, row, stat)
+    qg, kg, vg, pre_own = back_stage(flags(piece % 2 == 0, t_place), states, q, k, v, nlow, clow, start, nvec, col, row, stat)
     pre_other = across(pre_own)
     skip = skip_weight[None]
     edge = along(edge_stage(qg, kg, pre_own, pre_other, sgrad, conv, skip, coefs, gwt), -stride)

time: 492 us -> 470 us (0.955)
  Pallas kernels: 168 us -> 151 us
  waiting for transfers between devices: 128 us -> 116 us
  local copies, waits for them, and re-layouts: 48.7 us -> 58 us
    ppermute x8 -> x12, waiting for transfers between devices: 41.9 us -> 25.8 us  [swap(): return lax.ppermute(value, 'dp', route)]
    pallas_call x8 -> x11, Pallas kernels: 88.1 us -> 75.6 us  [the longest x1 37.8 us: back_stage(): pl.pallas_call(back_kernel, grid=(tiles,), in_specs=[smem, *pack_specs(BA...]
    unnamed x83 -> x125, local copies, waits for them, and re-layouts: 18.4 us -> 29.3 us
    ppermute x19, waiting for transfers between devices: 73.6 us -> 78.9 us  [exchanged(): return lax.ppermute(value, 'dp', route)]
    ppermute x8 -> x12, starting transfers between devices: 12.9 us -> 12.7 us  [swap(): return lax.ppermute(value, 'dp', route)]
  transfers between devices with their start and end apart: 40 -> 44, of which waited for: 24 -> 25; matrix products, arithmetic and copies ran while one was open for 25% -> 25% of each run, Pallas kernels for 27% -> 26%
where the time goes in v3:
time: 470 us; the launch traced here: 462 us
  Pallas kernels  151 us (32%)
  waiting for transfers between devices  116 us (25%)
  local copies, waits for them, and re-layouts  58 us (12%)
  other arithmetic  42 us (9%)
  matrix products  39.1 us (8%)
  starting transfers between devices  37.6 us (8%)
  between operations  18.1 us (4%)
    ppermute x19, waiting for transfers between devices, exchanged(): return lax.ppermute(value, 'dp', route)  78.9 us
    pallas_call x1, Pallas kernels, back_stage(): pl.pallas_call(back_kernel, grid=(tiles,), in_specs=[smem, *pack_specs(BA...  37.8 us
    pallas_call x1, Pallas kernels, maps_stage(): pl.pallas_call(maps_kernel, grid=(tiles,), in_specs=[smem, flip, flip, fl...  30.8 us
    pallas_call x1, Pallas kernels, middle_stage(): pl.pallas_call(middle_kernel, grid=(count // TILE,), in_specs=[smem, *pac...  30.7 us
    unnamed x125, local copies, waits for them, and re-layouts  29.3 us
    ppermute x12, waiting for transfers between devices, swap(): return lax.ppermute(value, 'dp', route)  25.8 us
    pallas_call x1, Pallas kernels, first_stage(): pl.pallas_call(first_kernel, grid=(count // TILE,), in_specs=[smem, rows(...  25.7 us
    ppermute x19, starting transfers between devices, exchanged(): return lax.ppermute(value, 'dp', route)  17.3 us
  transfers between devices with their start and end apart: 44, of which 25 were waited for; matrix products, arithmetic and copies ran while one was open for 25% of the time, Pallas kernels for 26%

profile of v3, /device:TPU:0, one launch (start us, length us, event | category | flops | bytes accessed | tf_op | source)
XLA Modules:
  0.0 461.6 jit_solution(17646859020261777506)
XLA Ops:
  8.5 4.5 collective-permute-start.1
  17.0 1.9 copy.40.gate_ref
  20.0 25.7 %first.1 = (bf16[1024,1024]{1,0:T(8,128)(2,1)}, f32[1024,1024]{1,0:T(8,128)}, f32[1024,1024]{1,0:T(8,128)}, f32[1024,1024]{1,0:T(8,128)}, bf16[1024,1024]{1,0:T(...) custom-call(s32[2]{0:T(128)} %pad_add_fusion.2.flag, ...), custom_call_target="tpu_custom_call" | custom-call | flops 8589934592 | bytes 20971520 | tf_op jit(solution)/shard_map/first/pallas_call | solution.py:173
  50.7 7.2 %ends.1 = (f32[520,256]{1,0:T(8,128)}, f32[520,256]{1,0:T(8,128)}, bf16[528,256]{1,0:T(8,128)(2,1)}, bf16[528,256]{1,0:T(8,128)(2,1)}) custom-call(s32[1]{0:T(128)} %bitcast.1.flag, bf16[1024,1024]{1,0:T(8,128)(2,1)} %get-tuple-element.102.k_ref.refs_5_.refs_3_, bf16[1024,1024]{1,0:T(8,128)(2,1)} %get-tuple-element.103.v_ref.refs_6_.refs_4_, ...), custom_call_target="tpu_custom_call" | custom-call | flops 2147483648 | bytes 4194304 | tf_op jit(solution)/shard_map/ends/pallas_call | solution.py:455
  64.3 8.1 %inside.1 = (f32[1024,1024]{1,0:T(8,128)S(1)}, f32[1024,128]{1,0:T(8,128)S(1)}) custom-call(bf16[1024,1024]{1,0:T(8,128)(2,1)S(1)} %copy-done.1, bf16[1024,1024]{1,0:T(8,128)(2,1)S(1)} %copy-done.2, bf16[1024,1024]{1,0:T(8,128)(2,1)S(1)} %copy-done.3, f32[1024,128]{1,0:T(8,128)S(1)} %copy-done.5, f32[16,8,64]{2,1,0:T(8,128)S(1)} %get-tuple-element.118.row_ref.refs_10_), custom_call_target="tpu_custom_call" | custom-call | flops 268435456 | bytes 10485760 | tf_op jit(solution)/shard_map/inside/pallas_call | solution.py:506
  75.8 4.3 fusion.9.refs_11_
  80.1 2.8 collective-permute-done.8.got_ref
  83.8 2.6 collective-permute-start.10
  86.4 5.0 %collective-permute-done.5.got_ref = bf16[528,256]{1,0:T(8,128)(2,1)S(1)} collective-permute-done((bf16[528,256]{1,0:T(8,128)(2,1)S(1)}, bf16[528,256]{1,0:T(8,128)(2,1)S(1)}, u32[]{:S(2)}, u32[]{:S(2)}) %collective-permute-start.5) | collective-permute-done | bytes 270368 | tf_op jit(solution)/shard_map/ppermute | solution.py:353
  92.3 4.4 fusion.21.refs_10_
  96.8 7.3 %collective-permute-done.10.got_ref = bf16[528,256]{1,0:T(8,128)(2,1)S(1)} collective-permute-done((bf16[528,256]{1,0:T(8,128)(2,1)S(1)}, bf16[528,256]{1,0:T(8,128)(2,1)S(1)}, u32[]{:S(2)}, u32[]{:S(2)}) %collective-permute-start.10) | collective-permute-done | bytes 270368 | tf_op jit(solution)/shard_map/ppermute | solution.py:353
  113.0 4.8 %collective-permute-done.11.refs_2_ = bf16[528,256]{1,0:T(8,128)(2,1)S(1)} collective-permute-done((bf16[528,256]{1,0:T(8,128)(2,1)S(1)}, bf16[528,256]{1,0:T(8,128)(2,1)S(1)}, u32[]{:S(2)}, u32[]{:S(2)}) %collective-permute-start.11) | collective-permute-done | bytes 270368 | tf_op jit(solution)/shard_map/ppermute | solution.py:353
  118.6 30.7 %middle.1 = (bf16[1024,1024]{1,0:T(8,128)(2,1)}, bf16[1024,1024]{1,0:T(8,128)(2,1)}, f32[1024,1024]{1,0:T(8,128)}, bf16[1024,1024]{1,0:T(8,128)(2,1)}, bf16[1024...) custom-call(s32[1]{0:T(128)} %bitcast.1.flag, ...), custom_call_target="tpu_custom_call" | custom-call | flops 5368709120 | bytes 41943040 | tf_op jit(solution)/shard_map/middle/pallas_call | solution.py:624
  150.7 4.3 convolution_convert_fusion
  156.6 2.3 convolution_convert_fusion.1
  159.4 3.0 collective-permute-done.13.got_ref
  166.3 6.8 %fusion.22 = f32[1024,1024]{1,0:T(8,128)} fusion(bf16[1024,1024]{1,0:T(8,128)(2,1)} %get-tuple-element.140, bf16[1024,1024]{1,0:T(8,128)(2,1)} %param.31), kind=kOutput, calls=%fused_computation.104 | convolution fusion | flops 2147483648 | bytes 8388608 | tf_op jit(solution)/shard_map/dot_general | solution.py:32
  173.1 8.3 %collective-permute-done.18 = bf16[512,1024]{1,0:T(8,128)(2,1)} collective-permute-done((bf16[512,1024]{1,0:T(8,128)(2,1)}, bf16[512,1024]{1,0:T(8,128)(2,1)}, u32[]{:S(2)}, u32[]{:S(2)}) %collective-permute-start.18) | collective-permute-done | bytes 1048608 | tf_op jit(solution)/shard_map/ppermute | solution.py:896
  181.5 2.7 convert_add_fusion.2
  185.5 15.8 %collective-permute-done.17 = bf16[512,1024]{1,0:T(8,128)(2,1)} collective-permute-done((bf16[512,1024]{1,0:T(8,128)(2,1)}, bf16[512,1024]{1,0:T(8,128)(2,1)}, u32[]{:S(2)}, u32[]{:S(2)}) %collective-permute-start.17) | collective-permute-done | bytes 1048608 | tf_op jit(solution)/shard_map/ppermute | solution.py:896
  201.3 2.5 convert_add_fusion.3
  205.7 2.5 pad_maximum_fusion
  215.0 16.8 %collective-permute-done.20 = bf16[512,1024]{1,0:T(8,128)(2,1)} collective-permute-done((bf16[512,1024]{1,0:T(8,128)(2,1)}, bf16[512,1024]{1,0:T(8,128)(2,1)}, u32[]{:S(2)}, u32[]{:S(2)}) %collective-permute-start.20) | collective-permute-done | bytes 1048608 | tf_op jit(solution)/shard_map/ppermute | solution.py:896
  231.8 3.7 convert_add_fusion.1
  236.3 37.8 %back.1 = (f32[1024,1024]{1,0:T(8,128)}, f32[1024,1024]{1,0:T(8,128)}, f32[1024,1024]{1,0:T(8,128)}, bf16[1024,128]{1,0:T(8,128)(2,1)}) custom-call(s32[2]{0:T(128)} %pad_add_fusion.3.flag, f32[520,512]{1,0:T(8,128)} %copy-done.7, bf16[528,512]{1,0:T(8,128)(2,1)} %copy-done.44, bf16[1024,1024]{1,0:T(8,128)(2,1)} %get-tuple-element.117.q_ref.refs_4_.refs_2_, ...), custom_call_target="tpu_custom_call" | custom-call | flops 7516192768 | bytes 31457280 | tf_op jit(solution)/shard_map/back/pallas_call | solution.py:728
  276.6 2.3 edge.1
  280.2 8.4 %reduce-scatter.2.cloned.1.call-done = f32[128,1024]{1,0:T(8,128)} async-done(((f32[512,1024]{1,0:T(8,128)}), f32[128,1024]{1,0:T(8,128)}) %reduce-scatter.2.cloned.1.call-update) | async-done | bytes 524304 | tf_op jit(solution)/shard_map/reduce_scatter | solution.py:937
  293.2 30.8 %maps.1 = (bf16[1024,1024]{1,0:T(8,128)(2,1)}, f32[48,1024]{1,0:T(8,128)}) custom-call(s32[1]{0:T(128)} %bitcast.17.flag, f32[1024,1024]{1,0:T(8,128)} %get-tuple-element.162.qg_ref, f32[1024,1024]{1,0:T(8,128)} %get-tuple-element.163.kg_ref, f32[1024,1024]{1,0:T(8,128)} %get-tuple-element.164.vg_ref, bf16[1024,128]{1,0:T(8,128)(2,1)} %get-tuple-element.165.pre_ref.mine_ref, ...), custom_call_target="tpu_custom_call" | custom-call | flops 5368709120 | bytes 33554432 | tf_op jit(solution)/shard_map/maps/pallas_call | solution.py:877
  324.0 4.6 %fusion.23 = f32[1024,1024]{1,0:T(8,128)S(1)} fusion(bf16[1024,1024]{1,0:T(8,128)(2,1)} %get-tuple-element.126, bf16[1024,1024]{1,0:T(8,128)(2,1)} %get-tuple-element.176), kind=kOutput, calls=%fused_computation.105 | convolution fusion | flops 2147483648 | bytes 8388608 | tf_op jit(solution)/shard_map/dot_general | solution.py:36
  331.5 2.4 fusion.24
  333.9 4.8 %multiply_reduce_fusion.1 = (f32[1024]{0:T(1024)S(1)}, f32[1024]{0:T(1024)S(1)}, f32[1024,1024]{1,0:T(8,128)}, f32[1024,1024]{1,0:T(8,128)S(1)}) fusion(f32[1024]{0:T(1024)S(1)} %copy-done.49, f32[1024]{0:T(1024)S(1)} %add_rsqrt_fusion, f32[1024]{0:T(1024)S(1)} %broadcast_multiply_fusion.1, bf16[1024,512]{1,0:T(8,128)(2,1)S(1)} %copy-done.24, ...), kind=kOutput, calls=%fused_computation.14 | convolution fusion | flops 2159015936 | bytes 18894848 | tf_op jit(solution)/shard_map/dot_general | solution.py:40
  338.7 8.1 %collective-permute-done.24 = bf16[256,1024]{1,0:T(8,128)(2,1)S(1)} collective-permute-done((bf16[256,1024]{1,0:T(8,128)(2,1)S(1)}, bf16[256,1024]{1,0:T(8,128)(2,1)S(1)}, u32[]{:S(2)}, u32[]{:S(2)}) %collective-permute-start.24) | collective-permute-done | bytes 524320 | tf_op jit(solution)/shard_map/ppermute | solution.py:896
  355.8 2.5 collective-permute-start.26
  360.3 4.5 collective-permute-done.26
  368.3 4.5 convert_add_fusion
  376.8 4.4 multiply_reduce_fusion.2
  387.2 3.8 collective-permute-done.30
  391.9 3.4 collective-permute-done.35
  397.3 2.0 collective-permute-start.32
  399.3 4.3 collective-permute-done.36
  405.7 3.3 convert_bitcast_fusion
  409.0 2.3 copy.46
  411.3 2.3 copy.48
  413.6 2.9 collective-permute-done.33
  416.5 2.8 reshape.101
  421.0 2.6 slice_bitcast_fusion.2
  428.4 4.3 collective-permute-done.40
  450.9 2.5 maximum_convert_fusion
  (275 shorter events, 114.2 us)
Async XLA Ops:
  7.2 85.1 %copy-start = (bf16[1024,1024]{1,0:T(8,128)(2,1)S(1)}, bf16[1024,1024]{1,0:T(8,128)(2,1)}, u32[]{:S(2)}) copy-start(bf16[1024,1024]{1,0:T(8,128)(2,1)} %param.21) | copy-start | bytes 6291460
  7.2 281.3 %reduce-scatter.2.cloned.1.call-start = ((), (), s32[]{:S(2)}) async-start(), calls=%async_computation.1 | async-start | bytes 2621440 | tf_op jit(solution)/shard_map/reduce_scatter | solution.py:937
  7.2 11.7 %collective-permute-start = (bf16[1024,512]{1,0:T(8,128)(2,1)}, bf16[1024,512]{1,0:T(8,128)(2,1)S(1)}, u32[]{:S(2)}, u32[]{:S(2)}) collective-permute-start(bf16[1024,512]{1,0:T(8,128)(2,1)} %own_ref.1), channel_id=1, source_target_pairs={{0,1},{1,0},{2,3},{3,2},{4,5},{5,4},{6,7},{7,6},{8,9},{9,8},{10,11... | collective-permute-start | bytes 3145736 | tf_op jit(solution)/shard_map/ppermute | solution.py:974
  8.5 7.5 %collective-permute-start.1 = (bf16[16,512]{1,0:T(8,128)(2,1)S(1)}, bf16[16,512]{1,0:T(8,128)(2,1)S(1)}, u32[]{:S(2)}, u32[]{:S(2)}) collective-permute-start(bf16[16,512]{1,0:T(8,128)(2,1)S(1)} %slice.57), channel_id=1, source_target_pairs={{0,4},{2,6},{4,8},{6,10},{8,12},{10,14},{12,16},{14,18},{16,20},{1... | collective-permute-start | bytes 49160 | tf_op jit(solution)/shard_map/ppermute | solution.py:981
  13.0 47.0 %collective-permute-start.9 = (bf16[1024,512]{1,0:T(8,128)(2,1)}, bf16[1024,512]{1,0:T(8,128)(2,1)}, u32[]{:S(2)}, u32[]{:S(2)}) collective-permute-start(bf16[1024,512]{1,0:T(8,128)(2,1)} %param.18), channel_id=1, source_target_pairs={{0,1},{1,0},{2,3},{3,2},{4,5},{5,4},{6,7},{7,6},{8,9},{9,8},{10,11... | collective-permute-start | bytes 3145736 | tf_op jit(solution)/shard_map/ppermute | solution.py:974
  16.0 3.0 collective-permute-start.2
  19.9 25.9 %copy-start.50 = (f32[8]{0:T(128)S(1)}, f32[8]{0:T(128)}, u32[]{:S(2)}) copy-start(f32[8]{0:T(128)} %param.28) | copy-start | bytes 100
  45.7 1.5 collective-permute-start.3
  58.0 15.2 %collective-permute-start.7 = (bf16[528,256]{1,0:T(8,128)(2,1)}, bf16[528,256]{1,0:T(8,128)(2,1)S(1)}, u32[]{:S(2)}, u32[]{:S(2)}) collective-permute-start(bf16[528,256]{1,0:T(8,128)(2,1)} %get-tuple-element.116), channel_id=1, source_target_pairs={{4,0},{6,2},{0,4},{2,6},{12,8},{14,10},{8,12},{10,14},{20,16},{22,... | collective-permute-start | bytes 811016 | tf_op jit(solution)/shard_map/ppermute | solution.py:353
  59.5 15.5 %collective-permute-start.4 = (bf16[528,256]{1,0:T(8,128)(2,1)}, bf16[528,256]{1,0:T(8,128)(2,1)S(1)}, u32[]{:S(2)}, u32[]{:S(2)}) collective-permute-start(bf16[528,256]{1,0:T(8,128)(2,1)} %get-tuple-element.108), channel_id=1, source_target_pairs={{4,0},{6,2},{0,4},{2,6},{12,8},{14,10},{8,12},{10,14},{20,16},{22,... | collective-permute-start | bytes 811016 | tf_op jit(solution)/shard_map/ppermute | solution.py:353
  73.4 9.5 %collective-permute-start.8 = (bf16[528,256]{1,0:T(8,128)(2,1)S(1)}, bf16[528,256]{1,0:T(8,128)(2,1)S(1)}, u32[]{:S(2)}, u32[]{:S(2)}) collective-permute-start(bf16[528,256]{1,0:T(8,128)(2,1)S(1)} %get-tuple-element.123), channel_id=1, source_target_pairs={{8,0},{10,2},{12,4},{14,6},{0,8},{2,10},{4,12},{6,14},{24,16},{26,... | collective-permute-start | bytes 811016 | tf_op jit(solution)/shard_map/ppermute | solution.py:353
  75.3 16.1 %collective-permute-start.5 = (bf16[528,256]{1,0:T(8,128)(2,1)S(1)}, bf16[528,256]{1,0:T(8,128)(2,1)S(1)}, u32[]{:S(2)}, u32[]{:S(2)}) collective-permute-start(bf16[528,256]{1,0:T(8,128)(2,1)S(1)} %get-tuple-element.110), channel_id=1, source_target_pairs={{8,0},{10,2},{12,4},{14,6},{0,8},{2,10},{4,12},{6,14},{24,16},{26,... | collective-permute-start | bytes 811016 | tf_op jit(solution)/shard_map/ppermute | solution.py:353
  83.8 20.2 %collective-permute-start.10 = (bf16[528,256]{1,0:T(8,128)(2,1)S(1)}, bf16[528,256]{1,0:T(8,128)(2,1)S(1)}, u32[]{:S(2)}, u32[]{:S(2)}) collective-permute-start(bf16[528,256]{1,0:T(8,128)(2,1)S(1)} %get-tuple-element.125), channel_id=1, source_target_pairs={{16,0},{18,2},{20,4},{22,6},{24,8},{26,10},{28,12},{30,14},{0,16},... | collective-permute-start | bytes 811016 | tf_op jit(solution)/shard_map/ppermute | solution.py:353
  92.3 16.0 %collective-permute-start.6 = (bf16[528,256]{1,0:T(8,128)(2,1)S(1)}, bf16[528,256]{1,0:T(8,128)(2,1)S(1)}, u32[]{:S(2)}, u32[]{:S(2)}) collective-permute-start(bf16[528,256]{1,0:T(8,128)(2,1)S(1)} %get-tuple-element.111), channel_id=1, source_target_pairs={{16,0},{18,2},{20,4},{22,6},{24,8},{26,10},{28,12},{30,14},{0,16},... | collective-permute-start | bytes 811016 | tf_op jit(solution)/shard_map/ppermute | solution.py:353
  105.6 7.4 %collective-permute-start.12 = (bf16[528,256]{1,0:T(8,128)(2,1)S(1)}, bf16[528,256]{1,0:T(8,128)(2,1)S(1)}, u32[]{:S(2)}, u32[]{:S(2)}) collective-permute-start(bf16[528,256]{1,0:T(8,128)(2,1)S(1)} %get-tuple-element.132), channel_id=1, source_target_pairs={{4,0},{6,2},{0,4},{2,6},{12,8},{14,10},{8,12},{10,14},{20,16},{22,... | collective-permute-start | bytes 811016 | tf_op jit(solution)/shard_map/ppermute | solution.py:353
  109.9 8.0 %collective-permute-start.11 = (bf16[528,256]{1,0:T(8,128)(2,1)S(1)}, bf16[528,256]{1,0:T(8,128)(2,1)S(1)}, u32[]{:S(2)}, u32[]{:S(2)}) collective-permute-start(bf16[528,256]{1,0:T(8,128)(2,1)S(1)} %get-tuple-element.131), channel_id=1, source_target_pairs={{4,0},{6,2},{0,4},{2,6},{12,8},{14,10},{8,12},{10,14},{20,16},{22,... | collective-permute-start | bytes 811016 | tf_op jit(solution)/shard_map/ppermute | solution.py:353
  149.2 13.1 %collective-permute-start.13 = (bf16[528,512]{1,0:T(8,128)(2,1)}, bf16[528,512]{1,0:T(8,128)(2,1)S(1)}, u32[]{:S(2)}, u32[]{:S(2)}) collective-permute-start(bf16[528,512]{1,0:T(8,128)(2,1)} %get-tuple-element.139), channel_id=1, source_target_pairs={{4,0},{6,2},{0,4},{2,6},{12,8},{14,10},{8,12},{10,14},{20,16},{22,... | collective-permute-start | bytes 1622024 | tf_op jit(solution)/shard_map/ppermute | solution.py:353
  155.1 26.4 %collective-permute-start.18 = (bf16[512,1024]{1,0:T(8,128)(2,1)}, bf16[512,1024]{1,0:T(8,128)(2,1)}, u32[]{:S(2)}, u32[]{:S(2)}) collective-permute-start(bf16[512,1024]{1,0:T(8,128)(2,1)} %convolution_convert_fusion), channel_id=1, source_target_pairs={{2,0},{0,2},{6,4},{4,6},{10,8},{8,10},{14,12},{12,14},{18,16},{16,... | collective-permute-start | bytes 3145736 | tf_op jit(solution)/shard_map/ppermute | solution.py:896
  158.9 42.4 %collective-permute-start.17 = (bf16[512,1024]{1,0:T(8,128)(2,1)}, bf16[512,1024]{1,0:T(8,128)(2,1)}, u32[]{:S(2)}, u32[]{:S(2)}) collective-permute-start(bf16[512,1024]{1,0:T(8,128)(2,1)} %convolution_convert_fusion.1), channel_id=1, source_target_pairs={{2,0},{0,2},{6,4},{4,6},{10,8},{8,10},{14,12},{12,14},{18,16},{16,... | collective-permute-start | bytes 3145736 | tf_op jit(solution)/shard_map/ppermute | solution.py:896
  165.8 18.3 %collective-permute-start.14 = (bf16[528,512]{1,0:T(8,128)(2,1)S(1)}, bf16[528,512]{1,0:T(8,128)(2,1)S(1)}, u32[]{:S(2)}, u32[]{:S(2)}) collective-permute-start(bf16[528,512]{1,0:T(8,128)(2,1)S(1)} %get-tuple-element.143), channel_id=1, source_target_pairs={{8,0},{10,2},{12,4},{14,6},{0,8},{2,10},{4,12},{6,14},{24,16},{26,... | collective-permute-start | bytes 1622024 | tf_op jit(solution)/shard_map/ppermute | solution.py:353
  185.5 22.6 %collective-permute-start.16 = (bf16[528,512]{1,0:T(8,128)(2,1)S(1)}, bf16[528,512]{1,0:T(8,128)(2,1)S(1)}, u32[]{:S(2)}, u32[]{:S(2)}) collective-permute-start(bf16[528,512]{1,0:T(8,128)(2,1)S(1)} %get-tuple-element.147), channel_id=1, source_target_pairs={{16,0},{18,2},{20,4},{22,6},{24,8},{26,10},{28,12},{30,14},{0,16},... | collective-permute-start | bytes 1622024 | tf_op jit(solution)/shard_map/ppermute | solution.py:353
  209.0 22.9 %collective-permute-start.20 = (bf16[512,1024]{1,0:T(8,128)(2,1)}, bf16[512,1024]{1,0:T(8,128)(2,1)}, u32[]{:S(2)}, u32[]{:S(2)}) collective-permute-start(bf16[512,1024]{1,0:T(8,128)(2,1)} %fusion.4), channel_id=1, source_target_pairs={{8,0},{10,2},{12,4},{14,6},{0,8},{2,10},{4,12},{6,14},{24,16},{26,... | collective-permute-start | bytes 3145736 | tf_op jit(solution)/shard_map/ppermute | solution.py:896
  214.0 21.5 %collective-permute-start.19 = (bf16[528,512]{1,0:T(8,128)(2,1)}, bf16[528,512]{1,0:T(8,128)(2,1)S(1)}, u32[]{:S(2)}, u32[]{:S(2)}) collective-permute-start(bf16[528,512]{1,0:T(8,128)(2,1)} %get-tuple-element.152), channel_id=1, source_target_pairs={{4,0},{6,2},{0,4},{2,6},{12,8},{14,10},{8,12},{10,14},{20,16},{22,... | collective-permute-start | bytes 1622024 | tf_op jit(solution)/shard_map/ppermute | solution.py:353
  235.5 137.3 %all-gather.2.cloned.1.call-start = ((), (), s32[]{:S(2)}) async-start(), calls=%async_computation.2 | async-start | bytes 4456448 | tf_op jit(solution)/shard_map/all_gather | solution.py:1049
  236.3 37.9 %copy-start.47 = (bf16[3,1024,8]{1,2,0:T(8,128)(2,1)S(1)}, bf16[3,1024,8]{1,2,0:T(8,128)(2,1)}, u32[]{:S(2)}) copy-start(bf16[3,1024,8]{1,2,0:T(8,128)(2,1)} %param.27) | copy-start | bytes 147460
  236.3 38.0 %copy-start.51 = (s32[8]{0:T(128)S(1)}, s32[8]{0:T(128)}, u32[]{:S(2)}) copy-start(s32[8]{0:T(128)} %constant.217) | copy-start | bytes 100
  274.1 1.8 collective-permute-start.21
  278.9 11.4 %collective-permute-start.22 = (f32[8,1024]{1,0:T(8,128)}, f32[8,1024]{1,0:T(8,128)S(1)}, u32[]{:S(2)}, u32[]{:S(2)}) collective-permute-start(f32[8,1024]{1,0:T(8,128)} %edge.1), channel_id=1, source_target_pairs={{4,0},{6,2},{8,4},{10,6},{12,8},{14,10},{16,12},{18,14},{20,16},{2... | collective-permute-start | bytes 98312 | tf_op jit(solution)/shard_map/ppermute | solution.py:981
  329.1 17.7 %collective-permute-start.24 = (bf16[256,1024]{1,0:T(8,128)(2,1)S(1)}, bf16[256,1024]{1,0:T(8,128)(2,1)S(1)}, u32[]{:S(2)}, u32[]{:S(2)}) collective-permute-start(bf16[256,1024]{1,0:T(8,128)(2,1)S(1)} %dynamic-slice_convert_fusion), channel_id=1, source_target_pairs={{4,0},{6,2},{0,4},{2,6},{12,8},{14,10},{8,12},{10,14},{20,16},{22,... | collective-permute-start | bytes 1572872 | tf_op jit(solution)/shard_map/ppermute | solution.py:896
  329.9 18.5 %collective-permute-start.23 = (bf16[256,1024]{1,0:T(8,128)(2,1)S(1)}, bf16[256,1024]{1,0:T(8,128)(2,1)S(1)}, u32[]{:S(2)}, u32[]{:S(2)}) collective-permute-start(bf16[256,1024]{1,0:T(8,128)(2,1)S(1)} %dynamic-slice_convert_fusion.1), channel_id=1, source_target_pairs={{2,0},{0,2},{6,4},{4,6},{10,8},{8,10},{14,12},{12,14},{18,16},{16,... | collective-permute-start | bytes 1572872 | tf_op jit(solution)/shard_map/ppermute | solution.py:896
  351.1 17.2 %collective-permute-start.27 = (f32[1024,512]{1,0:T(8,128)}, f32[1024,512]{1,0:T(8,128)}, u32[]{:S(2)}, u32[]{:S(2)}) collective-permute-start(f32[1024,512]{1,0:T(8,128)} %constant_dynamic-slice_fusion), channel_id=1, source_target_pairs={{0,1},{1,0},{2,3},{3,2},{4,5},{5,4},{6,7},{7,6},{8,9},{9,8},{10,11... | collective-permute-start | bytes 6291464 | tf_op jit(solution)/shard_map/ppermute | solution.py:974
  354.1 22.8 %collective-permute-start.15 = (f32[1024,512]{1,0:T(8,128)}, f32[1024,512]{1,0:T(8,128)}, u32[]{:S(2)}, u32[]{:S(2)}) collective-permute-start(f32[1024,512]{1,0:T(8,128)} %constant_dynamic-slice_fusion.1), channel_id=1, source_target_pairs={{0,1},{1,0},{2,3},{3,2},{4,5},{5,4},{6,7},{7,6},{8,9},{9,8},{10,11... | collective-permute-start | bytes 6291464 | tf_op jit(solution)/shard_map/ppermute | solution.py:974
  354.1 6.2 %collective-permute-start.28 = (f32[2,1024]{1,0:T(2,128)S(1)}, f32[2,1024]{1,0:T(2,128)S(1)}, u32[]{:S(2)}, u32[]{:S(2)}) collective-permute-start(f32[2,1024]{1,0:T(2,128)S(1)} %pad_maximum_fusion.10), channel_id=1, source_target_pairs={{0,1},{1,0},{2,3},{3,2},{4,5},{5,4},{6,7},{7,6},{8,9},{9,8},{10,11... | collective-permute-start | bytes 24584 | tf_op jit(solution)/shard_map/ppermute | solution.py:974
  355.8 9.1 %collective-permute-start.26 = (bf16[128,1024]{1,0:T(8,128)(2,1)S(1)}, bf16[128,1024]{1,0:T(8,128)(2,1)S(1)}, u32[]{:S(2)}, u32[]{:S(2)}) collective-permute-start(bf16[128,1024]{1,0:T(8,128)(2,1)S(1)} %dynamic-slice_convert_fusion.3), channel_id=1, source_target_pairs={{2,0},{0,2},{6,4},{4,6},{10,8},{8,10},{14,12},{12,14},{18,16},{16,... | collective-permute-start | bytes 786440 | tf_op jit(solution)/shard_map/ppermute | solution.py:896
  359.4 8.1 %collective-permute-start.25 = (bf16[128,1024]{1,0:T(8,128)(2,1)S(1)}, bf16[128,1024]{1,0:T(8,128)(2,1)S(1)}, u32[]{:S(2)}, u32[]{:S(2)}) collective-permute-start(bf16[128,1024]{1,0:T(8,128)(2,1)S(1)} %dynamic-slice_convert_fusion.4), channel_id=1, source_target_pairs={{4,0},{6,2},{0,4},{2,6},{12,8},{14,10},{8,12},{10,14},{20,16},{22,... | collective-permute-start | bytes 786440 | tf_op jit(solution)/shard_map/ppermute | solution.py:896
  376.8 8.2 %collective-permute-start.34 = (bf16[128,1024]{1,0:T(8,128)(2,1)}, bf16[128,1024]{1,0:T(8,128)(2,1)}, u32[]{:S(2)}, u32[]{:S(2)}) collective-permute-start(bf16[128,1024]{1,0:T(8,128)(2,1)} %dynamic-slice_convert_fusion.2), channel_id=1, source_target_pairs={{8,0},{10,2},{12,4},{14,6},{0,8},{2,10},{4,12},{6,14},{24,16},{26,... | collective-permute-start | bytes 786440 | tf_op jit(solution)/shard_map/ppermute | solution.py:896
  381.3 1.4 collective-permute-start.29
  383.9 7.1 %collective-permute-start.30 = (f32[48,1024]{1,0:T(8,128)S(1)}, f32[48,1024]{1,0:T(8,128)S(1)}, u32[]{:S(2)}, u32[]{:S(2)}) collective-permute-start(f32[48,1024]{1,0:T(8,128)S(1)} %pad_add_fusion), channel_id=1, source_target_pairs={{2,0},{0,2},{6,4},{4,6},{10,8},{8,10},{14,12},{12,14},{18,16},{16,... | collective-permute-start | bytes 589832 | tf_op jit(solution)/shard_map/ppermute | solution.py:896
  386.3 9.1 %collective-permute-start.35 = (bf16[64,1024]{1,0:T(8,128)(2,1)S(1)}, bf16[64,1024]{1,0:T(8,128)(2,1)S(1)}, u32[]{:S(2)}, u32[]{:S(2)}) collective-permute-start(bf16[64,1024]{1,0:T(8,128)(2,1)S(1)} %dynamic-slice_convert_fusion.5), channel_id=1, source_target_pairs={{16,0},{18,2},{20,4},{22,6},{24,8},{26,10},{28,12},{30,14},{0,16},... | collective-permute-start | bytes 393224 | tf_op jit(solution)/shard_map/ppermute | solution.py:896
  391.0 6.3 %collective-permute-start.31 = (f32[48,1024]{1,0:T(8,128)S(1)}, f32[48,1024]{1,0:T(8,128)S(1)}, u32[]{:S(2)}, u32[]{:S(2)}) collective-permute-start(f32[48,1024]{1,0:T(8,128)S(1)} %fusion.38), channel_id=1, source_target_pairs={{4,0},{6,2},{0,4},{2,6},{12,8},{14,10},{8,12},{10,14},{20,16},{22,... | collective-permute-start | bytes 589832 | tf_op jit(solution)/shard_map/ppermute | solution.py:896
  395.4 8.2 %collective-permute-start.36 = (bf16[64,1024]{1,0:T(8,128)(2,1)S(1)}, bf16[64,1024]{1,0:T(8,128)(2,1)S(1)}, u32[]{:S(2)}, u32[]{:S(2)}) collective-permute-start(bf16[64,1024]{1,0:T(8,128)(2,1)S(1)} %add_convert_fusion), channel_id=1, source_target_pairs={{16,0},{18,2},{20,4},{22,6},{24,8},{26,10},{28,12},{30,14},{0,16},... | collective-permute-start | bytes 393224 | tf_op jit(solution)/shard_map/ppermute | solution.py:896
  397.3 8.3 %collective-permute-start.32 = (f32[48,1024]{1,0:T(8,128)S(1)}, f32[48,1024]{1,0:T(8,128)S(1)}, u32[]{:S(2)}, u32[]{:S(2)}) collective-permute-start(f32[48,1024]{1,0:T(8,128)S(1)} %add.239), channel_id=1, source_target_pairs={{8,0},{10,2},{12,4},{14,6},{0,8},{2,10},{4,12},{6,14},{24,16},{26,... | collective-permute-start | bytes 589832 | tf_op jit(solution)/shard_map/ppermute | solution.py:896
  403.7 16.3 %collective-permute-start.37 = (bf16[128,1024]{1,0:T(8,128)(2,1)S(1)}, bf16[128,1024]{1,0:T(8,128)(2,1)S(1)}, u32[]{:S(2)}, u32[]{:S(2)}) collective-permute-start(bf16[128,1024]{1,0:T(8,128)(2,1)S(1)} %pad_maximum_fusion.8), channel_id=1, source_target_pairs={{8,0},{10,2},{12,4},{14,6},{0,8},{2,10},{4,12},{6,14},{24,16},{26,... | collective-permute-start | bytes 786440 | tf_op jit(solution)/shard_map/ppermute | solution.py:896
  405.6 10.8 %collective-permute-start.33 = (f32[48,1024]{1,0:T(8,128)S(1)}, f32[48,1024]{1,0:T(8,128)S(1)}, u32[]{:S(2)}, u32[]{:S(2)}) collective-permute-start(f32[48,1024]{1,0:T(8,128)S(1)} %add.240), channel_id=1, source_target_pairs={{16,0},{18,2},{20,4},{22,6},{24,8},{26,10},{28,12},{30,14},{0,16},... | collective-permute-start | bytes 589832 | tf_op jit(solution)/shard_map/ppermute | solution.py:896
  420.1 6.4 %collective-permute-start.38 = (bf16[128,1024]{1,0:T(8,128)(2,1)S(1)}, bf16[128,1024]{1,0:T(8,128)(2,1)S(1)}, u32[]{:S(2)}, u32[]{:S(2)}) collective-permute-start(bf16[128,1024]{1,0:T(8,128)(2,1)S(1)} %get-tuple-element.228), channel_id=1, source_target_pairs={{4,0},{6,2},{0,4},{2,6},{12,8},{14,10},{8,12},{10,14},{20,16},{22,... | collective-permute-start | bytes 786440 | tf_op jit(solution)/shard_map/ppermute | solution.py:896
  423.5 9.2 %collective-permute-start.40 = (bf16[128,1024]{1,0:T(8,128)(2,1)S(1)}, bf16[128,1024]{1,0:T(8,128)(2,1)S(1)}, u32[]{:S(2)}, u32[]{:S(2)}) collective-permute-start(bf16[128,1024]{1,0:T(8,128)(2,1)S(1)} %get-tuple-element.229), channel_id=1, source_target_pairs={{2,0},{0,2},{6,4},{4,6},{10,8},{8,10},{14,12},{12,14},{18,16},{16,... | collective-permute-start | bytes 786440 | tf_op jit(solution)/shard_map/ppermute | solution.py:896
  427.4 20.9 %collective-permute-start.39 = (bf16[256,1024]{1,0:T(8,128)(2,1)}, bf16[256,1024]{1,0:T(8,128)(2,1)}, u32[]{:S(2)}, u32[]{:S(2)}) collective-permute-start(bf16[256,1024]{1,0:T(8,128)(2,1)} %pad_maximum_fusion.6), channel_id=1, source_target_pairs={{2,0},{0,2},{6,4},{4,6},{10,8},{8,10},{14,12},{12,14},{18,16},{16,... | collective-permute-start | bytes 1572872 | tf_op jit(solution)/shard_map/ppermute | solution.py:896
  433.6 16.0 %collective-permute-start.41 = (bf16[256,1024]{1,0:T(8,128)(2,1)}, bf16[256,1024]{1,0:T(8,128)(2,1)}, u32[]{:S(2)}, u32[]{:S(2)}) collective-permute-start(bf16[256,1024]{1,0:T(8,128)(2,1)} %pad_maximum_fusion.7), channel_id=1, source_target_pairs={{4,0},{6,2},{0,4},{2,6},{12,8},{14,10},{8,12},{10,14},{20,16},{22,... | collective-permute-start | bytes 1572872 | tf_op jit(solution)/shard_map/ppermute | solution.py:896
  (55 other events, 326.0 us)
Sparse Core Ops, SparseCore 0:
  235.6 52.8 reduce-scatter.1
  291.7 78.5 all-gather.1

commit v4 on v3

--- a/solution.py
+++ b/solution.py
@@ -639,7 +639,7 @@
                         pltpu.VMEM((2, DH, DH), f32), pltpu.VMEM((8, DH), f32),
                         pltpu.VMEM((TILE, chan), f32), pltpu.VMEM((TILE, LANES), f32)],
         compiler_params=params(LIMIT),
-        cost_estimate=cost(10 * count * chan * DH, count * chan * 40),
+        cost_estimate=cost(10 * count * chan * DH, count * chan * 107),
         name="middle",
     )(flag, *states, q, k, v, inside, norms, col, gate, dgated, active, group, skip, total)
 
@@ -716,7 +716,7 @@
         pre_ref[here, :] = lanes_of(*in_cols, *forget, offset=4 * flag[1]).astype(bf16)
         return carry
 
-    lax.fori_loop(0, per, body, 0, unroll=2)
+    lax.fori_loop(0, per, body, 0, unroll=4)
 
 
 def back_stage(flag, states, q, k, v, nlow, clow, start, nvec, col, row, stat):
@@ -736,7 +736,7 @@
         out_shape=[shape_of(count, chan)] * 3 + [shape_of(count, LANES, dtype=bf16)],
         scratch_shapes=[pltpu.VMEM((2, DH, DH), f32), pltpu.VMEM((8, DH), f32)],
         compiler_params=params(LIMIT),
-        cost_estimate=cost(14 * count * chan * DH, count * chan * 30),
+        cost_estimate=cost(14 * count * chan * DH, count * chan * 133),
         name="back",
     )(flag, *states, q, k, v, nlow, clow, start, nvec, col, row, stat)
 
@@ -886,7 +886,7 @@
         scratch_shapes=[pltpu.VMEM((TILE + 8, chan), f32), pltpu.VMEM((3, groups, GROUP, GROUP), bf16),
                         pltpu.VMEM((3, groups, GROUP, GROUP), bf16), pltpu.VMEM((3, groups, GROUP, GROUP), f32)],
         compiler_params=params(LIMIT),
-        cost_estimate=cost(20 * count * chan * GROUP, count * chan * 32),
+        cost_estimate=cost(20 * count * chan * GROUP, count * chan * 110),
         name="maps",
     )(flag, qg, kg, vg, pre, other, sgrad, conv, inner, q, k, v, edge, skip, cw, coefs, gwt, ggroup, gskip)
 

time: 470 us -> 470 us (level)
  no operation moved by 1% of the time
where the time goes in v4:
time: 470 us; the launch traced here: 462 us
  Pallas kernels  150 us (32%)
  waiting for transfers between devices  116 us (25%)
  local copies, waits for them, and re-layouts  58 us (12%)
  other arithmetic  42.1 us (9%)
  matrix products  39 us (8%)
  starting transfers between devices  37.7 us (8%)
  between operations  18.4 us (4%)
    ppermute x19, waiting for transfers between devices, exchanged(): return lax.ppermute(value, 'dp', route)  79 us
    pallas_call x1, Pallas kernels, back_stage(): pl.pallas_call(back_kernel, grid=(tiles,), in_specs=[smem, *pack_specs(BA...  37 us
    pallas_call x1, Pallas kernels, middle_stage(): pl.pallas_call(middle_kernel, grid=(count // TILE,), in_specs=[smem, *pac...  30.9 us
    pallas_call x1, Pallas kernels, maps_stage(): pl.pallas_call(maps_kernel, grid=(tiles,), in_specs=[smem, flip, flip, fl...  30.6 us
    unnamed x125, local copies, waits for them, and re-layouts  29.3 us
    pallas_call x1, Pallas kernels, first_stage(): pl.pallas_call(first_kernel, grid=(count // TILE,), in_specs=[smem, rows(...  25.7 us
    ppermute x12, waiting for transfers between devices, swap(): return lax.ppermute(value, 'dp', route)  25.6 us
    ppermute x19, starting transfers between devices, exchanged(): return lax.ppermute(value, 'dp', route)  17.6 us
  transfers between devices with their start and end apart: 44, of which 25 were waited for; matrix products, arithmetic and copies ran while one was open for 25% of the time, Pallas kernels for 26%

profile of v4, /device:TPU:0, one launch (start us, length us, event | category | flops | bytes accessed | tf_op | source)
XLA Modules:
  0.0 461.6 jit_solution(10155559338492231925)
XLA Ops:
  8.5 4.5 collective-permute-start.1
  20.0 25.7 %first.1 = (bf16[1024,1024]{1,0:T(8,128)(2,1)}, f32[1024,1024]{1,0:T(8,128)}, f32[1024,1024]{1,0:T(8,128)}, f32[1024,1024]{1,0:T(8,128)}, bf16[1024,1024]{1,0:T(...) custom-call(s32[2]{0:T(128)} %pad_add_fusion.2.flag, ...), custom_call_target="tpu_custom_call" | custom-call | flops 8589934592 | bytes 20971520 | tf_op jit(solution)/shard_map/first/pallas_call | solution.py:173
  50.8 7.2 %ends.1 = (f32[520,256]{1,0:T(8,128)}, f32[520,256]{1,0:T(8,128)}, bf16[528,256]{1,0:T(8,128)(2,1)}, bf16[528,256]{1,0:T(8,128)(2,1)}) custom-call(s32[1]{0:T(128)} %bitcast.1.flag, bf16[1024,1024]{1,0:T(8,128)(2,1)} %get-tuple-element.102.k_ref.refs_5_.refs_3_, bf16[1024,1024]{1,0:T(8,128)(2,1)} %get-tuple-element.103.v_ref.refs_6_.refs_4_, ...), custom_call_target="tpu_custom_call" | custom-call | flops 2147483648 | bytes 4194304 | tf_op jit(solution)/shard_map/ends/pallas_call | solution.py:455
  64.3 7.8 %inside.1 = (f32[1024,1024]{1,0:T(8,128)S(1)}, f32[1024,128]{1,0:T(8,128)S(1)}) custom-call(bf16[1024,1024]{1,0:T(8,128)(2,1)S(1)} %copy-done.1, bf16[1024,1024]{1,0:T(8,128)(2,1)S(1)} %copy-done.2, bf16[1024,1024]{1,0:T(8,128)(2,1)S(1)} %copy-done.3, f32[1024,128]{1,0:T(8,128)S(1)} %copy-done.5, f32[16,8,64]{2,1,0:T(8,128)S(1)} %get-tuple-element.118.row_ref.refs_10_), custom_call_target="tpu_custom_call" | custom-call | flops 268435456 | bytes 10485760 | tf_op jit(solution)/shard_map/inside/pallas_call | solution.py:506
  75.5 4.3 fusion.9.refs_11_
  79.8 2.8 collective-permute-done.8.got_ref
  83.5 2.6 collective-permute-start.10
  86.1 4.9 %collective-permute-done.5.got_ref = bf16[528,256]{1,0:T(8,128)(2,1)S(1)} collective-permute-done((bf16[528,256]{1,0:T(8,128)(2,1)S(1)}, bf16[528,256]{1,0:T(8,128)(2,1)S(1)}, u32[]{:S(2)}, u32[]{:S(2)}) %collective-permute-start.5) | collective-permute-done | bytes 270368 | tf_op jit(solution)/shard_map/ppermute | solution.py:353
  92.0 4.4 fusion.21.refs_10_
  96.4 7.3 %collective-permute-done.10.got_ref = bf16[528,256]{1,0:T(8,128)(2,1)S(1)} collective-permute-done((bf16[528,256]{1,0:T(8,128)(2,1)S(1)}, bf16[528,256]{1,0:T(8,128)(2,1)S(1)}, u32[]{:S(2)}, u32[]{:S(2)}) %collective-permute-start.10) | collective-permute-done | bytes 270368 | tf_op jit(solution)/shard_map/ppermute | solution.py:353
  112.7 4.8 %collective-permute-done.11.refs_2_ = bf16[528,256]{1,0:T(8,128)(2,1)S(1)} collective-permute-done((bf16[528,256]{1,0:T(8,128)(2,1)S(1)}, bf16[528,256]{1,0:T(8,128)(2,1)S(1)}, u32[]{:S(2)}, u32[]{:S(2)}) %collective-permute-start.11) | collective-permute-done | bytes 270368 | tf_op jit(solution)/shard_map/ppermute | solution.py:353
  118.2 30.9 %middle.1 = (bf16[1024,1024]{1,0:T(8,128)(2,1)}, bf16[1024,1024]{1,0:T(8,128)(2,1)}, f32[1024,1024]{1,0:T(8,128)}, bf16[1024,1024]{1,0:T(8,128)(2,1)}, bf16[1024...) custom-call(s32[1]{0:T(128)} %bitcast.1.flag, ...), custom_call_target="tpu_custom_call" | custom-call | flops 5368709120 | bytes 112197632 | tf_op jit(solution)/shard_map/middle/pallas_call | solution.py:624
  150.7 4.3 convolution_convert_fusion
  156.5 2.3 convolution_convert_fusion.1
  159.4 2.9 collective-permute-done.13.got_ref
  166.1 6.7 %fusion.22 = f32[1024,1024]{1,0:T(8,128)} fusion(bf16[1024,1024]{1,0:T(8,128)(2,1)} %get-tuple-element.140, bf16[1024,1024]{1,0:T(8,128)(2,1)} %param.31), kind=kOutput, calls=%fused_computation.104 | convolution fusion | flops 2147483648 | bytes 8388608 | tf_op jit(solution)/shard_map/dot_general | solution.py:32
  172.8 8.6 %collective-permute-done.18 = bf16[512,1024]{1,0:T(8,128)(2,1)} collective-permute-done((bf16[512,1024]{1,0:T(8,128)(2,1)}, bf16[512,1024]{1,0:T(8,128)(2,1)}, u32[]{:S(2)}, u32[]{:S(2)}) %collective-permute-start.18) | collective-permute-done | bytes 1048608 | tf_op jit(solution)/shard_map/ppermute | solution.py:896
  181.4 2.6 convert_add_fusion.2
  185.5 15.8 %collective-permute-done.17 = bf16[512,1024]{1,0:T(8,128)(2,1)} collective-permute-done((bf16[512,1024]{1,0:T(8,128)(2,1)}, bf16[512,1024]{1,0:T(8,128)(2,1)}, u32[]{:S(2)}, u32[]{:S(2)}) %collective-permute-start.17) | collective-permute-done | bytes 1048608 | tf_op jit(solution)/shard_map/ppermute | solution.py:896
  201.3 2.5 convert_add_fusion.3
  205.7 2.5 pad_maximum_fusion
  214.8 17.1 %collective-permute-done.20 = bf16[512,1024]{1,0:T(8,128)(2,1)} collective-permute-done((bf16[512,1024]{1,0:T(8,128)(2,1)}, bf16[512,1024]{1,0:T(8,128)(2,1)}, u32[]{:S(2)}, u32[]{:S(2)}) %collective-permute-start.20) | collective-permute-done | bytes 1048608 | tf_op jit(solution)/shard_map/ppermute | solution.py:896
  231.9 3.7 convert_add_fusion.1
  236.3 37.0 %back.1 = (f32[1024,1024]{1,0:T(8,128)}, f32[1024,1024]{1,0:T(8,128)}, f32[1024,1024]{1,0:T(8,128)}, bf16[1024,128]{1,0:T(8,128)(2,1)}) custom-call(s32[2]{0:T(128)} %pad_add_fusion.3.flag, f32[520,512]{1,0:T(8,128)} %copy-done.7, bf16[528,512]{1,0:T(8,128)(2,1)} %copy-done.44, bf16[1024,1024]{1,0:T(8,128)(2,1)} %get-tuple-element.117.q_ref.refs_4_.refs_2_, ...), custom_call_target="tpu_custom_call" | custom-call | flops 7516192768 | bytes 139460608 | tf_op jit(solution)/shard_map/back/pallas_call | solution.py:728
  275.9 2.3 edge.1
  279.4 9.2 %reduce-scatter.2.cloned.1.call-done = f32[128,1024]{1,0:T(8,128)} async-done(((f32[512,1024]{1,0:T(8,128)}), f32[128,1024]{1,0:T(8,128)}) %reduce-scatter.2.cloned.1.call-update) | async-done | bytes 524304 | tf_op jit(solution)/shard_map/reduce_scatter | solution.py:937
  293.2 30.6 %maps.1 = (bf16[1024,1024]{1,0:T(8,128)(2,1)}, f32[48,1024]{1,0:T(8,128)}) custom-call(s32[1]{0:T(128)} %bitcast.17.flag, f32[1024,1024]{1,0:T(8,128)} %get-tuple-element.162.qg_ref, f32[1024,1024]{1,0:T(8,128)} %get-tuple-element.163.kg_ref, f32[1024,1024]{1,0:T(8,128)} %get-tuple-element.164.vg_ref, bf16[1024,128]{1,0:T(8,128)(2,1)} %get-tuple-element.165.pre_ref.mine_ref, ...), custom_call_target="tpu_custom_call" | custom-call | flops 5368709120 | bytes 115343360 | tf_op jit(solution)/shard_map/maps/pallas_call | solution.py:877
  323.8 4.6 fusion.23
  331.2 2.4 fusion.24
  333.7 4.8 %multiply_reduce_fusion.1 = (f32[1024]{0:T(1024)S(1)}, f32[1024]{0:T(1024)S(1)}, f32[1024,1024]{1,0:T(8,128)}, f32[1024,1024]{1,0:T(8,128)S(1)}) fusion(f32[1024]{0:T(1024)S(1)} %copy-done.49, f32[1024]{0:T(1024)S(1)} %add_rsqrt_fusion, f32[1024]{0:T(1024)S(1)} %broadcast_multiply_fusion.1, bf16[1024,512]{1,0:T(8,128)(2,1)S(1)} %copy-done.24, ...), kind=kOutput, calls=%fused_computation.14 | convolution fusion | flops 2159015936 | bytes 18894848 | tf_op jit(solution)/shard_map/dot_general | solution.py:40
  338.5 7.8 %collective-permute-done.24 = bf16[256,1024]{1,0:T(8,128)(2,1)S(1)} collective-permute-done((bf16[256,1024]{1,0:T(8,128)(2,1)S(1)}, bf16[256,1024]{1,0:T(8,128)(2,1)S(1)}, u32[]{:S(2)}, u32[]{:S(2)}) %collective-permute-start.24) | collective-permute-done | bytes 524320 | tf_op jit(solution)/shard_map/ppermute | solution.py:896
  355.3 2.6 collective-permute-start.26
  359.9 4.6 collective-permute-done.26
  367.9 4.6 convert_add_fusion
  376.5 4.4 multiply_reduce_fusion.2
  387.2 3.5 collective-permute-done.30
  391.6 3.4 collective-permute-done.35
  397.0 2.0 collective-permute-start.32
  399.0 4.1 collective-permute-done.36
  403.2 2.1 collective-permute-done.32
  405.4 3.3 convert_bitcast_fusion
  408.6 2.3 copy.46
  411.0 2.3 copy.48
  413.3 2.9 collective-permute-done.33
  416.2 2.8 reshape.101
  420.6 2.6 slice_bitcast_fusion.2
  428.1 4.3 collective-permute-done.40
  450.6 2.5 maximum_convert_fusion
  (275 shorter events, 114.1 us)
Async XLA Ops:
  7.2 84.8 %copy-start = (bf16[1024,1024]{1,0:T(8,128)(2,1)S(1)}, bf16[1024,1024]{1,0:T(8,128)(2,1)}, u32[]{:S(2)}) copy-start(bf16[1024,1024]{1,0:T(8,128)(2,1)} %param.21) | copy-start | bytes 6291460
  7.2 281.4 %reduce-scatter.2.cloned.1.call-start = ((), (), s32[]{:S(2)}) async-start(), calls=%async_computation.1 | async-start | bytes 2621440 | tf_op jit(solution)/shard_map/reduce_scatter | solution.py:937
  7.2 11.7 %collective-permute-start = (bf16[1024,512]{1,0:T(8,128)(2,1)}, bf16[1024,512]{1,0:T(8,128)(2,1)S(1)}, u32[]{:S(2)}, u32[]{:S(2)}) collective-permute-start(bf16[1024,512]{1,0:T(8,128)(2,1)} %own_ref.1), channel_id=1, source_target_pairs={{0,1},{1,0},{2,3},{3,2},{4,5},{5,4},{6,7},{7,6},{8,9},{9,8},{10,11... | collective-permute-start | bytes 3145736 | tf_op jit(solution)/shard_map/ppermute | solution.py:974
  8.5 7.5 %collective-permute-start.1 = (bf16[16,512]{1,0:T(8,128)(2,1)S(1)}, bf16[16,512]{1,0:T(8,128)(2,1)S(1)}, u32[]{:S(2)}, u32[]{:S(2)}) collective-permute-start(bf16[16,512]{1,0:T(8,128)(2,1)S(1)} %slice.57), channel_id=1, source_target_pairs={{0,4},{2,6},{4,8},{6,10},{8,12},{10,14},{12,16},{14,18},{16,20},{1... | collective-permute-start | bytes 49160 | tf_op jit(solution)/shard_map/ppermute | solution.py:981
  13.0 47.0 %collective-permute-start.9 = (bf16[1024,512]{1,0:T(8,128)(2,1)}, bf16[1024,512]{1,0:T(8,128)(2,1)}, u32[]{:S(2)}, u32[]{:S(2)}) collective-permute-start(bf16[1024,512]{1,0:T(8,128)(2,1)} %param.18), channel_id=1, source_target_pairs={{0,1},{1,0},{2,3},{3,2},{4,5},{5,4},{6,7},{7,6},{8,9},{9,8},{10,11... | collective-permute-start | bytes 3145736 | tf_op jit(solution)/shard_map/ppermute | solution.py:974
  16.0 3.0 collective-permute-start.2
  19.9 25.9 %copy-start.50 = (f32[8]{0:T(128)S(1)}, f32[8]{0:T(128)}, u32[]{:S(2)}) copy-start(f32[8]{0:T(128)} %param.28) | copy-start | bytes 100
  45.7 1.5 collective-permute-start.3
  58.0 14.9 %collective-permute-start.7 = (bf16[528,256]{1,0:T(8,128)(2,1)}, bf16[528,256]{1,0:T(8,128)(2,1)S(1)}, u32[]{:S(2)}, u32[]{:S(2)}) collective-permute-start(bf16[528,256]{1,0:T(8,128)(2,1)} %get-tuple-element.116), channel_id=1, source_target_pairs={{4,0},{6,2},{0,4},{2,6},{12,8},{14,10},{8,12},{10,14},{20,16},{22,... | collective-permute-start | bytes 811016 | tf_op jit(solution)/shard_map/ppermute | solution.py:353
  59.5 15.2 %collective-permute-start.4 = (bf16[528,256]{1,0:T(8,128)(2,1)}, bf16[528,256]{1,0:T(8,128)(2,1)S(1)}, u32[]{:S(2)}, u32[]{:S(2)}) collective-permute-start(bf16[528,256]{1,0:T(8,128)(2,1)} %get-tuple-element.108), channel_id=1, source_target_pairs={{4,0},{6,2},{0,4},{2,6},{12,8},{14,10},{8,12},{10,14},{20,16},{22,... | collective-permute-start | bytes 811016 | tf_op jit(solution)/shard_map/ppermute | solution.py:353
  73.1 9.5 %collective-permute-start.8 = (bf16[528,256]{1,0:T(8,128)(2,1)S(1)}, bf16[528,256]{1,0:T(8,128)(2,1)S(1)}, u32[]{:S(2)}, u32[]{:S(2)}) collective-permute-start(bf16[528,256]{1,0:T(8,128)(2,1)S(1)} %get-tuple-element.123), channel_id=1, source_target_pairs={{8,0},{10,2},{12,4},{14,6},{0,8},{2,10},{4,12},{6,14},{24,16},{26,... | collective-permute-start | bytes 811016 | tf_op jit(solution)/shard_map/ppermute | solution.py:353
  75.0 16.1 %collective-permute-start.5 = (bf16[528,256]{1,0:T(8,128)(2,1)S(1)}, bf16[528,256]{1,0:T(8,128)(2,1)S(1)}, u32[]{:S(2)}, u32[]{:S(2)}) collective-permute-start(bf16[528,256]{1,0:T(8,128)(2,1)S(1)} %get-tuple-element.110), channel_id=1, source_target_pairs={{8,0},{10,2},{12,4},{14,6},{0,8},{2,10},{4,12},{6,14},{24,16},{26,... | collective-permute-start | bytes 811016 | tf_op jit(solution)/shard_map/ppermute | solution.py:353
  83.5 20.2 %collective-permute-start.10 = (bf16[528,256]{1,0:T(8,128)(2,1)S(1)}, bf16[528,256]{1,0:T(8,128)(2,1)S(1)}, u32[]{:S(2)}, u32[]{:S(2)}) collective-permute-start(bf16[528,256]{1,0:T(8,128)(2,1)S(1)} %get-tuple-element.125), channel_id=1, source_target_pairs={{16,0},{18,2},{20,4},{22,6},{24,8},{26,10},{28,12},{30,14},{0,16},... | collective-permute-start | bytes 811016 | tf_op jit(solution)/shard_map/ppermute | solution.py:353
  92.0 16.0 %collective-permute-start.6 = (bf16[528,256]{1,0:T(8,128)(2,1)S(1)}, bf16[528,256]{1,0:T(8,128)(2,1)S(1)}, u32[]{:S(2)}, u32[]{:S(2)}) collective-permute-start(bf16[528,256]{1,0:T(8,128)(2,1)S(1)} %get-tuple-element.111), channel_id=1, source_target_pairs={{16,0},{18,2},{20,4},{22,6},{24,8},{26,10},{28,12},{30,14},{0,16},... | collective-permute-start | bytes 811016 | tf_op jit(solution)/shard_map/ppermute | solution.py:353
  105.2 7.4 %collective-permute-start.12 = (bf16[528,256]{1,0:T(8,128)(2,1)S(1)}, bf16[528,256]{1,0:T(8,128)(2,1)S(1)}, u32[]{:S(2)}, u32[]{:S(2)}) collective-permute-start(bf16[528,256]{1,0:T(8,128)(2,1)S(1)} %get-tuple-element.132), channel_id=1, source_target_pairs={{4,0},{6,2},{0,4},{2,6},{12,8},{14,10},{8,12},{10,14},{20,16},{22,... | collective-permute-start | bytes 811016 | tf_op jit(solution)/shard_map/ppermute | solution.py:353
  109.5 8.0 %collective-permute-start.11 = (bf16[528,256]{1,0:T(8,128)(2,1)S(1)}, bf16[528,256]{1,0:T(8,128)(2,1)S(1)}, u32[]{:S(2)}, u32[]{:S(2)}) collective-permute-start(bf16[528,256]{1,0:T(8,128)(2,1)S(1)} %get-tuple-element.131), channel_id=1, source_target_pairs={{4,0},{6,2},{0,4},{2,6},{12,8},{14,10},{8,12},{10,14},{20,16},{22,... | collective-permute-start | bytes 811016 | tf_op jit(solution)/shard_map/ppermute | solution.py:353
  149.1 13.1 %collective-permute-start.13 = (bf16[528,512]{1,0:T(8,128)(2,1)}, bf16[528,512]{1,0:T(8,128)(2,1)S(1)}, u32[]{:S(2)}, u32[]{:S(2)}) collective-permute-start(bf16[528,512]{1,0:T(8,128)(2,1)} %get-tuple-element.139), channel_id=1, source_target_pairs={{4,0},{6,2},{0,4},{2,6},{12,8},{14,10},{8,12},{10,14},{20,16},{22,... | collective-permute-start | bytes 1622024 | tf_op jit(solution)/shard_map/ppermute | solution.py:353
  155.0 26.4 %collective-permute-start.18 = (bf16[512,1024]{1,0:T(8,128)(2,1)}, bf16[512,1024]{1,0:T(8,128)(2,1)}, u32[]{:S(2)}, u32[]{:S(2)}) collective-permute-start(bf16[512,1024]{1,0:T(8,128)(2,1)} %convolution_convert_fusion), channel_id=1, source_target_pairs={{2,0},{0,2},{6,4},{4,6},{10,8},{8,10},{14,12},{12,14},{18,16},{16,... | collective-permute-start | bytes 3145736 | tf_op jit(solution)/shard_map/ppermute | solution.py:896
  158.8 42.5 %collective-permute-start.17 = (bf16[512,1024]{1,0:T(8,128)(2,1)}, bf16[512,1024]{1,0:T(8,128)(2,1)}, u32[]{:S(2)}, u32[]{:S(2)}) collective-permute-start(bf16[512,1024]{1,0:T(8,128)(2,1)} %convolution_convert_fusion.1), channel_id=1, source_target_pairs={{2,0},{0,2},{6,4},{4,6},{10,8},{8,10},{14,12},{12,14},{18,16},{16,... | collective-permute-start | bytes 3145736 | tf_op jit(solution)/shard_map/ppermute | solution.py:896
  165.7 18.4 %collective-permute-start.14 = (bf16[528,512]{1,0:T(8,128)(2,1)S(1)}, bf16[528,512]{1,0:T(8,128)(2,1)S(1)}, u32[]{:S(2)}, u32[]{:S(2)}) collective-permute-start(bf16[528,512]{1,0:T(8,128)(2,1)S(1)} %get-tuple-element.143), channel_id=1, source_target_pairs={{8,0},{10,2},{12,4},{14,6},{0,8},{2,10},{4,12},{6,14},{24,16},{26,... | collective-permute-start | bytes 1622024 | tf_op jit(solution)/shard_map/ppermute | solution.py:353
  185.5 22.7 %collective-permute-start.16 = (bf16[528,512]{1,0:T(8,128)(2,1)S(1)}, bf16[528,512]{1,0:T(8,128)(2,1)S(1)}, u32[]{:S(2)}, u32[]{:S(2)}) collective-permute-start(bf16[528,512]{1,0:T(8,128)(2,1)S(1)} %get-tuple-element.147), channel_id=1, source_target_pairs={{16,0},{18,2},{20,4},{22,6},{24,8},{26,10},{28,12},{30,14},{0,16},... | collective-permute-start | bytes 1622024 | tf_op jit(solution)/shard_map/ppermute | solution.py:353
  209.0 22.9 %collective-permute-start.20 = (bf16[512,1024]{1,0:T(8,128)(2,1)}, bf16[512,1024]{1,0:T(8,128)(2,1)}, u32[]{:S(2)}, u32[]{:S(2)}) collective-permute-start(bf16[512,1024]{1,0:T(8,128)(2,1)} %fusion.4), channel_id=1, source_target_pairs={{8,0},{10,2},{12,4},{14,6},{0,8},{2,10},{4,12},{6,14},{24,16},{26,... | collective-permute-start | bytes 3145736 | tf_op jit(solution)/shard_map/ppermute | solution.py:896
  214.0 21.5 %collective-permute-start.19 = (bf16[528,512]{1,0:T(8,128)(2,1)}, bf16[528,512]{1,0:T(8,128)(2,1)S(1)}, u32[]{:S(2)}, u32[]{:S(2)}) collective-permute-start(bf16[528,512]{1,0:T(8,128)(2,1)} %get-tuple-element.152), channel_id=1, source_target_pairs={{4,0},{6,2},{0,4},{2,6},{12,8},{14,10},{8,12},{10,14},{20,16},{22,... | collective-permute-start | bytes 1622024 | tf_op jit(solution)/shard_map/ppermute | solution.py:353
  235.5 137.0 %all-gather.2.cloned.1.call-start = ((), (), s32[]{:S(2)}) async-start(), calls=%async_computation.2 | async-start | bytes 4456448 | tf_op jit(solution)/shard_map/all_gather | solution.py:1049
  236.3 37.1 %copy-start.47 = (bf16[3,1024,8]{1,2,0:T(8,128)(2,1)S(1)}, bf16[3,1024,8]{1,2,0:T(8,128)(2,1)}, u32[]{:S(2)}) copy-start(bf16[3,1024,8]{1,2,0:T(8,128)(2,1)} %param.27) | copy-start | bytes 147460
  236.3 37.2 %copy-start.51 = (s32[8]{0:T(128)S(1)}, s32[8]{0:T(128)}, u32[]{:S(2)}) copy-start(s32[8]{0:T(128)} %constant.217) | copy-start | bytes 100
  273.4 1.8 collective-permute-start.21
  278.1 12.2 %collective-permute-start.22 = (f32[8,1024]{1,0:T(8,128)}, f32[8,1024]{1,0:T(8,128)S(1)}, u32[]{:S(2)}, u32[]{:S(2)}) collective-permute-start(f32[8,1024]{1,0:T(8,128)} %edge.1), channel_id=1, source_target_pairs={{4,0},{6,2},{8,4},{10,6},{12,8},{14,10},{16,12},{18,14},{20,16},{2... | collective-permute-start | bytes 98312 | tf_op jit(solution)/shard_map/ppermute | solution.py:981
  328.8 17.4 %collective-permute-start.24 = (bf16[256,1024]{1,0:T(8,128)(2,1)S(1)}, bf16[256,1024]{1,0:T(8,128)(2,1)S(1)}, u32[]{:S(2)}, u32[]{:S(2)}) collective-permute-start(bf16[256,1024]{1,0:T(8,128)(2,1)S(1)} %dynamic-slice_convert_fusion), channel_id=1, source_target_pairs={{4,0},{6,2},{0,4},{2,6},{12,8},{14,10},{8,12},{10,14},{20,16},{22,... | collective-permute-start | bytes 1572872 | tf_op jit(solution)/shard_map/ppermute | solution.py:896
  329.7 18.3 %collective-permute-start.23 = (bf16[256,1024]{1,0:T(8,128)(2,1)S(1)}, bf16[256,1024]{1,0:T(8,128)(2,1)S(1)}, u32[]{:S(2)}, u32[]{:S(2)}) collective-permute-start(bf16[256,1024]{1,0:T(8,128)(2,1)S(1)} %dynamic-slice_convert_fusion.1), channel_id=1, source_target_pairs={{2,0},{0,2},{6,4},{4,6},{10,8},{8,10},{14,12},{12,14},{18,16},{16,... | collective-permute-start | bytes 1572872 | tf_op jit(solution)/shard_map/ppermute | solution.py:896
  350.6 17.2 %collective-permute-start.27 = (f32[1024,512]{1,0:T(8,128)}, f32[1024,512]{1,0:T(8,128)}, u32[]{:S(2)}, u32[]{:S(2)}) collective-permute-start(f32[1024,512]{1,0:T(8,128)} %constant_dynamic-slice_fusion), channel_id=1, source_target_pairs={{0,1},{1,0},{2,3},{3,2},{4,5},{5,4},{6,7},{7,6},{8,9},{9,8},{10,11... | collective-permute-start | bytes 6291464 | tf_op jit(solution)/shard_map/ppermute | solution.py:974
  353.6 22.9 %collective-permute-start.15 = (f32[1024,512]{1,0:T(8,128)}, f32[1024,512]{1,0:T(8,128)}, u32[]{:S(2)}, u32[]{:S(2)}) collective-permute-start(f32[1024,512]{1,0:T(8,128)} %constant_dynamic-slice_fusion.1), channel_id=1, source_target_pairs={{0,1},{1,0},{2,3},{3,2},{4,5},{5,4},{6,7},{7,6},{8,9},{9,8},{10,11... | collective-permute-start | bytes 6291464 | tf_op jit(solution)/shard_map/ppermute | solution.py:974
  353.7 6.2 %collective-permute-start.28 = (f32[2,1024]{1,0:T(2,128)S(1)}, f32[2,1024]{1,0:T(2,128)S(1)}, u32[]{:S(2)}, u32[]{:S(2)}) collective-permute-start(f32[2,1024]{1,0:T(2,128)S(1)} %pad_maximum_fusion.10), channel_id=1, source_target_pairs={{0,1},{1,0},{2,3},{3,2},{4,5},{5,4},{6,7},{7,6},{8,9},{9,8},{10,11... | collective-permute-start | bytes 24584 | tf_op jit(solution)/shard_map/ppermute | solution.py:974
  355.3 9.1 %collective-permute-start.26 = (bf16[128,1024]{1,0:T(8,128)(2,1)S(1)}, bf16[128,1024]{1,0:T(8,128)(2,1)S(1)}, u32[]{:S(2)}, u32[]{:S(2)}) collective-permute-start(bf16[128,1024]{1,0:T(8,128)(2,1)S(1)} %dynamic-slice_convert_fusion.3), channel_id=1, source_target_pairs={{2,0},{0,2},{6,4},{4,6},{10,8},{8,10},{14,12},{12,14},{18,16},{16,... | collective-permute-start | bytes 786440 | tf_op jit(solution)/shard_map/ppermute | solution.py:896
  358.9 8.1 %collective-permute-start.25 = (bf16[128,1024]{1,0:T(8,128)(2,1)S(1)}, bf16[128,1024]{1,0:T(8,128)(2,1)S(1)}, u32[]{:S(2)}, u32[]{:S(2)}) collective-permute-start(bf16[128,1024]{1,0:T(8,128)(2,1)S(1)} %dynamic-slice_convert_fusion.4), channel_id=1, source_target_pairs={{4,0},{6,2},{0,4},{2,6},{12,8},{14,10},{8,12},{10,14},{20,16},{22,... | collective-permute-start | bytes 786440 | tf_op jit(solution)/shard_map/ppermute | solution.py:896
  376.5 8.2 %collective-permute-start.34 = (bf16[128,1024]{1,0:T(8,128)(2,1)}, bf16[128,1024]{1,0:T(8,128)(2,1)}, u32[]{:S(2)}, u32[]{:S(2)}) collective-permute-start(bf16[128,1024]{1,0:T(8,128)(2,1)} %dynamic-slice_convert_fusion.2), channel_id=1, source_target_pairs={{8,0},{10,2},{12,4},{14,6},{0,8},{2,10},{4,12},{6,14},{24,16},{26,... | collective-permute-start | bytes 786440 | tf_op jit(solution)/shard_map/ppermute | solution.py:896
  380.9 1.4 collective-permute-start.29
  383.6 7.1 %collective-permute-start.30 = (f32[48,1024]{1,0:T(8,128)S(1)}, f32[48,1024]{1,0:T(8,128)S(1)}, u32[]{:S(2)}, u32[]{:S(2)}) collective-permute-start(f32[48,1024]{1,0:T(8,128)S(1)} %pad_add_fusion), channel_id=1, source_target_pairs={{2,0},{0,2},{6,4},{4,6},{10,8},{8,10},{14,12},{12,14},{18,16},{16,... | collective-permute-start | bytes 589832 | tf_op jit(solution)/shard_map/ppermute | solution.py:896
  385.9 9.1 %collective-permute-start.35 = (bf16[64,1024]{1,0:T(8,128)(2,1)S(1)}, bf16[64,1024]{1,0:T(8,128)(2,1)S(1)}, u32[]{:S(2)}, u32[]{:S(2)}) collective-permute-start(bf16[64,1024]{1,0:T(8,128)(2,1)S(1)} %dynamic-slice_convert_fusion.5), channel_id=1, source_target_pairs={{16,0},{18,2},{20,4},{22,6},{24,8},{26,10},{28,12},{30,14},{0,16},... | collective-permute-start | bytes 393224 | tf_op jit(solution)/shard_map/ppermute | solution.py:896
  390.7 6.3 %collective-permute-start.31 = (f32[48,1024]{1,0:T(8,128)S(1)}, f32[48,1024]{1,0:T(8,128)S(1)}, u32[]{:S(2)}, u32[]{:S(2)}) collective-permute-start(f32[48,1024]{1,0:T(8,128)S(1)} %fusion.38), channel_id=1, source_target_pairs={{4,0},{6,2},{0,4},{2,6},{12,8},{14,10},{8,12},{10,14},{20,16},{22,... | collective-permute-start | bytes 589832 | tf_op jit(solution)/shard_map/ppermute | solution.py:896
  395.1 8.0 %collective-permute-start.36 = (bf16[64,1024]{1,0:T(8,128)(2,1)S(1)}, bf16[64,1024]{1,0:T(8,128)(2,1)S(1)}, u32[]{:S(2)}, u32[]{:S(2)}) collective-permute-start(bf16[64,1024]{1,0:T(8,128)(2,1)S(1)} %add_convert_fusion), channel_id=1, source_target_pairs={{16,0},{18,2},{20,4},{22,6},{24,8},{26,10},{28,12},{30,14},{0,16},... | collective-permute-start | bytes 393224 | tf_op jit(solution)/shard_map/ppermute | solution.py:896
  397.0 8.3 %collective-permute-start.32 = (f32[48,1024]{1,0:T(8,128)S(1)}, f32[48,1024]{1,0:T(8,128)S(1)}, u32[]{:S(2)}, u32[]{:S(2)}) collective-permute-start(f32[48,1024]{1,0:T(8,128)S(1)} %add.239), channel_id=1, source_target_pairs={{8,0},{10,2},{12,4},{14,6},{0,8},{2,10},{4,12},{6,14},{24,16},{26,... | collective-permute-start | bytes 589832 | tf_op jit(solution)/shard_map/ppermute | solution.py:896
  403.1 16.5 %collective-permute-start.37 = (bf16[128,1024]{1,0:T(8,128)(2,1)S(1)}, bf16[128,1024]{1,0:T(8,128)(2,1)S(1)}, u32[]{:S(2)}, u32[]{:S(2)}) collective-permute-start(bf16[128,1024]{1,0:T(8,128)(2,1)S(1)} %pad_maximum_fusion.8), channel_id=1, source_target_pairs={{8,0},{10,2},{12,4},{14,6},{0,8},{2,10},{4,12},{6,14},{24,16},{26,... | collective-permute-start | bytes 786440 | tf_op jit(solution)/shard_map/ppermute | solution.py:896
  405.3 10.8 %collective-permute-start.33 = (f32[48,1024]{1,0:T(8,128)S(1)}, f32[48,1024]{1,0:T(8,128)S(1)}, u32[]{:S(2)}, u32[]{:S(2)}) collective-permute-start(f32[48,1024]{1,0:T(8,128)S(1)} %add.240), channel_id=1, source_target_pairs={{16,0},{18,2},{20,4},{22,6},{24,8},{26,10},{28,12},{30,14},{0,16},... | collective-permute-start | bytes 589832 | tf_op jit(solution)/shard_map/ppermute | solution.py:896
  419.7 6.4 %collective-permute-start.38 = (bf16[128,1024]{1,0:T(8,128)(2,1)S(1)}, bf16[128,1024]{1,0:T(8,128)(2,1)S(1)}, u32[]{:S(2)}, u32[]{:S(2)}) collective-permute-start(bf16[128,1024]{1,0:T(8,128)(2,1)S(1)} %get-tuple-element.228), channel_id=1, source_target_pairs={{4,0},{6,2},{0,4},{2,6},{12,8},{14,10},{8,12},{10,14},{20,16},{22,... | collective-permute-start | bytes 786440 | tf_op jit(solution)/shard_map/ppermute | solution.py:896
  423.2 9.2 %collective-permute-start.40 = (bf16[128,1024]{1,0:T(8,128)(2,1)S(1)}, bf16[128,1024]{1,0:T(8,128)(2,1)S(1)}, u32[]{:S(2)}, u32[]{:S(2)}) collective-permute-start(bf16[128,1024]{1,0:T(8,128)(2,1)S(1)} %get-tuple-element.229), channel_id=1, source_target_pairs={{2,0},{0,2},{6,4},{4,6},{10,8},{8,10},{14,12},{12,14},{18,16},{16,... | collective-permute-start | bytes 786440 | tf_op jit(solution)/shard_map/ppermute | solution.py:896
  427.1 20.9 %collective-permute-start.39 = (bf16[256,1024]{1,0:T(8,128)(2,1)}, bf16[256,1024]{1,0:T(8,128)(2,1)}, u32[]{:S(2)}, u32[]{:S(2)}) collective-permute-start(bf16[256,1024]{1,0:T(8,128)(2,1)} %pad_maximum_fusion.6), channel_id=1, source_target_pairs={{2,0},{0,2},{6,4},{4,6},{10,8},{8,10},{14,12},{12,14},{18,16},{16,... | collective-permute-start | bytes 1572872 | tf_op jit(solution)/shard_map/ppermute | solution.py:896
  433.3 16.0 %collective-permute-start.41 = (bf16[256,1024]{1,0:T(8,128)(2,1)}, bf16[256,1024]{1,0:T(8,128)(2,1)}, u32[]{:S(2)}, u32[]{:S(2)}) collective-permute-start(bf16[256,1024]{1,0:T(8,128)(2,1)} %pad_maximum_fusion.7), channel_id=1, source_target_pairs={{4,0},{6,2},{0,4},{2,6},{12,8},{14,10},{8,12},{10,14},{20,16},{22,... | collective-permute-start | bytes 1572872 | tf_op jit(solution)/shard_map/ppermute | solution.py:896
  (55 other events, 324.2 us)
Sparse Core Ops, SparseCore 0:
  235.7 52.8 reduce-scatter.1
  291.7 78.9 all-gather.1
